TPU v7x, 32 devices: a whole 2x2x4 slice. The times are simulated.
32 devices in a mesh: gx: 4 (over z), gz: 8 (over y, x, core).
Axes of the slice: x: 2, y: 2, z: 4, core: 2. Of those that a mesh axis runs over, the one named last changes fastest.
Arguments:
- fields: float32 [2, 16, 512, 512], P(None, 'gz', 'gx'), may hold values from -6 to 6
- grain_ids: int32 [16, 512, 512], P('gz', 'gx'), may hold values from 0 to 31, as said below
- grain_rates: float32 [32, 2], replicated, may hold values from 0.5 to 2.5
- die_mask: int32 [512, 512], P('gx'), may hold values from 0 to 1, as said below
Outputs:
- updated: float32 [2, 16, 512, 512], P(None, 'gz', 'gx')
Inputs may be any that keep to these rules, and one draw needn't show every extreme that they name: `grain_ids`: grain ids are constant on aligned blocks of 2 cells along z by 8 by 8 cells along x and y. `die_mask`: the mask is constant on aligned blocks of 16 by 16 cells.
All inputs are finite; a program needn't handle non-finite values.
Results may differ from a plain program's by a relative error of at most 0.0003.
Values sent between devices are 32-bit elements; how exact they have to be, the bound alone decides.
No kernel may reach another device: no remote copies, remote signals or barrier semaphores. Data moves between devices by JAX's collectives and lax.ppermute only.
A program may use at most 128 MiB of HBM per device.

v0:
```python
import jax
import jax.numpy as jnp
from jax import lax
from jax.sharding import PartitionSpec as P

heat_loss = 4.0
spread_solute = 2.0
spread_heat = 100.0
exact = lax.Precision.HIGHEST


def swapped(block, axis, distance):
    count = lax.axis_size(axis)
    route = []
    for low in range(count):
        high = low | 1 << distance
        if high != low and high < count:
            route += [(low, high), (high, low)]
    return lax.ppermute(block, axis, route)


def entering(part, axis, combine, identity, reverse):
    count = lax.axis_size(axis)
    place = lax.axis_index(axis)
    ahead = count - 1 - place if reverse else place
    gathered = jax.tree.map(lambda a: lax.all_gather(a, axis), part)
    state = jax.tree.map(lambda a, e: jnp.zeros_like(a) + jnp.asarray(e, a.dtype), part, identity)

    def one(step, state):
        source = count - 1 - step if reverse else step
        return combine(
            state, jax.tree.map(lambda a: lax.dynamic_index_in_dim(a, source, 0, False), gathered)
        )

    return lax.fori_loop(0, ahead, one, state)


def angle_table(length_rows, length_cols, period):
    row_ids = lax.broadcasted_iota(jnp.int32, (length_rows, length_cols), 0)
    col_ids = lax.broadcasted_iota(jnp.int32, (length_rows, length_cols), 1)
    phases = (row_ids * col_ids % period).astype(jnp.float32) * (2.0 * jnp.pi / period)
    return (jnp.cos(phases), jnp.sin(phases))


def contract(left_side, right_side, form):
    return jnp.einsum(
        form, left_side, right_side, precision=exact, preferred_element_type=jnp.float32
    )


def rotate(real_part, imag_part, cosine, sine):
    return (real_part * cosine - imag_part * sine, real_part * sine + imag_part * cosine)


def compose_maps(earlier, later):
    pivot_pivot = later[0] * earlier[0] + later[1] * earlier[2]
    pivot_scale = later[0] * earlier[1] + later[1] * earlier[3]
    scale_pivot = later[2] * earlier[0] + later[3] * earlier[2]
    scale_scale = later[2] * earlier[1] + later[3] * earlier[3]
    value_value = later[4] * earlier[4]
    value_pivot_real = later[5] * earlier[0] + later[4] * earlier[5] + later[7] * earlier[2]
    value_pivot_imag = later[6] * earlier[0] + later[4] * earlier[6] + later[8] * earlier[2]
    value_scale_real = later[5] * earlier[1] + later[4] * earlier[7] + later[7] * earlier[3]
    value_scale_imag = later[6] * earlier[1] + later[4] * earlier[8] + later[8] * earlier[3]
    norm_scale = 1.0 / (
        jnp.abs(pivot_pivot) + jnp.abs(pivot_scale) + jnp.abs(scale_pivot) + jnp.abs(scale_scale)
    )
    return (
        pivot_pivot * norm_scale,
        pivot_scale * norm_scale,
        scale_pivot * norm_scale,
        scale_scale * norm_scale,
        value_value * norm_scale,
        value_pivot_real * norm_scale,
        value_pivot_imag * norm_scale,
        value_scale_real * norm_scale,
        value_scale_imag * norm_scale,
    )


def compose_affine(earlier, later):
    return (
        later[0] * earlier[0],
        later[0] * earlier[1] + later[1],
        later[0] * earlier[2] + later[2],
    )


def on_device(fields, grain_ids, grain_rates, die_mask):
    depth_rows = fields.shape[1]
    local_x = fields.shape[2]
    span_y = fields.shape[3]
    devices_x = lax.axis_size("gx")
    devices_z = lax.axis_size("gz")
    place_x = lax.axis_index("gx")
    place_z = lax.axis_index("gz")
    total_x = local_x * devices_x
    total_z = depth_rows * devices_z
    solute = fields[0]
    heat_now = fields[1]
    grain_count = grain_rates.shape[0]
    grain_axis = lax.broadcasted_iota(jnp.int32, (grain_count, 1, 1, 1), 0)
    matches = grain_ids[None] == grain_axis
    rate_solute = jnp.sum(
        jnp.where(matches, grain_rates[:, 0].reshape(grain_count, 1, 1, 1), 0.0), axis=0
    )
    rate_heat = jnp.sum(
        jnp.where(matches, grain_rates[:, 1].reshape(grain_count, 1, 1, 1), 0.0), axis=0
    )
    rhs_solute = solute + rate_solute * jnp.tanh(heat_now - solute)
    rhs_heat = heat_now + rate_heat * solute * solute / (1.0 + solute * solute)
    layer_ids = place_z * depth_rows + lax.broadcasted_iota(jnp.int32, (depth_rows, 1, 1), 0)
    die_sink = heat_loss * die_mask.astype(jnp.float32)[None] * (heat_now + 1.0)
    rhs_heat = rhs_heat - jnp.where(layer_ids == 0, die_sink, 0.0)
    stacked = jnp.stack([rhs_solute, rhs_heat]).reshape(2 * depth_rows * local_x, span_y)
    cosine_y, sine_y = angle_table(span_y, span_y, span_y)
    wave_real = jnp.dot(stacked, cosine_y, precision=exact, preferred_element_type=jnp.float32)
    wave_imag = -jnp.dot(stacked, sine_y, precision=exact, preferred_element_type=jnp.float32)
    wave_real = wave_real.reshape(2 * depth_rows, local_x, span_y)
    wave_imag = wave_imag.reshape(2 * depth_rows, local_x, span_y)
    section_count = devices_x.bit_length() - 1
    for section_bit in reversed(range(section_count)):
        half_span = 1 << section_bit
        other_real, other_imag = swapped((wave_real, wave_imag), "gx", section_bit)
        is_upper = place_x // half_span % 2 == 1
        phases = jnp.pi / half_span * (place_x % half_span).astype(jnp.float32)
        diff_real, diff_imag = rotate(
            other_real - wave_real, other_imag - wave_imag, jnp.cos(phases), -jnp.sin(phases)
        )
        wave_real = jnp.where(is_upper, diff_real, wave_real + other_real)
        wave_imag = jnp.where(is_upper, diff_imag, wave_imag + other_imag)
    mode_block = jnp.zeros((), jnp.int32)
    for section_bit in range(section_count):
        mode_block = mode_block + place_x // (1 << section_bit) % 2 * (
            1 << section_count - 1 - section_bit
        )
    line_ids = lax.broadcasted_iota(jnp.int32, (local_x, 1), 0)
    twist_angle = (line_ids * mode_block % total_x).astype(jnp.float32) * (2.0 * jnp.pi / total_x)
    twist_cos = jnp.cos(twist_angle)
    twist_sin = jnp.sin(twist_angle)
    wave_real, wave_imag = rotate(wave_real, wave_imag, twist_cos, -twist_sin)
    cosine_line, sine_line = angle_table(local_x, local_x, local_x)
    mode_real = contract(wave_real, cosine_line, "alb,lk->akb") + contract(
        wave_imag, sine_line, "alb,lk->akb"
    )
    mode_imag = contract(wave_imag, cosine_line, "alb,lk->akb") - contract(
        wave_real, sine_line, "alb,lk->akb"
    )
    wave_x = (mode_block + devices_x * line_ids).astype(jnp.float32)
    spectrum_real = mode_real.reshape(2, depth_rows, local_x, span_y)
    spectrum_imag = mode_imag.reshape(2, depth_rows, local_x, span_y)
    spreads = jnp.array([spread_solute, spread_heat], jnp.float32).reshape(2, 1, 1)
    wave_y = lax.broadcasted_iota(jnp.int32, (1, span_y), 1).astype(jnp.float32)
    mode_values = (
        4.0 * jnp.sin(jnp.pi * wave_x / total_x) ** 2 + 4.0 * jnp.sin(jnp.pi * wave_y / span_y) ** 2
    )
    base_diag = 1.0 + spreads * mode_values[None] + 2.0 * spreads
    ones_plane = jnp.ones_like(base_diag)
    zero_plane = jnp.zeros_like(base_diag)
    first_row = place_z * depth_rows
    row_diag = []
    row_upper = []
    for layer_id in range(depth_rows):
        global_row = first_row + layer_id
        at_ends = jnp.logical_or(global_row == 0, global_row == total_z - 1)
        row_diag.append(base_diag - jnp.where(at_ends, spreads, 0.0))
        row_upper.append(jnp.where(global_row == total_z - 1, 0.0, -spreads) * ones_plane)
    pivots = []
    values_real = []
    values_imag = []
    identity_map = (
        ones_plane,
        zero_plane,
        zero_plane,
        ones_plane,
        ones_plane,
        zero_plane,
        zero_plane,
        zero_plane,
        zero_plane,
    )
    local_map = identity_map
    for layer_id in range(depth_rows):
        row_map = (
            zero_plane,
            row_upper[layer_id],
            spreads * ones_plane,
            row_diag[layer_id],
            spreads * ones_plane,
            zero_plane,
            zero_plane,
            spectrum_real[:, layer_id],
            spectrum_imag[:, layer_id],
        )
        local_map = compose_maps(local_map, row_map)
    prefix_map = entering(local_map, "gz", compose_maps, identity_map, False)
    pivot_now = prefix_map[1] / prefix_map[3]
    value_real = prefix_map[7] / prefix_map[3]
    value_imag = prefix_map[8] / prefix_map[3]
    for layer_id in range(depth_rows):
        denominator = row_diag[layer_id] + spreads * pivot_now
        pivot_now = row_upper[layer_id] / denominator
        value_real = (spectrum_real[:, layer_id] + spreads * value_real) / denominator
        value_imag = (spectrum_imag[:, layer_id] + spreads * value_imag) / denominator
        pivots.append(pivot_now)
        values_real.append(value_real)
        values_imag.append(value_imag)
    local_back = (ones_plane, zero_plane, zero_plane)
    for layer_id in reversed(range(depth_rows)):
        local_back = compose_affine(
            local_back, (-pivots[layer_id], values_real[layer_id], values_imag[layer_id])
        )
    above_map = entering(
        local_back, "gz", compose_affine, (ones_plane, zero_plane, zero_plane), True
    )
    above_real = above_map[1]
    above_imag = above_map[2]
    solved_real = [zero_plane] * depth_rows
    solved_imag = [zero_plane] * depth_rows
    for layer_id in reversed(range(depth_rows)):
        above_real = values_real[layer_id] - pivots[layer_id] * above_real
        above_imag = values_imag[layer_id] - pivots[layer_id] * above_imag
        solved_real[layer_id] = above_real
        solved_imag[layer_id] = above_imag
    mode_real = jnp.stack(solved_real, axis=1).reshape(2 * depth_rows, local_x, span_y)
    mode_imag = jnp.stack(solved_imag, axis=1).reshape(2 * depth_rows, local_x, span_y)
    back_real = (
        contract(mode_real, cosine_line, "akb,kl->alb")
        - contract(mode_imag, sine_line, "akb,kl->alb")
    ) / local_x
    back_imag = (
        contract(mode_real, sine_line, "akb,kl->alb")
        + contract(mode_imag, cosine_line, "akb,kl->alb")
    ) / local_x
    back_real, back_imag = rotate(back_real, back_imag, twist_cos, twist_sin)
    for section_bit in range(section_count):
        half_span = 1 << section_bit
        other_real, other_imag = swapped((back_real, back_imag), "gx", section_bit)
        is_upper = place_x // half_span % 2 == 1
        phases = jnp.pi / half_span * (place_x % half_span).astype(jnp.float32)
        turn_real = jnp.where(is_upper, back_real, other_real)
        turn_imag = jnp.where(is_upper, back_imag, other_imag)
        keep_real = jnp.where(is_upper, other_real, back_real)
        keep_imag = jnp.where(is_upper, other_imag, back_imag)
        rotated_real, rotated_imag = rotate(turn_real, turn_imag, jnp.cos(phases), jnp.sin(phases))
        weight_sign = jnp.where(is_upper, -0.5, 0.5)
        back_real = 0.5 * keep_real + weight_sign * rotated_real
        back_imag = 0.5 * keep_imag + weight_sign * rotated_imag
    flat_real = back_real.reshape(2 * depth_rows * local_x, span_y)
    flat_imag = back_imag.reshape(2 * depth_rows * local_x, span_y)
    updated = (
        jnp.dot(flat_real, cosine_y, precision=exact, preferred_element_type=jnp.float32)
        - jnp.dot(flat_imag, sine_y, precision=exact, preferred_element_type=jnp.float32)
    ) / span_y
    return updated.reshape(2, depth_rows, local_x, span_y)


def solution(mesh):
    placed = (P(None, "gz", "gx", None), P("gz", "gx", None), P(), P("gx", None))
    return jax.shard_map(
        on_device, mesh=mesh, in_specs=placed, out_specs=P(None, "gz", "gx", None), check_vma=False
    )
```

profile of v0, /device:TPU:0, one launch (start us, length us, event | category | flops | bytes accessed | tf_op | source)
XLA Modules:
  0.0 859.6 jit_solution(3317551479093158938)
XLA Ops:
  24.4 6.4 convolution_negate_fusion
  31.1 62.2 %collective-permute-done = f32[4,128,512]{2,1,0:T(8,128)S(1)} collective-permute-done((f32[4,128,512]{2,1,0:T(8,128)S(1)}, f32[4,128,512]{2,1,0:T(8,128)S(1)}, u32[]{:S(2)}, u32[]{:S(2)}) %collective-permute-start) | collective-permute-done | bytes 1048608 | tf_op jit(solution)/shard_map/ppermute | solution.py:19
  94.3 20.8 %collective-permute-done.1 = f32[4,128,512]{2,1,0:T(8,128)} collective-permute-done((f32[4,128,512]{2,1,0:T(8,128)S(1)}, f32[4,128,512]{2,1,0:T(8,128)}, u32[]{:S(2)}, u32[]{:S(2)}) %collective-permute-start.1) | collective-permute-done | bytes 1048608 | tf_op jit(solution)/shard_map/ppermute | solution.py:19
  119.9 23.7 %collective-permute-done.2 = f32[4,128,512]{2,1,0:T(8,128)S(1)} collective-permute-done((f32[4,128,512]{2,1,0:T(8,128)S(1)}, f32[4,128,512]{2,1,0:T(8,128)S(1)}, u32[]{:S(2)}, u32[]{:S(2)}) %collective-permute-start.2) | collective-permute-done | bytes 1048608 | tf_op jit(solution)/shard_map/ppermute | solution.py:19
  143.6 20.8 %collective-permute-done.3 = f32[4,128,512]{2,1,0:T(8,128)} collective-permute-done((f32[4,128,512]{2,1,0:T(8,128)S(1)}, f32[4,128,512]{2,1,0:T(8,128)}, u32[]{:S(2)}, u32[]{:S(2)}) %collective-permute-start.3) | collective-permute-done | bytes 1048608 | tf_op jit(solution)/shard_map/ppermute | solution.py:19
  181.5 33.3 %all-gather.16.cloned.1.call-done = f32[8,2,128,512]{3,2,1,0:T(8,128)} async-done(((f32[1,2,128,512]{3,2,1,0:T(8,128)}), f32[8,2,128,512]{3,2,1,0:T(8,128)}) %all-gather.16.cloned.1.call-update) | async-done | bytes 4194320 | tf_op jit(solution)/shard_map/all_gather | solution.py:26
  214.8 38.6 %all-gather.18.cloned.1.call-done = f32[8,2,128,512]{3,2,1,0:T(8,128)} async-done(((f32[1,2,128,512]{3,2,1,0:T(8,128)}), f32[8,2,128,512]{3,2,1,0:T(8,128)}) %all-gather.18.cloned.1.call-update) | async-done | bytes 4194320 | tf_op jit(solution)/shard_map/all_gather | solution.py:26
  253.4 38.6 %all-gather.20.cloned.1.call-done = f32[8,2,128,512]{3,2,1,0:T(8,128)} async-done(((f32[1,2,128,512]{3,2,1,0:T(8,128)}), f32[8,2,128,512]{3,2,1,0:T(8,128)}) %all-gather.20.cloned.1.call-update) | async-done | bytes 4194320 | tf_op jit(solution)/shard_map/all_gather | solution.py:26
  292.1 38.5 %all-gather.22.cloned.1.call-done = f32[8,2,128,512]{3,2,1,0:T(8,128)} async-done(((f32[1,2,128,512]{3,2,1,0:T(8,128)}), f32[8,2,128,512]{3,2,1,0:T(8,128)}) %all-gather.22.cloned.1.call-update) | async-done | bytes 4194320 | tf_op jit(solution)/shard_map/all_gather | solution.py:26
  330.6 38.5 %all-gather.24.cloned.1.call-done = f32[8,2,128,512]{3,2,1,0:T(8,128)} async-done(((f32[1,2,128,512]{3,2,1,0:T(8,128)}), f32[8,2,128,512]{3,2,1,0:T(8,128)}) %all-gather.24.cloned.1.call-update) | async-done | bytes 4194320 | tf_op jit(solution)/shard_map/all_gather | solution.py:26
  369.1 38.5 %all-gather.26.cloned.1.call-done = f32[8,2,128,512]{3,2,1,0:T(8,128)} async-done(((f32[1,2,128,512]{3,2,1,0:T(8,128)}), f32[8,2,128,512]{3,2,1,0:T(8,128)}) %all-gather.26.cloned.1.call-update) | async-done | bytes 4194320 | tf_op jit(solution)/shard_map/all_gather | solution.py:26
  407.5 38.6 %all-gather.28.cloned.1.call-done = f32[8,2,128,512]{3,2,1,0:T(8,128)} async-done(((f32[1,2,128,512]{3,2,1,0:T(8,128)}), f32[8,2,128,512]{3,2,1,0:T(8,128)}) %all-gather.28.cloned.1.call-update) | async-done | bytes 4194320 | tf_op jit(solution)/shard_map/all_gather | solution.py:26
  446.2 38.6 %all-gather.30.cloned.1.call-done = f32[8,2,128,512]{3,2,1,0:T(8,128)} async-done(((f32[1,2,128,512]{3,2,1,0:T(8,128)}), f32[8,2,128,512]{3,2,1,0:T(8,128)}) %all-gather.30.cloned.1.call-update) | async-done | bytes 4194320 | tf_op jit(solution)/shard_map/all_gather | solution.py:26
  484.8 38.6 %all-gather.32.cloned.1.call-done = f32[8,2,128,512]{3,2,1,0:T(8,128)} async-done(((f32[1,2,128,512]{3,2,1,0:T(8,128)}), f32[8,2,128,512]{3,2,1,0:T(8,128)}) %all-gather.32.cloned.1.call-update) | async-done | bytes 4194320 | tf_op jit(solution)/shard_map/all_gather | solution.py:26
  529.9 70.1 %all-gather.34.cloned.1.call-done = f32[16,128,512]{2,1,0:T(8,128)} async-done(((f32[2,128,512]{2,1,0:T(8,128)}), f32[16,128,512]{2,1,0:T(8,128)}) %all-gather.34.cloned.1.call-update) | async-done | bytes 4194320 | tf_op jit(solution)/shard_map/all_gather | solution.py:26
  600.0 38.6 %all-gather.36.cloned.1.call-done = f32[16,128,512]{2,1,0:T(8,128)} async-done(((f32[2,128,512]{2,1,0:T(8,128)}), f32[16,128,512]{2,1,0:T(8,128)}) %all-gather.36.cloned.1.call-update) | async-done | bytes 4194320 | tf_op jit(solution)/shard_map/all_gather | solution.py:26
  638.6 38.5 %all-gather.38.cloned.1.call-done = f32[16,128,512]{2,1,0:T(8,128)} async-done(((f32[2,128,512]{2,1,0:T(8,128)}), f32[16,128,512]{2,1,0:T(8,128)}) %all-gather.38.cloned.1.call-update) | async-done | bytes 4194320 | tf_op jit(solution)/shard_map/all_gather | solution.py:26
  677.3 12.7 %while.42 = (s32[]{:T(128)}, f32[2,128,512]{2,1,0:T(8,128)S(1)}, f32[2,128,512]{2,1,0:T(8,128)S(1)}, s32[]{:T(128)}, f32[8,2,128,512]{3,2,1,0:T(8,128)}, /*index...) while((s32[]{:T(128)}, f32[2,128,512]{2,1,0:T(8,128)S(1)}, ...), condition=%wide.region_5.6_spmd, body=%wide.region_4.5_spmd.sunk | while | flops 524294 | bytes 3670175 | solution.py:35
  699.8 24.1 %collective-permute-done.4 = f32[4,128,512]{2,1,0:T(8,128)S(1)} collective-permute-done((f32[4,128,512]{2,1,0:T(8,128)S(1)}, f32[4,128,512]{2,1,0:T(8,128)S(1)}, u32[]{:S(2)}, u32[]{:S(2)}) %collective-permute-start.4) | collective-permute-done | bytes 1048608 | tf_op jit(solution)/shard_map/ppermute | solution.py:19
  724.8 19.0 %collective-permute-done.5 = f32[4,128,512]{2,1,0:T(8,128)} collective-permute-done((f32[4,128,512]{2,1,0:T(8,128)S(1)}, f32[4,128,512]{2,1,0:T(8,128)}, u32[]{:S(2)}, u32[]{:S(2)}) %collective-permute-start.5) | collective-permute-done | bytes 1048608 | tf_op jit(solution)/shard_map/ppermute | solution.py:19
  749.2 66.6 %collective-permute-done.6 = f32[4,128,512]{2,1,0:T(8,128)S(1)} collective-permute-done((f32[4,128,512]{2,1,0:T(8,128)S(1)}, f32[4,128,512]{2,1,0:T(8,128)S(1)}, u32[]{:S(2)}, u32[]{:S(2)}) %collective-permute-start.6) | collective-permute-done | bytes 1048608 | tf_op jit(solution)/shard_map/ppermute | solution.py:19
  815.8 21.5 %collective-permute-done.7 = f32[4,128,512]{2,1,0:T(8,128)} collective-permute-done((f32[4,128,512]{2,1,0:T(8,128)S(1)}, f32[4,128,512]{2,1,0:T(8,128)}, u32[]{:S(2)}, u32[]{:S(2)}) %collective-permute-start.7) | collective-permute-done | bytes 1048608 | tf_op jit(solution)/shard_map/ppermute | solution.py:19
  839.1 6.6 fusion.53
  845.7 6.6 fusion.10
  (105 shorter events, 77.3 us)
Async XLA Ops:
  6.5 208.3 %all-gather.16.cloned.1.call-start = ((), (), s32[]{:S(2)}) async-start(), calls=%async_computation | async-start | bytes 4718592 | tf_op jit(solution)/shard_map/all_gather | solution.py:26
  20.3 73.0 %collective-permute-start = (f32[4,128,512]{2,1,0:T(8,128)S(1)}, f32[4,128,512]{2,1,0:T(8,128)S(1)}, u32[]{:S(2)}, u32[]{:S(2)}) collective-permute-start(f32[4,128,512]{2,1,0:T(8,128)S(1)} %fusion.14), channel_id=1, source_target_pairs={{0,16},{16,0},{8,24},{24,8},{1,17},{17,1},{9,25},{25,9},{2,18},{18... | collective-permute-start | bytes 3145736 | tf_op jit(solution)/shard_map/ppermute | solution.py:19
  30.8 62.5 %copy-start.7 = (f32[512,512]{1,0:T(8,128)}, f32[512,512]{1,0:T(8,128)S(1)}, u32[]{:S(2)}) copy-start(f32[512,512]{1,0:T(8,128)S(1)} %convolution_negate_fusion) | copy-start | bytes 3145732
  30.8 89.0 %copy-start.9 = (f32[2]{0:T(128)S(1)}, f32[2]{0:T(128)}, u32[]{:S(2)}) copy-start(f32[2]{0:T(128)} %constant.234.clone) | copy-start | bytes 28
  30.8 89.0 %copy-start.11 = (f32[2]{0:T(128)S(1)}, f32[2]{0:T(128)}, u32[]{:S(2)}) copy-start(f32[2]{0:T(128)} %constant.237) | copy-start | bytes 28
  30.8 84.2 %collective-permute-start.1 = (f32[4,128,512]{2,1,0:T(8,128)S(1)}, f32[4,128,512]{2,1,0:T(8,128)}, u32[]{:S(2)}, u32[]{:S(2)}) collective-permute-start(f32[4,128,512]{2,1,0:T(8,128)S(1)} %bitcast.277), channel_id=1, source_target_pairs={{0,16},{16,0},{8,24},{24,8},{1,17},{17,1},{9,25},{25,9},{2,18},{18... | collective-permute-start | bytes 3145736 | tf_op jit(solution)/shard_map/ppermute | solution.py:19
  117.4 26.2 %collective-permute-start.2 = (f32[4,128,512]{2,1,0:T(8,128)S(1)}, f32[4,128,512]{2,1,0:T(8,128)S(1)}, u32[]{:S(2)}, u32[]{:S(2)}) collective-permute-start(f32[4,128,512]{2,1,0:T(8,128)S(1)} %get-tuple-element.379), channel_id=1, source_target_pairs={{0,8},{8,0},{16,24},{24,16},{1,9},{9,1},{17,25},{25,17},{2,10},{10... | collective-permute-start | bytes 3145736 | tf_op jit(solution)/shard_map/ppermute | solution.py:19
  118.1 46.3 %collective-permute-start.3 = (f32[4,128,512]{2,1,0:T(8,128)S(1)}, f32[4,128,512]{2,1,0:T(8,128)}, u32[]{:S(2)}, u32[]{:S(2)}) collective-permute-start(f32[4,128,512]{2,1,0:T(8,128)S(1)} %get-tuple-element.380), channel_id=1, source_target_pairs={{0,8},{8,0},{16,24},{24,16},{1,9},{9,1},{17,25},{25,17},{2,10},{10... | collective-permute-start | bytes 3145736 | tf_op jit(solution)/shard_map/ppermute | solution.py:19
  176.0 77.4 %all-gather.18.cloned.1.call-start = ((), (), s32[]{:S(2)}) async-start(), calls=%async_computation.1 | async-start | bytes 4718592 | tf_op jit(solution)/shard_map/all_gather | solution.py:26
  176.8 115.3 %all-gather.20.cloned.1.call-start = ((), (), s32[]{:S(2)}) async-start(), calls=%async_computation.2 | async-start | bytes 4718592 | tf_op jit(solution)/shard_map/all_gather | solution.py:26
  177.5 153.1 %all-gather.22.cloned.1.call-start = ((), (), s32[]{:S(2)}) async-start(), calls=%async_computation.3 | async-start | bytes 4718592 | tf_op jit(solution)/shard_map/all_gather | solution.py:26
  178.1 191.0 %all-gather.24.cloned.1.call-start = ((), (), s32[]{:S(2)}) async-start(), calls=%async_computation.4 | async-start | bytes 4718592 | tf_op jit(solution)/shard_map/all_gather | solution.py:26
  178.7 228.9 %all-gather.26.cloned.1.call-start = ((), (), s32[]{:S(2)}) async-start(), calls=%async_computation.5 | async-start | bytes 4718592 | tf_op jit(solution)/shard_map/all_gather | solution.py:26
  179.2 267.0 %all-gather.28.cloned.1.call-start = ((), (), s32[]{:S(2)}) async-start(), calls=%async_computation.6 | async-start | bytes 4718592 | tf_op jit(solution)/shard_map/all_gather | solution.py:26
  180.0 304.8 %all-gather.30.cloned.1.call-start = ((), (), s32[]{:S(2)}) async-start(), calls=%async_computation.7 | async-start | bytes 4718592 | tf_op jit(solution)/shard_map/all_gather | solution.py:26
  180.7 342.7 %all-gather.32.cloned.1.call-start = ((), (), s32[]{:S(2)}) async-start(), calls=%async_computation.8 | async-start | bytes 4718592 | tf_op jit(solution)/shard_map/all_gather | solution.py:26
  181.5 418.5 %all-gather.34.cloned.1.call-start = ((), (), s32[]{:S(2)}) async-start(), calls=%async_computation.9 | async-start | bytes 4718592 | tf_op jit(solution)/shard_map/all_gather | solution.py:26
  528.6 110.1 %all-gather.36.cloned.1.call-start = ((), (), s32[]{:S(2)}) async-start(), calls=%async_computation.10 | async-start | bytes 4718592 | tf_op jit(solution)/shard_map/all_gather | solution.py:26
  529.3 147.8 %all-gather.38.cloned.1.call-start = ((), (), s32[]{:S(2)}) async-start(), calls=%async_computation.11 | async-start | bytes 4718592 | tf_op jit(solution)/shard_map/all_gather | solution.py:26
  697.7 26.2 %copy-start.5 = (f32[4,128,512]{2,1,0:T(8,128)}, f32[4,128,512]{2,1,0:T(8,128)S(1)}, u32[]{:S(2)}) copy-start(f32[4,128,512]{2,1,0:T(8,128)S(1)} %get-tuple-element.386) | copy-start | bytes 3145732
  697.7 26.2 %collective-permute-start.4 = (f32[4,128,512]{2,1,0:T(8,128)S(1)}, f32[4,128,512]{2,1,0:T(8,128)S(1)}, u32[]{:S(2)}, u32[]{:S(2)}) collective-permute-start(f32[4,128,512]{2,1,0:T(8,128)S(1)} %get-tuple-element.385), channel_id=1, source_target_pairs={{0,8},{8,0},{16,24},{24,16},{1,9},{9,1},{17,25},{25,17},{2,10},{10... | collective-permute-start | bytes 3145736 | tf_op jit(solution)/shard_map/ppermute | solution.py:19
  699.2 44.6 %collective-permute-start.5 = (f32[4,128,512]{2,1,0:T(8,128)S(1)}, f32[4,128,512]{2,1,0:T(8,128)}, u32[]{:S(2)}, u32[]{:S(2)}) collective-permute-start(f32[4,128,512]{2,1,0:T(8,128)S(1)} %get-tuple-element.386), channel_id=1, source_target_pairs={{0,8},{8,0},{16,24},{24,16},{1,9},{9,1},{17,25},{25,17},{2,10},{10... | collective-permute-start | bytes 3145736 | tf_op jit(solution)/shard_map/ppermute | solution.py:19
  746.2 69.6 %collective-permute-start.6 = (f32[4,128,512]{2,1,0:T(8,128)S(1)}, f32[4,128,512]{2,1,0:T(8,128)S(1)}, u32[]{:S(2)}, u32[]{:S(2)}) collective-permute-start(f32[4,128,512]{2,1,0:T(8,128)S(1)} %get-tuple-element.375), channel_id=1, source_target_pairs={{0,16},{16,0},{8,24},{24,8},{1,17},{17,1},{9,25},{25,9},{2,18},{18... | collective-permute-start | bytes 3145736 | tf_op jit(solution)/shard_map/ppermute | solution.py:19
  748.7 88.6 %collective-permute-start.7 = (f32[4,128,512]{2,1,0:T(8,128)S(1)}, f32[4,128,512]{2,1,0:T(8,128)}, u32[]{:S(2)}, u32[]{:S(2)}) collective-permute-start(f32[4,128,512]{2,1,0:T(8,128)S(1)} %get-tuple-element.376), channel_id=1, source_target_pairs={{0,16},{16,0},{8,24},{24,8},{1,17},{17,1},{9,25},{25,9},{2,18},{18... | collective-permute-start | bytes 3145736 | tf_op jit(solution)/shard_map/ppermute | solution.py:19
  (8 other events, 29.6 us)
Sparse Core Ops, SparseCore 0:
  176.1 38.6 all-gather.15
  216.7 36.7 all-gather.17
  255.3 36.7 all-gather.19
  293.8 36.7 all-gather.21
  332.3 36.7 all-gather.23
  370.8 36.7 all-gather.25
  409.4 36.7 all-gather.27
  448.1 36.7 all-gather.29
  486.7 36.7 all-gather.31
  528.7 71.2 all-gather.33
  601.9 36.7 all-gather.35
  640.4 36.7 all-gather.37
where the time goes:
time: 867 us; the launch traced here: 860 us
  waiting for transfers between devices  754 us (87%)
  other arithmetic  37.5 us (4%)
  matrix products  36.8 us (4%)
  between operations  14.6 us (2%)
  starting transfers between devices  11.8 us (1%)
    all_gather x12, waiting for transfers between devices, entering(): gathered = jax.tree.map(lambda a: lax.all_gather(a, axis), part)  489 us
    ppermute x8, waiting for transfers between devices, swapped(): return lax.ppermute(block, axis, route)  259 us
  transfers between devices with their start and end apart: 20, of which 20 were waited for; matrix products, arithmetic and copies ran while one was open for 1% of the time, Pallas kernels for 0%

commit v1 on v0

v1 whole, which is shorter than its diff:
```python
import math

import numpy as np
import jax
import jax.numpy as jnp
from jax import lax
from jax.experimental import pallas as pl
from jax.experimental.pallas import tpu as pltpu
from jax.sharding import PartitionSpec as P

heat_loss = 4.0
spread_solute = 2.0
spread_heat = 100.0
SUB = 8
LANES = 128
VMEM_LIMIT = 48 * 1024 * 1024


def split_tables(n):
    half = n // 2
    y = np.arange(half)
    cols, freq = [], []
    for j in range(half // 2 + 1):
        k = 2 * j
        scale = math.sqrt((1.0 if k in (0, half) else 2.0) / n)
        cols.append(scale * np.cos(2 * np.pi * k * y / n))
        freq.append(k)
        if 0 < j < half // 2:
            cols.append(scale * np.sin(2 * np.pi * k * y / n))
            freq.append(k)
    even = np.stack(cols, 1)
    cols, odd_freq = [], []
    for j in range(half // 2):
        k = 2 * j + 1
        scale = math.sqrt(2.0 / n)
        cols.append(scale * np.cos(2 * np.pi * k * y / n))
        cols.append(scale * np.sin(2 * np.pi * k * y / n))
        odd_freq += [k, k]
    odd = np.stack(cols, 1)
    eig = 4.0 * np.sin(np.pi * np.array(freq + odd_freq) / n) ** 2
    return even, odd, eig.astype(np.float32)


def hi_lo(a):
    hi = jnp.asarray(a, jnp.float32).astype(jnp.bfloat16)
    lo = (jnp.asarray(a, jnp.float32) - hi.astype(jnp.float32)).astype(jnp.bfloat16)
    return hi, lo


def table_pair(a):
    bf16 = jnp.bfloat16
    hi = a.astype(np.float32).astype(bf16)
    lo = (a - hi.astype(np.float64)).astype(np.float32).astype(bf16)
    return hi, lo


def dot3(x, q_hi, q_lo, dims):
    hi, lo = hi_lo(x)
    dn = (dims, ((), ()))
    f32 = jnp.float32
    return (
        lax.dot_general(hi, q_hi, dn, preferred_element_type=f32)
        + lax.dot_general(hi, q_lo, dn, preferred_element_type=f32)
        + lax.dot_general(lo, q_hi, dn, preferred_element_type=f32)
    )


def cosine_forward(v):
    n = len(v)
    if n == 1:
        return [v[0]]
    h = n // 2
    sums = [v[z] + v[n - 1 - z] for z in range(h)]
    diffs = [v[z] - v[n - 1 - z] for z in range(h)]
    even = cosine_forward(sums)
    out = [None] * n
    for j in range(h):
        out[2 * j] = even[j]
        k = 2 * j + 1
        acc = None
        for z in range(h):
            term = diffs[z] * float(math.cos(math.pi * k * (z + 0.5) / n))
            acc = term if acc is None else acc + term
        out[k] = acc
    return out


def cosine_backward(c):
    n = len(c)
    if n == 1:
        return [c[0]]
    h = n // 2
    even = cosine_backward([c[2 * j] for j in range(h)])
    out = [None] * n
    for z in range(h):
        acc = None
        for j in range(h):
            k = 2 * j + 1
            term = c[k] * float(math.cos(math.pi * k * (z + 0.5) / n))
            acc = term if acc is None else acc + term
        out[z] = even[z] + acc
        out[n - 1 - z] = even[z] - acc
    return out


def line_factors(eig_rows, spread, layer_eig):
    rest = 1.0 + spread * (eig_rows + layer_eig)
    root = jnp.sqrt(rest * (rest + 4.0 * spread))
    decay = 2.0 * spread / (rest + 2.0 * spread + root)
    return decay, root


def power(base, exponent):
    out = None
    square = base
    while exponent:
        if exponent & 1:
            out = square if out is None else out * square
        exponent >>= 1
        if exponent:
            square = square * square
    return out


def sublane_powers(step_decay, row, reverse):
    out = jnp.ones_like(step_decay)
    factor = step_decay
    place = (SUB - 1 - row) if reverse else row
    for bit in range(3):
        out = jnp.where((place >> bit) & 1 == 1, out * factor, out)
        factor = factor * factor
    return out


def on_device_fn(fields, grain_ids, grain_rates, die_mask):
    depth = fields.shape[1]
    local_x = fields.shape[2]
    span_y = fields.shape[3]
    half = span_y // 2
    devices_x = lax.axis_size("gx")
    devices_z = lax.axis_size("gz")
    layers = depth * devices_z
    chunks = devices_z // 2
    lanes = span_y // chunks
    steps = local_x // SUB
    tiles = span_y // LANES
    grain_count = grain_rates.shape[0]
    even, odd, eig = split_tables(span_y)
    even_hi, even_lo = table_pair(even)
    odd_hi, odd_lo = table_pair(odd)
    tables = [jnp.asarray(t) for t in (even_hi, even_lo, odd_hi, odd_lo)]
    eig_table = jnp.asarray(eig.reshape(chunks, lanes))
    f32 = jnp.float32
    params = pltpu.CompilerParams(vmem_limit_bytes=VMEM_LIMIT)
    piece = (depth, steps, SUB, lanes)
    grain_run = min(steps, 8)
    mask_run = min(steps, 16)

    def source_kernel(rates, *rest):
        f_refs, id_refs, mask_refs = rest[:tiles], rest[tiles : 2 * tiles], rest[2 * tiles : 3 * tiles]
        eh, el, oh, ol = rest[3 * tiles : 3 * tiles + 4]
        outs = rest[3 * tiles + 4 : 3 * tiles + 4 + devices_z]
        sums, diffs, modes = rest[3 * tiles + 4 + devices_z :]
        g = lax.axis_index("gz")
        layer = pl.program_id(0)
        first = jnp.where(g * depth + layer == 0, heat_loss, 0.0)
        for tile in range(tiles // 2):
            pair = (tile, tile + tiles // 2)
            rates_c, rates_h, sinks = [None] * 2, [None] * 2, [None] * 2
            for xi in range(steps):
                at = pl.ds(xi, SUB, stride=steps)
                rhs = [[None] * 2, [None] * 2]
                for side in range(2):
                    if xi % grain_run == 0:
                        ids = id_refs[pair[side]][0, at, :]
                        rate_c = jnp.zeros(ids.shape, f32)
                        rate_h = jnp.zeros(ids.shape, f32)
                        for grain in range(grain_count):
                            hit = ids == grain
                            rate_c = jnp.where(hit, rates[grain, 0], rate_c)
                            rate_h = jnp.where(hit, rates[grain, 1], rate_h)
                        rates_c[side], rates_h[side] = rate_c, rate_h
                    if xi % mask_run == 0:
                        sinks[side] = mask_refs[pair[side]][at, :].astype(f32) * first
                    c = f_refs[pair[side]][0, 0, at, :]
                    h = f_refs[pair[side]][1, 0, at, :]
                    square = c * c
                    rhs[0][side] = c + rates_c[side] * jnp.tanh(h - c)
                    rhs[1][side] = (
                        h + rates_h[side] * square / (1.0 + square) - sinks[side] * (h + 1.0)
                    )
                for f in range(2):
                    rows = pl.ds((f * steps + xi) * SUB, SUB)
                    cols = pl.ds(tile * LANES, LANES)
                    sums[rows, cols] = rhs[f][0] + rhs[f][1]
                    diffs[rows, cols] = rhs[f][0] - rhs[f][1]
        dims = ((1,), (0,))
        for f in range(2):
            rows = pl.ds(f * local_x, local_x)
            both = (
                dot3(sums[rows, :], eh[...], el[...], dims),
                dot3(diffs[rows, :], oh[...], ol[...], dims),
            )
            for chunk in range(chunks):
                part = both[chunk * lanes // half]
                at = chunk * lanes % half
                modes[2 * chunk + f] = part[:, at : at + lanes].reshape(steps, SUB, lanes)
        for k in range(devices_z):
            outs[k][0] = modes[g ^ k]

    whole = lambda shape: pl.BlockSpec(shape, lambda i: (0,) * len(shape))
    id_step = 2 if depth % 2 == 0 else 1
    pieces = pl.pallas_call(
        source_kernel,
        grid=(depth,),
        in_specs=[
            pl.BlockSpec(memory_space=pltpu.SMEM),
        ]
        + [
            pl.BlockSpec((2, 1, local_x, LANES), lambda i, t=t: (0, i, 0, t))
            for t in range(tiles)
        ]
        + [
            pl.BlockSpec((1, local_x, LANES), lambda i, t=t: (i // id_step * id_step, 0, t))
            for t in range(tiles)
        ]
        + [pl.BlockSpec((local_x, LANES), lambda i, t=t: (0, t)) for t in range(tiles)]
        + [whole((half, half))] * 4,
        out_specs=[pl.BlockSpec((1, steps, SUB, lanes), lambda i: (i, 0, 0, 0))] * devices_z,
        out_shape=[jax.ShapeDtypeStruct(piece, f32)] * devices_z,
        scratch_shapes=[
            pltpu.VMEM((2 * local_x, half), f32),
            pltpu.VMEM((2 * local_x, half), f32),
            pltpu.VMEM((devices_z, steps, SUB, lanes), f32),
        ],
        compiler_params=params,
        name="sources",
    )(grain_rates, *([fields] * tiles + [grain_ids] * tiles + [die_mask] * tiles), *tables)

    def exchange(arrays, axis):
        count = lax.axis_size(axis)
        out = [arrays[0]]
        for k in range(1, count):
            out.append(lax.ppermute(arrays[k], axis, [(i, i ^ k) for i in range(count)]))
        return out

    gathered = exchange(pieces, "gz")

    def line_setup(eig_ref):
        g = lax.axis_index("gz")
        spread = jnp.where(g % 2 == 0, spread_solute, spread_heat).astype(f32)
        eig_rows = jnp.broadcast_to(eig_ref[pl.ds(g // 2, 1), :], (SUB, lanes))
        return g, spread, eig_rows

    layer_eig = [4.0 * math.sin(math.pi * k / (2 * layers)) ** 2 for k in range(layers)]

    def gather_kernel(eig_ref, *rest):
        ins = rest[: devices_z]
        hat_ref, from_left, from_right, ends, field, sems = rest[devices_z :]
        g, spread, eig_rows = line_setup(eig_ref)
        copies = []
        for k in range(devices_z):
            copies.append(
                pltpu.make_async_copy(ins[k], field.at[pl.ds((g ^ k) * depth, depth)], sems.at[k])
            )
            copies[-1].start()
        for copy in copies:
            copy.wait()

        def transform(xi, carry):
            hat = cosine_forward([field[z, xi] for z in range(layers)])
            for k in range(layers):
                hat_ref[k, xi] = hat[k]
            return carry

        lax.fori_loop(0, steps, transform, 0)
        row = lax.broadcasted_iota(jnp.int32, (SUB, lanes), 0)
        for k in range(layers):
            decay, _ = line_factors(eig_rows, spread, layer_eig[k])
            left = hat_ref[k, 0]
            right = hat_ref[k, steps - 1]
            for xi in range(1, steps):
                left = hat_ref[k, xi] + decay * left
                right = hat_ref[k, steps - 1 - xi] + decay * right
            step_decay = power(decay, steps)
            up = sublane_powers(step_decay, row, False)
            down = sublane_powers(step_decay, row, True)
            ends[0, pl.ds(k, 1), :] = jnp.sum(left * down, axis=0, keepdims=True)
            ends[1, pl.ds(k, 1), :] = jnp.sum(right * up, axis=0, keepdims=True)
            left = jnp.where(row >= 1, pltpu.roll(left, 1, 0), 0.0)
            right = jnp.where(row < SUB - 1, pltpu.roll(right, SUB - 1, 0), 0.0)
            factor = step_decay
            for shift in (1, 2, 4):
                left = left + factor * jnp.where(row >= shift, pltpu.roll(left, shift, 0), 0.0)
                right = right + factor * jnp.where(
                    row < SUB - shift, pltpu.roll(right, SUB - shift, 0), 0.0
                )
                factor = factor * factor
            from_left[k] = left
            from_right[k] = right

    vmem = pl.BlockSpec(memory_space=pltpu.VMEM)
    anywhere = pl.BlockSpec(memory_space=pl.ANY)
    hat, from_left, from_right, ends = pl.pallas_call(
        gather_kernel,
        in_specs=[vmem] + [anywhere] * devices_z,
        out_specs=[vmem] * 4,
        out_shape=[
            jax.ShapeDtypeStruct((layers, steps, SUB, lanes), f32),
            jax.ShapeDtypeStruct((layers, SUB, lanes), f32),
            jax.ShapeDtypeStruct((layers, SUB, lanes), f32),
            jax.ShapeDtypeStruct((2, layers, lanes), f32),
        ],
        scratch_shapes=[
            pltpu.VMEM((layers, steps, SUB, lanes), f32),
            pltpu.SemaphoreType.DMA((devices_z,)),
        ],
        compiler_params=params,
        name="gather",
    )(eig_table, *gathered)

    all_ends = exchange([ends] * devices_x, "gx")

    def solve_kernel(eig_ref, hat_ref, left_ref, right_ref, *rest):
        end_refs = rest[: devices_x]
        outs = rest[devices_x : devices_x + devices_z]
        near, work, entry, end_sems, sems = rest[devices_x + devices_z :]
        g, spread, eig_rows = line_setup(eig_ref)
        place = lax.axis_index("gx")
        copies = []
        for k in range(devices_x):
            copies.append(pltpu.make_async_copy(end_refs[k], near.at[place ^ k], end_sems.at[k]))
            copies[-1].start()
        for copy in copies:
            copy.wait()
        row = lax.broadcasted_iota(jnp.int32, (SUB, lanes), 0)
        eig_one = eig_ref[pl.ds(g // 2, 1), :]
        kz = lax.broadcasted_iota(jnp.int32, (layers, lanes), 0).astype(f32)
        eig_z = 4.0 * jnp.sin(kz * (math.pi / (2 * layers))) ** 2
        decay_all, _ = line_factors(eig_one, spread, eig_z)
        block_decay = power(decay_all, local_x)
        total_left = near[(place + devices_x - 1) % devices_x, 0]
        total_right = near[(place + 1) % devices_x, 1]
        weight = block_decay
        for m in range(2, devices_x + 1):
            total_left = total_left + weight * near[(place + devices_x - m) % devices_x, 0]
            total_right = total_right + weight * near[(place + m) % devices_x, 1]
            weight = weight * block_decay
        entry[0] = total_left / (1.0 - weight)
        entry[1] = total_right / (1.0 - weight)
        for k in range(layers):
            decay, root = line_factors(eig_rows, spread, layer_eig[k])
            gain = ((1.0 if k == 0 else 2.0) / layers) / root
            step_decay = power(decay, steps)
            up = sublane_powers(step_decay, row, False)
            down = sublane_powers(step_decay, row, True)
            left = left_ref[k] + up * entry[0, pl.ds(k, 1), :]
            right = right_ref[k] + down * entry[1, pl.ds(k, 1), :]
            for xi in range(steps):
                left = hat_ref[k, xi] + decay * left
                work[k, xi] = left
            for xi in reversed(range(steps)):
                carried = decay * right
                work[k, xi] = gain * (work[k, xi] + carried)
                right = hat_ref[k, xi] + carried

        def back(xi, carry):
            values = cosine_backward([work[k, xi] for k in range(layers)])
            for z in range(layers):
                work[z, xi] = values[z]
            return carry

        lax.fori_loop(0, steps, back, 0)
        copies = []
        for k in range(devices_z):
            copies.append(
                pltpu.make_async_copy(work.at[pl.ds((g ^ k) * depth, depth)], outs[k], sems.at[k])
            )
            copies[-1].start()
        for copy in copies:
            copy.wait()

    solved = pl.pallas_call(
        solve_kernel,
        in_specs=[vmem] * 4 + [anywhere] * devices_x,
        out_specs=[anywhere] * devices_z,
        out_shape=[jax.ShapeDtypeStruct(piece, f32)] * devices_z,
        scratch_shapes=[
            pltpu.VMEM((devices_x, 2, layers, lanes), f32),
            pltpu.VMEM((layers, steps, SUB, lanes), f32),
            pltpu.VMEM((2, layers, lanes), f32),
            pltpu.SemaphoreType.DMA((devices_x,)),
            pltpu.SemaphoreType.DMA((devices_z,)),
        ],
        compiler_params=params,
        name="solve",
    )(eig_table, hat, from_left, from_right, *all_ends)

    returned = exchange(solved, "gz")

    def final_kernel(eh, el, oh, ol, *rest):
        ins = rest[: devices_z]
        out_ref, modes, buf, sems, out_sems = rest[devices_z :]
        g = lax.axis_index("gz")
        step = pl.program_id(0)

        @pl.when(step == 0)
        def _():
            copies = []
            for k in range(devices_z):
                copies.append(pltpu.make_async_copy(ins[k], modes.at[g ^ k], sems.at[k]))
                copies[-1].start()
            for copy in copies:
                copy.wait()

        f = step // depth
        layer = step % depth
        parts = [
            modes[2 * chunk + f, layer].reshape(local_x, lanes) for chunk in range(chunks)
        ]
        dims = ((1,), (1,))
        low = dot3(jnp.concatenate(parts[: chunks // 2], axis=1), eh[...], el[...], dims)
        high = dot3(jnp.concatenate(parts[chunks // 2 :], axis=1), oh[...], ol[...], dims)
        total = low + high
        other = low - high
        slot = step % 2

        def out_copies(step, slot):
            where = out_ref.at[step // depth, step % depth]
            return [
                pltpu.make_async_copy(
                    buf.at[slot, t], where.at[:, pl.ds(t * LANES, LANES)], out_sems.at[slot, t]
                )
                for t in range(tiles)
            ]

        @pl.when(step >= 2)
        def _():
            for copy in out_copies(step - 2, slot):
                copy.wait()

        for t in range(tiles):
            value = total if t < tiles // 2 else other
            at = t % (tiles // 2) * LANES
            for xi in range(steps):
                buf[slot, t, pl.ds(xi, SUB, stride=steps), :] = value[
                    xi * SUB : xi * SUB + SUB, at : at + LANES
                ]
        for copy in out_copies(step, slot):
            copy.start()

        @pl.when(step == 2 * depth - 1)
        def _():
            for back in (1, 0):
                for copy in out_copies(step - back, (step - back) % 2):
                    copy.wait()

    return pl.pallas_call(
        final_kernel,
        grid=(2 * depth,),
        in_specs=[whole((half, half))] * 4 + [anywhere] * devices_z,
        out_specs=anywhere,
        out_shape=jax.ShapeDtypeStruct((2, depth, local_x, span_y), f32),
        scratch_shapes=[
            pltpu.VMEM((devices_z, depth, steps, SUB, lanes), f32),
            pltpu.VMEM((2, tiles, local_x, LANES), f32),
            pltpu.SemaphoreType.DMA((devices_z,)),
            pltpu.SemaphoreType.DMA((2, tiles)),
        ],
        compiler_params=params,
        name="finish",
    )(*tables, *returned)


def solution(mesh):
    placed = (P(None, "gz", "gx", None), P("gz", "gx", None), P(), P("gx", None))
    return jax.shard_map(
        on_device_fn, mesh=mesh, in_specs=placed, out_specs=P(None, "gz", "gx", None), check_vma=False
    )
```

time: 867 us -> 60.7 us (0.07)
  waiting for transfers between devices: 754 us -> 19.7 us
  other arithmetic: 37.5 us -> 0 us
  matrix products: 36.8 us -> 0 us
  between operations: 14.6 us -> 0.11 us
  Pallas kernels: 0 us -> 11.8 us
  starting transfers between devices: 11.8 us -> 21.2 us
    all_gather x12 -> x0, waiting for transfers between devices: 489 us -> none  [entering(): gathered = jax.tree.map(lambda a: lax.all_gather(a, axis), part)]
    ppermute x8 -> x17, waiting for transfers between devices: 259 us -> 19.7 us  [exchange(): lax.ppermute(arrays[k], axis, [(i, i ^ k) for i in range(count)])]
    dot_general x12 -> x0, matrix products: 36.8 us -> none  [the longest x8 10.9 us: contract(): jnp.einsum(form, left_side, right_side, precision=exact, preferred_elemen...]
    add x13 -> x0, other arithmetic: 22.7 us -> none  [the longest x8 15.3 us: compose_affine(): later[0] * earlier[2] + later[2]]
    pallas_call x0 -> x4, Pallas kernels: none -> 11.8 us  [the longest x1 4.25 us: on_device_fn(): pl.pallas_call(final_kernel, grid=(2 * depth,), in_specs=[whole((half, ha...]
    ppermute x8 -> x17, starting transfers between devices: 11.4 us -> 21.2 us  [exchange(): lax.ppermute(arrays[k], axis, [(i, i ^ k) for i in range(count)])]
  transfers between devices with their start and end apart: 20 -> 17, of which waited for: 20 -> 7; matrix products, arithmetic and copies ran while one was open for 1% -> 0% of each run, Pallas kernels for 0% -> 0%
where the time goes in v1:
time: 60.7 us; the launch traced here: 60.4 us
  starting transfers between devices  21.2 us (35%)
  waiting for transfers between devices  19.7 us (32%)
  Pallas kernels  11.8 us (19%)
  local copies, waits for them, and re-layouts  7.61 us (13%)
    ppermute x17, starting transfers between devices, exchange(): lax.ppermute(arrays[k], axis, [(i, i ^ k) for i in range(count)])  21.2 us
    ppermute x17, waiting for transfers between devices, exchange(): lax.ppermute(arrays[k], axis, [(i, i ^ k) for i in range(count)])  19.7 us
    unnamed x25, local copies, waits for them, and re-layouts  7.61 us
    pallas_call x1, Pallas kernels, on_device_fn(): pl.pallas_call(final_kernel, grid=(2 * depth,), in_specs=[whole((half, ha...  4.25 us
    pallas_call x1, Pallas kernels, on_device_fn(): pl.pallas_call(solve_kernel, in_specs=[vmem] * 4 + [anywhere] * devices_x...  2.65 us
    pallas_call x1, Pallas kernels, on_device_fn(): pl.pallas_call(source_kernel, grid=(depth,), in_specs=[pl.BlockSpec(memor...  2.52 us
    pallas_call x1, Pallas kernels, on_device_fn(): pl.pallas_call(gather_kernel, in_specs=[vmem] + [anywhere] * devices_z, o...  2.36 us
  transfers between devices with their start and end apart: 17, of which 7 were waited for; matrix products, arithmetic and copies ran while one was open for 0% of the time, Pallas kernels for 0%

profile of v1, /device:TPU:0, one launch (start us, length us, event | category | flops | bytes accessed | tf_op | source)
XLA Modules:
  0.0 60.4 jit_solution(2134868620782279347)
XLA Ops:
  0.8 1.2 %copy-done = f32[2,2,128,512]{3,2,1,0:T(8,128)S(1)} copy-done((f32[2,2,128,512]{3,2,1,0:T(8,128)S(1)}, f32[2,2,128,512]{3,2,1,0:T(8,128)}, u32[]{:S(2)}) %copy-start) | copy-done | bytes 1048600
  2.0 1.0 %copy-done.1 = s32[2,128,512]{2,1,0:T(8,128)S(1)} copy-done((s32[2,128,512]{2,1,0:T(8,128)S(1)}, s32[2,128,512]{2,1,0:T(8,128)}, u32[]{:S(2)}) %copy-start.1) | copy-done | bytes 524312
  3.0 0.9 %copy-done.2 = s32[128,512]{1,0:T(8,128)S(1)} copy-done((s32[128,512]{1,0:T(8,128)S(1)}, s32[128,512]{1,0:T(8,128)}, u32[]{:S(2)}) %copy-start.2) | copy-done | bytes 262168
  4.0 0.9 %copy-done.3 = bf16[256,256]{1,0:T(8,128)(2,1)S(1)} copy-done((bf16[256,256]{1,0:T(8,128)(2,1)S(1)}, bf16[256,256]{1,0:T(8,128)(2,1)}, u32[]{:S(2)}) %copy-start.3) | copy-done | bytes 131096
  4.9 0.9 %copy-done.5 = bf16[256,256]{1,0:T(8,128)(2,1)S(1)} copy-done((bf16[256,256]{1,0:T(8,128)(2,1)S(1)}, bf16[256,256]{1,0:T(8,128)(2,1)}, u32[]{:S(2)}) %copy-start.5) | copy-done | bytes 131096
  5.8 0.9 %copy-done.7 = bf16[256,256]{1,0:T(8,128)(2,1)S(1)} copy-done((bf16[256,256]{1,0:T(8,128)(2,1)S(1)}, bf16[256,256]{1,0:T(8,128)(2,1)}, u32[]{:S(2)}) %copy-start.7) | copy-done | bytes 131096
  6.7 0.9 %copy-done.9 = bf16[256,256]{1,0:T(8,128)(2,1)S(1)} copy-done((bf16[256,256]{1,0:T(8,128)(2,1)S(1)}, bf16[256,256]{1,0:T(8,128)(2,1)}, u32[]{:S(2)}) %copy-start.9) | copy-done | bytes 131096
  7.6 2.5 %sources.1 = (f32[2,16,8,128]{3,2,1,0:T(8,128)S(1)}, f32[2,16,8,128]{3,2,1,0:T(8,128)S(1)}, f32[2,16,8,128]{3,2,1,0:T(8,128)S(1)}, f32[2,16,8,128]{3,2,1,0:T(8,1...) custom-call(f32[32,2]{1,0:T(8,128)S(1)} %copy.10.rates, ...), custom_call_target="tpu_custom_call" | custom-call | tf_op jit(solution)/shard_map/sources/pallas_call | solution.py:213
  10.6 2.6 %collective-permute-start.1 = (f32[2,16,8,128]{3,2,1,0:T(8,128)S(1)}, f32[2,16,8,128]{3,2,1,0:T(8,128)S(1)}, u32[]{:S(2)}, u32[]{:S(2)}) collective-permute-start(f32[2,16,8,128]{3,2,1,0:T(8,128)S(1)} %get-tuple-element.27), channel_id=1, source_target_pairs={{0,2},{1,3},{2,0},{3,1},{4,6},{5,7},{6,4},{7,5},{8,10},{9,11},{10,... | collective-permute-start | bytes 393224 | tf_op jit(solution)/shard_map/ppermute | solution.py:244
  13.3 1.8 %collective-permute-start.3 = (f32[2,16,8,128]{3,2,1,0:T(8,128)S(1)}, f32[2,16,8,128]{3,2,1,0:T(8,128)S(1)}, u32[]{:S(2)}, u32[]{:S(2)}) collective-permute-start(f32[2,16,8,128]{3,2,1,0:T(8,128)S(1)} %get-tuple-element.29), channel_id=1, source_target_pairs={{0,4},{1,5},{2,6},{3,7},{4,0},{5,1},{6,2},{7,3},{8,12},{9,13},{10,... | collective-permute-start | bytes 393224 | tf_op jit(solution)/shard_map/ppermute | solution.py:244
  15.1 2.6 %collective-permute-start.5 = (f32[2,16,8,128]{3,2,1,0:T(8,128)S(1)}, f32[2,16,8,128]{3,2,1,0:T(8,128)S(1)}, u32[]{:S(2)}, u32[]{:S(2)}) collective-permute-start(f32[2,16,8,128]{3,2,1,0:T(8,128)S(1)} %get-tuple-element.31), channel_id=1, source_target_pairs={{0,6},{1,7},{2,4},{3,5},{4,2},{5,3},{6,0},{7,1},{8,14},{9,15},{10,... | collective-permute-start | bytes 393224 | tf_op jit(solution)/shard_map/ppermute | solution.py:244
  17.7 1.6 %collective-permute-start.6 = (f32[2,16,8,128]{3,2,1,0:T(8,128)S(1)}, f32[2,16,8,128]{3,2,1,0:T(8,128)S(1)}, u32[]{:S(2)}, u32[]{:S(2)}) collective-permute-start(f32[2,16,8,128]{3,2,1,0:T(8,128)S(1)} %get-tuple-element.32), channel_id=1, source_target_pairs={{0,7},{1,6},{2,5},{3,4},{4,3},{5,2},{6,1},{7,0},{8,15},{9,14},{10,... | collective-permute-start | bytes 393224 | tf_op jit(solution)/shard_map/ppermute | solution.py:244
  19.8 6.9 %collective-permute-done.4.rest_5_ = f32[2,16,8,128]{3,2,1,0:T(8,128)S(1)} collective-permute-done((f32[2,16,8,128]{3,2,1,0:T(8,128)S(1)}, f32[2,16,8,128]{3,2,1,0:T(8,128)S(1)}, u32[]{:S(2)}, u32[]{:S(2)}) %collective-permute-start.4) | collective-permute-done | bytes 131104 | tf_op jit(solution)/shard_map/ppermute | solution.py:244
  26.7 2.4 %gather.1 = (f32[16,16,8,128]{3,2,1,0:T(8,128)S(1)}, f32[16,8,128]{2,1,0:T(8,128)S(1)}, f32[16,8,128]{2,1,0:T(8,128)S(1)}, f32[2,16,128]{2,1,0:T(8,128)S(1)}) custom-call(f32[4,128]{1,0:T(4,128)S(1)} %copy-done.11, f32[2,16,8,128]{3,2,1,0:T(8,128)S(1)} %get-tuple-element.25.rest_0_, f32[2,16,8,128]{3,2,1,0:T(8,128)S(1)} %collective-permute-done.rest_1_, ...), custom_call_target="tpu_custom_call" | custom-call | tf_op jit(solution)/shard_map/gather/pallas_call | solution.py:304
  29.1 4.1 %collective-permute-start.9 = (f32[2,16,128]{2,1,0:T(8,128)S(1)}, f32[2,16,128]{2,1,0:T(8,128)S(1)}, u32[]{:S(2)}, u32[]{:S(2)}) collective-permute-start(f32[2,16,128]{2,1,0:T(8,128)S(1)} %get-tuple-element.36.rest_0_), channel_id=1, source_target_pairs={{0,24},{8,16},{16,8},{24,0},{1,25},{9,17},{17,9},{25,1},{2,26},{10... | collective-permute-start | bytes 49160 | tf_op jit(solution)/shard_map/ppermute | solution.py:244
  33.8 1.0 %collective-permute-done.9.rest_3_ = f32[2,16,128]{2,1,0:T(8,128)S(1)} collective-permute-done((f32[2,16,128]{2,1,0:T(8,128)S(1)}, f32[2,16,128]{2,1,0:T(8,128)S(1)}, u32[]{:S(2)}, u32[]{:S(2)}) %collective-permute-start.9) | collective-permute-done | bytes 16416 | tf_op jit(solution)/shard_map/ppermute | solution.py:244
  34.9 2.9 %collective-permute-done.8.rest_2_ = f32[2,16,128]{2,1,0:T(8,128)S(1)} collective-permute-done((f32[2,16,128]{2,1,0:T(8,128)S(1)}, f32[2,16,128]{2,1,0:T(8,128)S(1)}, u32[]{:S(2)}, u32[]{:S(2)}) %collective-permute-start.8) | collective-permute-done | bytes 16416 | tf_op jit(solution)/shard_map/ppermute | solution.py:244
  37.9 2.6 %solve.1 = (f32[2,16,8,128]{3,2,1,0:T(8,128)S(1)}, f32[2,16,8,128]{3,2,1,0:T(8,128)S(1)}, f32[2,16,8,128]{3,2,1,0:T(8,128)S(1)}, f32[2,16,8,128]{3,2,1,0:T(8,128...) custom-call(f32[4,128]{1,0:T(4,128)S(1)} %copy-done.11, ...), custom_call_target="tpu_custom_call" | custom-call | tf_op jit(solution)/shard_map/solve/pallas_call | solution.py:383
  40.6 1.6 %collective-permute-start.11 = (f32[2,16,8,128]{3,2,1,0:T(8,128)S(1)}, f32[2,16,8,128]{3,2,1,0:T(8,128)S(1)}, u32[]{:S(2)}, u32[]{:S(2)}) collective-permute-start(f32[2,16,8,128]{3,2,1,0:T(8,128)S(1)} %get-tuple-element.39), channel_id=1, source_target_pairs={{0,2},{1,3},{2,0},{3,1},{4,6},{5,7},{6,4},{7,5},{8,10},{9,11},{10,... | collective-permute-start | bytes 393224 | tf_op jit(solution)/shard_map/ppermute | solution.py:244
  42.5 1.5 %collective-permute-start.13 = (f32[2,16,8,128]{3,2,1,0:T(8,128)S(1)}, f32[2,16,8,128]{3,2,1,0:T(8,128)S(1)}, u32[]{:S(2)}, u32[]{:S(2)}) collective-permute-start(f32[2,16,8,128]{3,2,1,0:T(8,128)S(1)} %get-tuple-element.41), channel_id=1, source_target_pairs={{0,4},{1,5},{2,6},{3,7},{4,0},{5,1},{6,2},{7,3},{8,12},{9,13},{10,... | collective-permute-start | bytes 393224 | tf_op jit(solution)/shard_map/ppermute | solution.py:244
  44.2 2.4 %collective-permute-start.15 = (f32[2,16,8,128]{3,2,1,0:T(8,128)S(1)}, f32[2,16,8,128]{3,2,1,0:T(8,128)S(1)}, u32[]{:S(2)}, u32[]{:S(2)}) collective-permute-start(f32[2,16,8,128]{3,2,1,0:T(8,128)S(1)} %get-tuple-element.43), channel_id=1, source_target_pairs={{0,6},{1,7},{2,4},{3,5},{4,2},{5,3},{6,0},{7,1},{8,14},{9,15},{10,... | collective-permute-start | bytes 393224 | tf_op jit(solution)/shard_map/ppermute | solution.py:244
  47.0 1.3 %collective-permute-start.16 = (f32[2,16,8,128]{3,2,1,0:T(8,128)S(1)}, f32[2,16,8,128]{3,2,1,0:T(8,128)S(1)}, u32[]{:S(2)}, u32[]{:S(2)}) collective-permute-start(f32[2,16,8,128]{3,2,1,0:T(8,128)S(1)} %get-tuple-element.44), channel_id=1, source_target_pairs={{0,7},{1,6},{2,5},{3,4},{4,3},{5,2},{6,1},{7,0},{8,15},{9,14},{10,... | collective-permute-start | bytes 393224 | tf_op jit(solution)/shard_map/ppermute | solution.py:244
  48.9 7.2 %collective-permute-done.14.rest_5_ = f32[2,16,8,128]{3,2,1,0:T(8,128)S(1)} collective-permute-done((f32[2,16,8,128]{3,2,1,0:T(8,128)S(1)}, f32[2,16,8,128]{3,2,1,0:T(8,128)S(1)}, u32[]{:S(2)}, u32[]{:S(2)}) %collective-permute-start.14) | collective-permute-done | bytes 131104 | tf_op jit(solution)/shard_map/ppermute | solution.py:244
  56.1 4.3 %finish.1 = f32[2,2,128,512]{3,2,1,0:T(8,128)} custom-call(bf16[256,256]{1,0:T(8,128)(2,1)S(1)} %copy-done.10, bf16[256,256]{1,0:T(8,128)(2,1)S(1)} %copy-done.8, bf16[256,256]{1,0:T(8,128)(2,1)S(1)} %copy-done.6, bf16[256,256]{1,0:T(8,128)(2,1)S(1)} %copy-done.4, f32[2,16,8,128]{3,2,1,0:T(8,128)S(1)} %get-tuple-element.37.rest_0_, ...), custom_call_target="tpu_custom_call" | custom-call | tf_op jit(solution)/shard_map/finish/pallas_call | solution.py:458
  (39 shorter events, 4.2 us)
Async XLA Ops:
  0.8 1.2 %copy-start = (f32[2,2,128,512]{3,2,1,0:T(8,128)S(1)}, f32[2,2,128,512]{3,2,1,0:T(8,128)}, u32[]{:S(2)}) copy-start(f32[2,2,128,512]{3,2,1,0:T(8,128)} %rest_3_.1) | copy-start | bytes 3145732
  2.0 1.0 %copy-start.1 = (s32[2,128,512]{2,1,0:T(8,128)S(1)}, s32[2,128,512]{2,1,0:T(8,128)}, u32[]{:S(2)}) copy-start(s32[2,128,512]{2,1,0:T(8,128)} %rest_7_.1) | copy-start | bytes 1572868
  10.1 4.9 %collective-permute-start = (f32[2,16,8,128]{3,2,1,0:T(8,128)S(1)}, f32[2,16,8,128]{3,2,1,0:T(8,128)S(1)}, u32[]{:S(2)}, u32[]{:S(2)}) collective-permute-start(f32[2,16,8,128]{3,2,1,0:T(8,128)S(1)} %get-tuple-element.26), channel_id=1, source_target_pairs={{0,1},{1,0},{2,3},{3,2},{4,5},{5,4},{6,7},{7,6},{8,9},{9,8},{10,11... | collective-permute-start | bytes 393224 | tf_op jit(solution)/shard_map/ppermute | solution.py:244
  10.6 7.0 %collective-permute-start.1 = (f32[2,16,8,128]{3,2,1,0:T(8,128)S(1)}, f32[2,16,8,128]{3,2,1,0:T(8,128)S(1)}, u32[]{:S(2)}, u32[]{:S(2)}) collective-permute-start(f32[2,16,8,128]{3,2,1,0:T(8,128)S(1)} %get-tuple-element.27), channel_id=1, source_target_pairs={{0,2},{1,3},{2,0},{3,1},{4,6},{5,7},{6,4},{7,5},{8,10},{9,11},{10,... | collective-permute-start | bytes 393224 | tf_op jit(solution)/shard_map/ppermute | solution.py:244
  13.2 6.6 %collective-permute-start.2 = (f32[2,16,8,128]{3,2,1,0:T(8,128)S(1)}, f32[2,16,8,128]{3,2,1,0:T(8,128)S(1)}, u32[]{:S(2)}, u32[]{:S(2)}) collective-permute-start(f32[2,16,8,128]{3,2,1,0:T(8,128)S(1)} %get-tuple-element.28), channel_id=1, source_target_pairs={{0,3},{1,2},{2,1},{3,0},{4,7},{5,6},{6,5},{7,4},{8,11},{9,10},{10,... | collective-permute-start | bytes 393224 | tf_op jit(solution)/shard_map/ppermute | solution.py:244
  13.3 6.6 %collective-permute-start.3 = (f32[2,16,8,128]{3,2,1,0:T(8,128)S(1)}, f32[2,16,8,128]{3,2,1,0:T(8,128)S(1)}, u32[]{:S(2)}, u32[]{:S(2)}) collective-permute-start(f32[2,16,8,128]{3,2,1,0:T(8,128)S(1)} %get-tuple-element.29), channel_id=1, source_target_pairs={{0,4},{1,5},{2,6},{3,7},{4,0},{5,1},{6,2},{7,3},{8,12},{9,13},{10,... | collective-permute-start | bytes 393224 | tf_op jit(solution)/shard_map/ppermute | solution.py:244
  15.0 11.7 %collective-permute-start.4 = (f32[2,16,8,128]{3,2,1,0:T(8,128)S(1)}, f32[2,16,8,128]{3,2,1,0:T(8,128)S(1)}, u32[]{:S(2)}, u32[]{:S(2)}) collective-permute-start(f32[2,16,8,128]{3,2,1,0:T(8,128)S(1)} %get-tuple-element.30), channel_id=1, source_target_pairs={{0,5},{1,4},{2,7},{3,6},{4,1},{5,0},{6,3},{7,2},{8,13},{9,12},{10,... | collective-permute-start | bytes 393224 | tf_op jit(solution)/shard_map/ppermute | solution.py:244
  15.1 11.7 %copy-start.11 = (f32[4,128]{1,0:T(4,128)S(1)}, f32[4,128]{1,0:T(4,128)}, u32[]{:S(2)}) copy-start(f32[4,128]{1,0:T(4,128)} %constant.14.clone.eig_ref) | copy-start | bytes 6148
  15.1 11.7 %collective-permute-start.5 = (f32[2,16,8,128]{3,2,1,0:T(8,128)S(1)}, f32[2,16,8,128]{3,2,1,0:T(8,128)S(1)}, u32[]{:S(2)}, u32[]{:S(2)}) collective-permute-start(f32[2,16,8,128]{3,2,1,0:T(8,128)S(1)} %get-tuple-element.31), channel_id=1, source_target_pairs={{0,6},{1,7},{2,4},{3,5},{4,2},{5,3},{6,0},{7,1},{8,14},{9,15},{10,... | collective-permute-start | bytes 393224 | tf_op jit(solution)/shard_map/ppermute | solution.py:244
  17.7 9.1 %collective-permute-start.6 = (f32[2,16,8,128]{3,2,1,0:T(8,128)S(1)}, f32[2,16,8,128]{3,2,1,0:T(8,128)S(1)}, u32[]{:S(2)}, u32[]{:S(2)}) collective-permute-start(f32[2,16,8,128]{3,2,1,0:T(8,128)S(1)} %get-tuple-element.32), channel_id=1, source_target_pairs={{0,7},{1,6},{2,5},{3,4},{4,3},{5,2},{6,1},{7,0},{8,15},{9,14},{10,... | collective-permute-start | bytes 393224 | tf_op jit(solution)/shard_map/ppermute | solution.py:244
  29.1 5.8 %collective-permute-start.9 = (f32[2,16,128]{2,1,0:T(8,128)S(1)}, f32[2,16,128]{2,1,0:T(8,128)S(1)}, u32[]{:S(2)}, u32[]{:S(2)}) collective-permute-start(f32[2,16,128]{2,1,0:T(8,128)S(1)} %get-tuple-element.36.rest_0_), channel_id=1, source_target_pairs={{0,24},{8,16},{16,8},{24,0},{1,25},{9,17},{17,9},{25,1},{2,26},{10... | collective-permute-start | bytes 49160 | tf_op jit(solution)/shard_map/ppermute | solution.py:244
  33.2 4.6 %collective-permute-start.8 = (f32[2,16,128]{2,1,0:T(8,128)S(1)}, f32[2,16,128]{2,1,0:T(8,128)S(1)}, u32[]{:S(2)}, u32[]{:S(2)}) collective-permute-start(f32[2,16,128]{2,1,0:T(8,128)S(1)} %get-tuple-element.36.rest_0_), channel_id=1, source_target_pairs={{0,16},{8,24},{16,0},{24,8},{1,17},{9,25},{17,1},{25,9},{2,18},{10... | collective-permute-start | bytes 49160 | tf_op jit(solution)/shard_map/ppermute | solution.py:244
  33.2 4.6 %collective-permute-start.7 = (f32[2,16,128]{2,1,0:T(8,128)S(1)}, f32[2,16,128]{2,1,0:T(8,128)S(1)}, u32[]{:S(2)}, u32[]{:S(2)}) collective-permute-start(f32[2,16,128]{2,1,0:T(8,128)S(1)} %get-tuple-element.36.rest_0_), channel_id=1, source_target_pairs={{0,8},{8,0},{16,24},{24,16},{1,9},{9,1},{17,25},{25,17},{2,10},{10... | collective-permute-start | bytes 49160 | tf_op jit(solution)/shard_map/ppermute | solution.py:244
  37.8 18.2 %copy-start.4 = (bf16[256,256]{1,0:T(8,128)(2,1)S(1)}, bf16[256,256]{1,0:T(8,128)(2,1)}, u32[]{:S(2)}) copy-start(bf16[256,256]{1,0:T(8,128)(2,1)} %constant.13.clone.rest_15_.ol) | copy-start | bytes 393220
  37.8 18.2 %copy-start.6 = (bf16[256,256]{1,0:T(8,128)(2,1)S(1)}, bf16[256,256]{1,0:T(8,128)(2,1)}, u32[]{:S(2)}) copy-start(bf16[256,256]{1,0:T(8,128)(2,1)} %constant.12.clone.rest_14_.oh) | copy-start | bytes 393220
  37.8 18.2 %copy-start.8 = (bf16[256,256]{1,0:T(8,128)(2,1)S(1)}, bf16[256,256]{1,0:T(8,128)(2,1)}, u32[]{:S(2)}) copy-start(bf16[256,256]{1,0:T(8,128)(2,1)} %constant.11.clone.rest_13_.el) | copy-start | bytes 393220
  37.8 18.2 %copy-start.10 = (bf16[256,256]{1,0:T(8,128)(2,1)S(1)}, bf16[256,256]{1,0:T(8,128)(2,1)}, u32[]{:S(2)}) copy-start(bf16[256,256]{1,0:T(8,128)(2,1)} %constant.10.clone.rest_12_.eh) | copy-start | bytes 393220
  40.5 3.6 %collective-permute-start.10 = (f32[2,16,8,128]{3,2,1,0:T(8,128)S(1)}, f32[2,16,8,128]{3,2,1,0:T(8,128)S(1)}, u32[]{:S(2)}, u32[]{:S(2)}) collective-permute-start(f32[2,16,8,128]{3,2,1,0:T(8,128)S(1)} %get-tuple-element.38), channel_id=1, source_target_pairs={{0,1},{1,0},{2,3},{3,2},{4,5},{5,4},{6,7},{7,6},{8,9},{9,8},{10,11... | collective-permute-start | bytes 393224 | tf_op jit(solution)/shard_map/ppermute | solution.py:244
  40.6 6.4 %collective-permute-start.11 = (f32[2,16,8,128]{3,2,1,0:T(8,128)S(1)}, f32[2,16,8,128]{3,2,1,0:T(8,128)S(1)}, u32[]{:S(2)}, u32[]{:S(2)}) collective-permute-start(f32[2,16,8,128]{3,2,1,0:T(8,128)S(1)} %get-tuple-element.39), channel_id=1, source_target_pairs={{0,2},{1,3},{2,0},{3,1},{4,6},{5,7},{6,4},{7,5},{8,10},{9,11},{10,... | collective-permute-start | bytes 393224 | tf_op jit(solution)/shard_map/ppermute | solution.py:244
  42.1 6.7 %collective-permute-start.12 = (f32[2,16,8,128]{3,2,1,0:T(8,128)S(1)}, f32[2,16,8,128]{3,2,1,0:T(8,128)S(1)}, u32[]{:S(2)}, u32[]{:S(2)}) collective-permute-start(f32[2,16,8,128]{3,2,1,0:T(8,128)S(1)} %get-tuple-element.40), channel_id=1, source_target_pairs={{0,3},{1,2},{2,1},{3,0},{4,7},{5,6},{6,5},{7,4},{8,11},{9,10},{10,... | collective-permute-start | bytes 393224 | tf_op jit(solution)/shard_map/ppermute | solution.py:244
  42.5 6.4 %collective-permute-start.13 = (f32[2,16,8,128]{3,2,1,0:T(8,128)S(1)}, f32[2,16,8,128]{3,2,1,0:T(8,128)S(1)}, u32[]{:S(2)}, u32[]{:S(2)}) collective-permute-start(f32[2,16,8,128]{3,2,1,0:T(8,128)S(1)} %get-tuple-element.41), channel_id=1, source_target_pairs={{0,4},{1,5},{2,6},{3,7},{4,0},{5,1},{6,2},{7,3},{8,12},{9,13},{10,... | collective-permute-start | bytes 393224 | tf_op jit(solution)/shard_map/ppermute | solution.py:244
  44.0 12.1 %collective-permute-start.14 = (f32[2,16,8,128]{3,2,1,0:T(8,128)S(1)}, f32[2,16,8,128]{3,2,1,0:T(8,128)S(1)}, u32[]{:S(2)}, u32[]{:S(2)}) collective-permute-start(f32[2,16,8,128]{3,2,1,0:T(8,128)S(1)} %get-tuple-element.42), channel_id=1, source_target_pairs={{0,5},{1,4},{2,7},{3,6},{4,1},{5,0},{6,3},{7,2},{8,13},{9,12},{10,... | collective-permute-start | bytes 393224 | tf_op jit(solution)/shard_map/ppermute | solution.py:244
  44.2 11.9 %collective-permute-start.15 = (f32[2,16,8,128]{3,2,1,0:T(8,128)S(1)}, f32[2,16,8,128]{3,2,1,0:T(8,128)S(1)}, u32[]{:S(2)}, u32[]{:S(2)}) collective-permute-start(f32[2,16,8,128]{3,2,1,0:T(8,128)S(1)} %get-tuple-element.43), channel_id=1, source_target_pairs={{0,6},{1,7},{2,4},{3,5},{4,2},{5,3},{6,0},{7,1},{8,14},{9,15},{10,... | collective-permute-start | bytes 393224 | tf_op jit(solution)/shard_map/ppermute | solution.py:244
  47.0 9.1 %collective-permute-start.16 = (f32[2,16,8,128]{3,2,1,0:T(8,128)S(1)}, f32[2,16,8,128]{3,2,1,0:T(8,128)S(1)}, u32[]{:S(2)}, u32[]{:S(2)}) collective-permute-start(f32[2,16,8,128]{3,2,1,0:T(8,128)S(1)} %get-tuple-element.44), channel_id=1, source_target_pairs={{0,7},{1,6},{2,5},{3,4},{4,3},{5,2},{6,1},{7,0},{8,15},{9,14},{10,... | collective-permute-start | bytes 393224 | tf_op jit(solution)/shard_map/ppermute | solution.py:244
  (5 other events, 4.6 us)

commit v2 on v1

v2 whole, which is shorter than its diff:
```python
import math

import numpy as np
import jax
import jax.numpy as jnp
from jax import lax
from jax.experimental import pallas as pl
from jax.experimental.pallas import tpu as pltpu
from jax.sharding import PartitionSpec as P

heat_loss = 4.0
spread_solute = 2.0
spread_heat = 100.0
SUB = 8
LANES = 128
VMEM_LIMIT = 48 * 1024 * 1024


def split_tables(n):
    half = n // 2
    y = np.arange(half)
    cols, freq = [], []
    for j in range(half // 2 + 1):
        k = 2 * j
        scale = math.sqrt((1.0 if k in (0, half) else 2.0) / n)
        cols.append(scale * np.cos(2 * np.pi * k * y / n))
        freq.append(k)
        if 0 < j < half // 2:
            cols.append(scale * np.sin(2 * np.pi * k * y / n))
            freq.append(k)
    even = np.stack(cols, 1)
    cols, odd_freq = [], []
    for j in range(half // 2):
        k = 2 * j + 1
        scale = math.sqrt(2.0 / n)
        cols.append(scale * np.cos(2 * np.pi * k * y / n))
        cols.append(scale * np.sin(2 * np.pi * k * y / n))
        odd_freq += [k, k]
    odd = np.stack(cols, 1)
    eig = 4.0 * np.sin(np.pi * np.array(freq + odd_freq) / n) ** 2
    return even, odd, eig.astype(np.float32)


def hi_lo(a):
    hi = jnp.asarray(a, jnp.float32).astype(jnp.bfloat16)
    lo = (jnp.asarray(a, jnp.float32) - hi.astype(jnp.float32)).astype(jnp.bfloat16)
    return hi, lo


def table_pair(a):
    bf16 = jnp.bfloat16
    hi = a.astype(np.float32).astype(bf16)
    lo = (a - hi.astype(np.float64)).astype(np.float32).astype(bf16)
    return hi, lo


def dot3(x, q_hi, q_lo, dims):
    hi, lo = hi_lo(x)
    dn = (dims, ((), ()))
    f32 = jnp.float32
    return (
        lax.dot_general(hi, q_hi, dn, preferred_element_type=f32)
        + lax.dot_general(hi, q_lo, dn, preferred_element_type=f32)
        + lax.dot_general(lo, q_hi, dn, preferred_element_type=f32)
    )


def cosine_forward(v):
    n = len(v)
    if n == 1:
        return [v[0]]
    h = n // 2
    sums = [v[z] + v[n - 1 - z] for z in range(h)]
    diffs = [v[z] - v[n - 1 - z] for z in range(h)]
    even = cosine_forward(sums)
    out = [None] * n
    for j in range(h):
        out[2 * j] = even[j]
        k = 2 * j + 1
        acc = None
        for z in range(h):
            term = diffs[z] * float(math.cos(math.pi * k * (z + 0.5) / n))
            acc = term if acc is None else acc + term
        out[k] = acc
    return out


def cosine_backward(c):
    n = len(c)
    if n == 1:
        return [c[0]]
    h = n // 2
    even = cosine_backward([c[2 * j] for j in range(h)])
    out = [None] * n
    for z in range(h):
        acc = None
        for j in range(h):
            k = 2 * j + 1
            term = c[k] * float(math.cos(math.pi * k * (z + 0.5) / n))
            acc = term if acc is None else acc + term
        out[z] = even[z] + acc
        out[n - 1 - z] = even[z] - acc
    return out


def line_factors(eig_rows, spread, layer_eig):
    rest = 1.0 + spread * (eig_rows + layer_eig)
    root = jnp.sqrt(rest * (rest + 4.0 * spread))
    decay = 2.0 * spread / (rest + 2.0 * spread + root)
    return decay, root


def power(base, exponent):
    out = None
    square = base
    while exponent:
        if exponent & 1:
            out = square if out is None else out * square
        exponent >>= 1
        if exponent:
            square = square * square
    return out


def sublane_powers(step_decay, row, reverse):
    out = jnp.ones_like(step_decay)
    factor = step_decay
    place = (SUB - 1 - row) if reverse else row
    for bit in range(3):
        out = jnp.where((place >> bit) & 1 == 1, out * factor, out)
        factor = factor * factor
    return out


def on_device_fn(fields, grain_ids, grain_rates, die_mask):
    depth = fields.shape[1]
    local_x = fields.shape[2]
    span_y = fields.shape[3]
    half = span_y // 2
    devices_x = lax.axis_size("gx")
    devices_z = lax.axis_size("gz")
    layers = depth * devices_z
    chunks = devices_z // 2
    lanes = span_y // chunks
    steps = local_x // SUB
    tiles = span_y // LANES
    grain_count = grain_rates.shape[0]
    even, odd, eig = split_tables(span_y)
    even_hi, even_lo = table_pair(even)
    odd_hi, odd_lo = table_pair(odd)
    tables = [jnp.asarray(t) for t in (even_hi, even_lo, odd_hi, odd_lo)]
    back_tables = [jnp.asarray(np.ascontiguousarray(t.T)) for t in (even_hi, even_lo, odd_hi, odd_lo)]
    eig_table = jnp.asarray(eig.reshape(chunks, lanes))
    f32 = jnp.float32
    params = pltpu.CompilerParams(vmem_limit_bytes=VMEM_LIMIT)
    piece = (depth, steps, SUB, lanes)
    grain_run = min(steps, 8)
    mask_run = min(steps, 16)

    vmem = pl.BlockSpec(memory_space=pltpu.VMEM)
    hbm = pl.BlockSpec(memory_space=pltpu.HBM)
    shared = 2 if depth % 2 == 0 else 1

    def source_kernel(rates_hbm, f_hbm, id_hbm, mask_hbm, eh_hbm, el_hbm, oh_hbm, ol_hbm, *rest):
        outs = rest[:devices_z]
        f_buf, id_buf, mask_buf, sums, diffs, modes, eh, el, oh, ol, rates = rest[devices_z:-3]
        f_sems, tile_sems, table_sems = rest[-3:]
        g = lax.axis_index("gz")
        field_copies = [
            pltpu.make_async_copy(
                f_hbm.at[:, layer, :, pl.ds(t * LANES, LANES)],
                f_buf.at[layer, t],
                f_sems.at[layer, t],
            )
            for layer in range(depth)
            for t in range(tiles)
        ]
        tile_copies = []
        for t in range(tiles):
            cols = pl.ds(t * LANES, LANES)
            for group in range(depth // shared):
                tile_copies.append(
                    pltpu.make_async_copy(
                        id_hbm.at[group * shared, :, cols],
                        id_buf.at[group, t],
                        tile_sems.at[0, group, t],
                    )
                )
            tile_copies.append(
                pltpu.make_async_copy(mask_hbm.at[:, cols], mask_buf.at[t], tile_sems.at[1, 0, t])
            )
        table_copies = [
            pltpu.make_async_copy(src, dst, table_sems.at[i])
            for i, (src, dst) in enumerate(
                ((eh_hbm, eh), (el_hbm, el), (oh_hbm, oh), (ol_hbm, ol))
            )
        ]
        tile_copies.append(pltpu.make_async_copy(rates_hbm, rates, table_sems.at[4]))
        for copy in tile_copies + field_copies + table_copies:
            copy.start()
        for copy in tile_copies:
            copy.wait()
        for layer in range(depth):
            first = jnp.where(g * depth + layer == 0, heat_loss, 0.0)
            for copy in field_copies[layer * tiles : (layer + 1) * tiles]:
                copy.wait()
            for tile in range(tiles // 2):
                pair = (tile, tile + tiles // 2)
                rates_c, rates_h, sinks = [None] * 2, [None] * 2, [None] * 2
                for xi in range(steps):
                    at = pl.ds(xi, SUB, stride=steps)
                    rhs = [[None] * 2, [None] * 2]
                    for side in range(2):
                        t = pair[side]
                        if xi % grain_run == 0:
                            ids = id_buf[layer // shared, t, at, :]
                            rate_c = jnp.zeros(ids.shape, f32)
                            rate_h = jnp.zeros(ids.shape, f32)
                            for grain in range(grain_count):
                                hit = ids == grain
                                rate_c = jnp.where(hit, rates[0, grain], rate_c)
                                rate_h = jnp.where(hit, rates[1, grain], rate_h)
                            rates_c[side], rates_h[side] = rate_c, rate_h
                        if xi % mask_run == 0:
                            sinks[side] = mask_buf[t, at, :].astype(f32) * first
                        c = f_buf[layer, t, 0, at, :]
                        h = f_buf[layer, t, 1, at, :]
                        square = c * c
                        rhs[0][side] = c + rates_c[side] * jnp.tanh(h - c)
                        rhs[1][side] = (
                            h + rates_h[side] * square / (1.0 + square) - sinks[side] * (h + 1.0)
                        )
                    for f in range(2):
                        rows = pl.ds((f * steps + xi) * SUB, SUB)
                        cols = pl.ds(tile * LANES, LANES)
                        sums[layer, rows, cols] = rhs[f][0] + rhs[f][1]
                        diffs[layer, rows, cols] = rhs[f][0] - rhs[f][1]
            if layer == 0:
                for copy in table_copies:
                    copy.wait()
            for parity, (src, hi, lo) in enumerate(((sums, eh, el), (diffs, oh, ol))):
                both = dot3(src[layer], hi[...], lo[...], ((1,), (0,)))
                for f in range(2):
                    for chunk in range(chunks // 2):
                        part = both[
                            f * local_x : (f + 1) * local_x, chunk * lanes : (chunk + 1) * lanes
                        ]
                        place = 2 * (chunk + parity * (chunks // 2)) + f
                        modes[place, layer] = part.reshape(steps, SUB, lanes)
        for k in range(devices_z):
            outs[k][...] = modes[g ^ k]

    square = (half, half)
    pieces = pl.pallas_call(
        source_kernel,
        in_specs=[hbm] * 8,
        out_specs=[vmem] * devices_z,
        out_shape=[jax.ShapeDtypeStruct(piece, f32)] * devices_z,
        scratch_shapes=[
            pltpu.VMEM((depth, tiles, 2, local_x, LANES), f32),
            pltpu.VMEM((depth // shared, tiles, local_x, LANES), jnp.int32),
            pltpu.VMEM((tiles, local_x, LANES), jnp.int32),
            pltpu.VMEM((depth, 2 * local_x, half), f32),
            pltpu.VMEM((depth, 2 * local_x, half), f32),
            pltpu.VMEM((devices_z,) + piece, f32),
        ]
        + [pltpu.VMEM(square, jnp.bfloat16)] * 4
        + [
            pltpu.SMEM((2, grain_count), f32),
            pltpu.SemaphoreType.DMA((depth, tiles)),
            pltpu.SemaphoreType.DMA((2, depth // shared, tiles)),
            pltpu.SemaphoreType.DMA((5,)),
        ],
        compiler_params=params,
        name="sources",
    )(
        *(
            pltpu.with_memory_space_constraint(a, pltpu.HBM)
            for a in (grain_rates.T, fields, grain_ids, die_mask, *tables)
        ),
    )

    def exchange(arrays, axis, order):
        count = lax.axis_size(axis)
        out = []
        for k in order:
            route = [(i, i ^ k) for i in range(count)]
            out.append(lax.ppermute(arrays[k], axis, route) if k else arrays[k])
        return out

    order_z = [0] + sorted(range(1, devices_z), key=lambda k: (k & 1, -k))
    order_x = list(range(devices_x))

    gathered = exchange(pieces, "gz", order_z)

    def line_setup(eig_ref):
        g = lax.axis_index("gz")
        spread = jnp.where(g % 2 == 0, spread_solute, spread_heat).astype(f32)
        eig_rows = jnp.broadcast_to(eig_ref[pl.ds(g // 2, 1), :], (SUB, lanes))
        return g, spread, eig_rows

    layer_eig = [4.0 * math.sin(math.pi * k / (2 * layers)) ** 2 for k in range(layers)]

    def gather_kernel(eig_ref, *rest):
        ins = rest[: devices_z]
        hat_ref, from_left, from_right, ends, field = rest[devices_z:]
        g, spread, eig_rows = line_setup(eig_ref)
        for i, k in enumerate(order_z):
            field[pl.ds((g ^ k) * depth, depth)] = ins[i][...]

        def transform(xi, carry):
            hat = cosine_forward([field[z, xi] for z in range(layers)])
            for k in range(layers):
                hat_ref[k, xi] = hat[k]
            return carry

        lax.fori_loop(0, steps, transform, 0)
        row = lax.broadcasted_iota(jnp.int32, (SUB, lanes), 0)
        for k in range(layers):
            decay, _ = line_factors(eig_rows, spread, layer_eig[k])
            left = hat_ref[k, 0]
            right = hat_ref[k, steps - 1]
            for xi in range(1, steps):
                left = hat_ref[k, xi] + decay * left
                right = hat_ref[k, steps - 1 - xi] + decay * right
            step_decay = power(decay, steps)
            up = sublane_powers(step_decay, row, False)
            down = sublane_powers(step_decay, row, True)
            ends[0, pl.ds(k, 1), :] = jnp.sum(left * down, axis=0, keepdims=True)
            ends[1, pl.ds(k, 1), :] = jnp.sum(right * up, axis=0, keepdims=True)
            left = jnp.where(row >= 1, pltpu.roll(left, 1, 0), 0.0)
            right = jnp.where(row < SUB - 1, pltpu.roll(right, SUB - 1, 0), 0.0)
            factor = step_decay
            for shift in (1, 2, 4):
                left = left + factor * jnp.where(row >= shift, pltpu.roll(left, shift, 0), 0.0)
                right = right + factor * jnp.where(
                    row < SUB - shift, pltpu.roll(right, SUB - shift, 0), 0.0
                )
                factor = factor * factor
            from_left[k] = left
            from_right[k] = right

    hat, from_left, from_right, ends = pl.pallas_call(
        gather_kernel,
        in_specs=[vmem] * (1 + devices_z),
        out_specs=[vmem] * 4,
        out_shape=[
            jax.ShapeDtypeStruct((layers, steps, SUB, lanes), f32),
            jax.ShapeDtypeStruct((layers, SUB, lanes), f32),
            jax.ShapeDtypeStruct((layers, SUB, lanes), f32),
            jax.ShapeDtypeStruct((2, layers, lanes), f32),
        ],
        scratch_shapes=[
            pltpu.VMEM((layers, steps, SUB, lanes), f32),
        ],
        compiler_params=params,
        name="gather",
    )(eig_table, *gathered)

    all_ends = exchange([ends] * devices_x, "gx", order_x)

    def solve_kernel(eig_ref, hat_ref, left_ref, right_ref, *rest):
        end_refs = rest[: devices_x]
        outs = rest[devices_x : devices_x + devices_z]
        near, work, entry = rest[devices_x + devices_z :]
        g, spread, eig_rows = line_setup(eig_ref)
        place = lax.axis_index("gx")
        for i, k in enumerate(order_x):
            near[place ^ k] = end_refs[i][...]
        row = lax.broadcasted_iota(jnp.int32, (SUB, lanes), 0)
        eig_one = eig_ref[pl.ds(g // 2, 1), :]
        kz = lax.broadcasted_iota(jnp.int32, (layers, lanes), 0).astype(f32)
        eig_z = 4.0 * jnp.sin(kz * (math.pi / (2 * layers))) ** 2
        decay_all, _ = line_factors(eig_one, spread, eig_z)
        block_decay = power(decay_all, local_x)
        total_left = near[(place + devices_x - 1) % devices_x, 0]
        total_right = near[(place + 1) % devices_x, 1]
        weight = block_decay
        for m in range(2, devices_x + 1):
            total_left = total_left + weight * near[(place + devices_x - m) % devices_x, 0]
            total_right = total_right + weight * near[(place + m) % devices_x, 1]
            weight = weight * block_decay
        entry[0] = total_left / (1.0 - weight)
        entry[1] = total_right / (1.0 - weight)
        for k in range(layers):
            decay, root = line_factors(eig_rows, spread, layer_eig[k])
            gain = ((1.0 if k == 0 else 2.0) / layers) / root
            step_decay = power(decay, steps)
            up = sublane_powers(step_decay, row, False)
            down = sublane_powers(step_decay, row, True)
            left = left_ref[k] + up * entry[0, pl.ds(k, 1), :]
            right = right_ref[k] + down * entry[1, pl.ds(k, 1), :]
            for xi in range(steps):
                left = hat_ref[k, xi] + decay * left
                work[k, xi] = left
            for xi in reversed(range(steps)):
                carried = decay * right
                work[k, xi] = gain * (work[k, xi] + carried)
                right = hat_ref[k, xi] + carried

        def back(xi, carry):
            values = cosine_backward([work[k, xi] for k in range(layers)])
            for z in range(layers):
                work[z, xi] = values[z]
            return carry

        lax.fori_loop(0, steps, back, 0)
        for k in range(devices_z):
            outs[k][...] = work[pl.ds((g ^ k) * depth, depth)]

    solved = pl.pallas_call(
        solve_kernel,
        in_specs=[vmem] * (4 + devices_x),
        out_specs=[vmem] * devices_z,
        out_shape=[jax.ShapeDtypeStruct(piece, f32)] * devices_z,
        scratch_shapes=[
            pltpu.VMEM((devices_x, 2, layers, lanes), f32),
            pltpu.VMEM((layers, steps, SUB, lanes), f32),
            pltpu.VMEM((2, layers, lanes), f32),
        ],
        compiler_params=params,
        name="solve",
    )(eig_table, hat, from_left, from_right, *all_ends)

    returned = exchange(solved, "gz", order_z)

    def final_kernel(eh, el, oh, ol, *rest):
        ins = rest[:devices_z]
        out_ref, modes, buf, out_sems = rest[devices_z:]
        g = lax.axis_index("gz")
        for i, k in enumerate(order_z):
            modes[g ^ k] = ins[i][...]
        copies = []
        dims = ((1,), (0,))
        for f in range(2):
            parts = [
                modes[2 * chunk + f].reshape(depth * local_x, lanes) for chunk in range(chunks)
            ]
            low = dot3(jnp.concatenate(parts[: chunks // 2], axis=1), eh[...], el[...], dims)
            high = dot3(jnp.concatenate(parts[chunks // 2 :], axis=1), oh[...], ol[...], dims)
            for side, value in enumerate((low + high, low - high)):
                for layer in range(depth):
                    for col in range(tiles // 2):
                        t = side * (tiles // 2) + col
                        for xi in range(steps):
                            at = (layer * steps + xi) * SUB
                            buf[f, layer, t, pl.ds(xi, SUB, stride=steps), :] = value[
                                at : at + SUB, col * LANES : (col + 1) * LANES
                            ]
                        copies.append(
                            pltpu.make_async_copy(
                                buf.at[f, layer, t],
                                out_ref.at[f, layer, :, pl.ds(t * LANES, LANES)],
                                out_sems.at[f, layer, t],
                            )
                        )
                        copies[-1].start()
        for copy in copies:
            copy.wait()

    return pl.pallas_call(
        final_kernel,
        in_specs=[vmem] * (4 + devices_z),
        out_specs=hbm,
        out_shape=jax.ShapeDtypeStruct((2, depth, local_x, span_y), f32),
        scratch_shapes=[
            pltpu.VMEM((devices_z,) + piece, f32),
            pltpu.VMEM((2, depth, tiles, local_x, LANES), f32),
            pltpu.SemaphoreType.DMA((2, depth, tiles)),
        ],
        compiler_params=params,
        name="finish",
    )(*back_tables, *returned)


def solution(mesh):
    placed = (P(None, "gz", "gx", None), P("gz", "gx", None), P(), P("gx", None))
    return jax.shard_map(
        on_device_fn, mesh=mesh, in_specs=placed, out_specs=P(None, "gz", "gx", None), check_vma=False
    )
```

time: 60.7 us -> 44.4 us (0.73)
  local copies, waits for them, and re-layouts: 7.61 us -> 0.02 us
  Pallas kernels: 11.8 us -> 6.69 us
  starting transfers between devices: 21.2 us -> 18.4 us
  waiting for transfers between devices: 19.7 us -> 19 us
    unnamed x25 -> x10, local copies, waits for them, and re-layouts: 7.61 us -> 0.02 us
    pallas_call x4, Pallas kernels: 11.8 us -> 6.69 us  [the longest x1 3 us: on_device_fn(): pl.pallas_call(source_kernel, in_specs=[hbm] * 8, out_specs=[vmem] * devi...]
    ppermute x17, starting transfers between devices: 21.2 us -> 18.4 us  [exchange(): out.append(lax.ppermute(arrays[k], axis, route) if k else arrays[k])]
    ppermute x17, waiting for transfers between devices: 19.7 us -> 19 us  [exchange(): out.append(lax.ppermute(arrays[k], axis, route) if k else arrays[k])]
  transfers between devices with their start and end apart: 17 -> 17, of which waited for: 7 -> 9; matrix products, arithmetic and copies ran while one was open for 0% -> 0% of each run, Pallas kernels for 0% -> 0%
where the time goes in v2:
time: 44.4 us; the launch traced here: 44.2 us
  waiting for transfers between devices  19 us (43%)
  starting transfers between devices  18.4 us (41%)
  Pallas kernels  6.69 us (15%)
    ppermute x17, waiting for transfers between devices, exchange(): out.append(lax.ppermute(arrays[k], axis, route) if k else arrays[k])  19 us
    ppermute x17, starting transfers between devices, exchange(): out.append(lax.ppermute(arrays[k], axis, route) if k else arrays[k])  18.4 us
    pallas_call x1, Pallas kernels, on_device_fn(): pl.pallas_call(source_kernel, in_specs=[hbm] * 8, out_specs=[vmem] * devi...  3 us
    pallas_call x1, Pallas kernels, on_device_fn(): pl.pallas_call(final_kernel, in_specs=[vmem] * (4 + devices_z), out_specs...  1.64 us
    pallas_call x1, Pallas kernels, on_device_fn(): pl.pallas_call(solve_kernel, in_specs=[vmem] * (4 + devices_x), out_specs...  1.03 us
    pallas_call x1, Pallas kernels, on_device_fn(): pl.pallas_call(gather_kernel, in_specs=[vmem] * (1 + devices_z), out_spec...  1.02 us
  transfers between devices with their start and end apart: 17, of which 9 were waited for; matrix products, arithmetic and copies ran while one was open for 0% of the time, Pallas kernels for 0%

profile of v2, /device:TPU:0, one launch (start us, length us, event | category | flops | bytes accessed | tf_op | source)
XLA Modules:
  0.0 44.2 jit_solution(11385754241691977450)
XLA Ops:
  0.0 3.0 %sources.1 = (f32[2,16,8,128]{3,2,1,0:T(8,128)S(1)}, f32[2,16,8,128]{3,2,1,0:T(8,128)S(1)}, f32[2,16,8,128]{3,2,1,0:T(8,128)S(1)}, f32[2,16,8,128]{3,2,1,0:T(8,1...) custom-call(f32[2,32]{1,0:T(2,128)} %bitcast.1, ...), custom_call_target="tpu_custom_call" | custom-call | tf_op jit(solution)/shard_map/sources/pallas_call | solution.py:254
  3.0 4.0 %collective-permute-start = (f32[2,16,8,128]{3,2,1,0:T(8,128)S(1)}, f32[2,16,8,128]{3,2,1,0:T(8,128)S(1)}, u32[]{:S(2)}, u32[]{:S(2)}) collective-permute-start(f32[2,16,8,128]{3,2,1,0:T(8,128)S(1)} %get-tuple-element.26), channel_id=1, source_target_pairs={{0,6},{1,7},{2,4},{3,5},{4,2},{5,3},{6,0},{7,1},{8,14},{9,15},{10,... | collective-permute-start | bytes 393224 | tf_op jit(solution)/shard_map/ppermute | solution.py:288
  7.0 0.5 %collective-permute-start.1 = (f32[2,16,8,128]{3,2,1,0:T(8,128)S(1)}, f32[2,16,8,128]{3,2,1,0:T(8,128)S(1)}, u32[]{:S(2)}, u32[]{:S(2)}) collective-permute-start(f32[2,16,8,128]{3,2,1,0:T(8,128)S(1)} %get-tuple-element.27), channel_id=1, source_target_pairs={{0,4},{1,5},{2,6},{3,7},{4,0},{5,1},{6,2},{7,3},{8,12},{9,13},{10,... | collective-permute-start | bytes 393224 | tf_op jit(solution)/shard_map/ppermute | solution.py:288
  7.5 0.1 collective-permute-start.2
  7.6 1.4 %collective-permute-start.3 = (f32[2,16,8,128]{3,2,1,0:T(8,128)S(1)}, f32[2,16,8,128]{3,2,1,0:T(8,128)S(1)}, u32[]{:S(2)}, u32[]{:S(2)}) collective-permute-start(f32[2,16,8,128]{3,2,1,0:T(8,128)S(1)} %get-tuple-element.29), channel_id=1, source_target_pairs={{0,7},{1,6},{2,5},{3,4},{4,3},{5,2},{6,1},{7,0},{8,15},{9,14},{10,... | collective-permute-start | bytes 393224 | tf_op jit(solution)/shard_map/ppermute | solution.py:288
  9.1 1.6 %collective-permute-start.4 = (f32[2,16,8,128]{3,2,1,0:T(8,128)S(1)}, f32[2,16,8,128]{3,2,1,0:T(8,128)S(1)}, u32[]{:S(2)}, u32[]{:S(2)}) collective-permute-start(f32[2,16,8,128]{3,2,1,0:T(8,128)S(1)} %get-tuple-element.30), channel_id=1, source_target_pairs={{0,5},{1,4},{2,7},{3,6},{4,1},{5,0},{6,3},{7,2},{8,13},{9,12},{10,... | collective-permute-start | bytes 393224 | tf_op jit(solution)/shard_map/ppermute | solution.py:288
  10.7 0.2 collective-permute-done.rest_1_
  10.9 5.1 %collective-permute-done.1.rest_2_ = f32[2,16,8,128]{3,2,1,0:T(8,128)S(1)} collective-permute-done((f32[2,16,8,128]{3,2,1,0:T(8,128)S(1)}, f32[2,16,8,128]{3,2,1,0:T(8,128)S(1)}, u32[]{:S(2)}, u32[]{:S(2)}) %collective-permute-start.1) | collective-permute-done | bytes 131104 | tf_op jit(solution)/shard_map/ppermute | solution.py:288
  16.0 0.5 %collective-permute-done.3.rest_4_ = f32[2,16,8,128]{3,2,1,0:T(8,128)S(1)} collective-permute-done((f32[2,16,8,128]{3,2,1,0:T(8,128)S(1)}, f32[2,16,8,128]{3,2,1,0:T(8,128)S(1)}, u32[]{:S(2)}, u32[]{:S(2)}) %collective-permute-start.3) | collective-permute-done | bytes 131104 | tf_op jit(solution)/shard_map/ppermute | solution.py:288
  16.5 2.3 %collective-permute-done.4.rest_5_ = f32[2,16,8,128]{3,2,1,0:T(8,128)S(1)} collective-permute-done((f32[2,16,8,128]{3,2,1,0:T(8,128)S(1)}, f32[2,16,8,128]{3,2,1,0:T(8,128)S(1)}, u32[]{:S(2)}, u32[]{:S(2)}) %collective-permute-start.4) | collective-permute-done | bytes 131104 | tf_op jit(solution)/shard_map/ppermute | solution.py:288
  18.8 1.0 %gather.1 = (f32[16,16,8,128]{3,2,1,0:T(8,128)S(1)}, f32[16,8,128]{2,1,0:T(8,128)S(1)}, f32[16,8,128]{2,1,0:T(8,128)S(1)}, f32[2,16,128]{2,1,0:T(8,128)S(1)}) custom-call(f32[4,128]{1,0:T(4,128)S(1)} %copy-done.4, f32[2,16,8,128]{3,2,1,0:T(8,128)S(1)} %get-tuple-element.25.rest_0_, f32[2,16,8,128]{3,2,1,0:T(8,128)S(1)} %collective-permute-done.rest_1_, ...), custom_call_target="tpu_custom_call" | custom-call | tf_op jit(solution)/shard_map/gather/pallas_call | solution.py:343
  19.8 3.9 %collective-permute-start.9 = (f32[2,16,128]{2,1,0:T(8,128)S(1)}, f32[2,16,128]{2,1,0:T(8,128)S(1)}, u32[]{:S(2)}, u32[]{:S(2)}) collective-permute-start(f32[2,16,128]{2,1,0:T(8,128)S(1)} %get-tuple-element.36.rest_0_), channel_id=1, source_target_pairs={{0,24},{8,16},{16,8},{24,0},{1,25},{9,17},{17,9},{25,1},{2,26},{10... | collective-permute-start | bytes 49160 | tf_op jit(solution)/shard_map/ppermute | solution.py:288
  23.7 0.6 %collective-permute-start.7 = (f32[2,16,128]{2,1,0:T(8,128)S(1)}, f32[2,16,128]{2,1,0:T(8,128)S(1)}, u32[]{:S(2)}, u32[]{:S(2)}) collective-permute-start(f32[2,16,128]{2,1,0:T(8,128)S(1)} %get-tuple-element.36.rest_0_), channel_id=1, source_target_pairs={{0,8},{8,0},{16,24},{24,16},{1,9},{9,1},{17,25},{25,17},{2,10},{10... | collective-permute-start | bytes 49160 | tf_op jit(solution)/shard_map/ppermute | solution.py:288
  24.3 1.1 %collective-permute-done.9.rest_3_ = f32[2,16,128]{2,1,0:T(8,128)S(1)} collective-permute-done((f32[2,16,128]{2,1,0:T(8,128)S(1)}, f32[2,16,128]{2,1,0:T(8,128)S(1)}, u32[]{:S(2)}, u32[]{:S(2)}) %collective-permute-start.9) | collective-permute-done | bytes 16416 | tf_op jit(solution)/shard_map/ppermute | solution.py:288
  25.4 2.9 %collective-permute-done.8.rest_2_ = f32[2,16,128]{2,1,0:T(8,128)S(1)} collective-permute-done((f32[2,16,128]{2,1,0:T(8,128)S(1)}, f32[2,16,128]{2,1,0:T(8,128)S(1)}, u32[]{:S(2)}, u32[]{:S(2)}) %collective-permute-start.8) | collective-permute-done | bytes 16416 | tf_op jit(solution)/shard_map/ppermute | solution.py:288
  28.4 1.0 %solve.1 = (f32[2,16,8,128]{3,2,1,0:T(8,128)S(1)}, f32[2,16,8,128]{3,2,1,0:T(8,128)S(1)}, f32[2,16,8,128]{3,2,1,0:T(8,128)S(1)}, f32[2,16,8,128]{3,2,1,0:T(8,128...) custom-call(f32[4,128]{1,0:T(4,128)S(1)} %copy-done.4, ...), custom_call_target="tpu_custom_call" | custom-call | tf_op jit(solution)/shard_map/solve/pallas_call | solution.py:411
  29.4 1.2 %collective-permute-start.10 = (f32[2,16,8,128]{3,2,1,0:T(8,128)S(1)}, f32[2,16,8,128]{3,2,1,0:T(8,128)S(1)}, u32[]{:S(2)}, u32[]{:S(2)}) collective-permute-start(f32[2,16,8,128]{3,2,1,0:T(8,128)S(1)} %get-tuple-element.38), channel_id=1, source_target_pairs={{0,6},{1,7},{2,4},{3,5},{4,2},{5,3},{6,0},{7,1},{8,14},{9,15},{10,... | collective-permute-start | bytes 393224 | tf_op jit(solution)/shard_map/ppermute | solution.py:288
  30.6 1.8 %collective-permute-start.11 = (f32[2,16,8,128]{3,2,1,0:T(8,128)S(1)}, f32[2,16,8,128]{3,2,1,0:T(8,128)S(1)}, u32[]{:S(2)}, u32[]{:S(2)}) collective-permute-start(f32[2,16,8,128]{3,2,1,0:T(8,128)S(1)} %get-tuple-element.39), channel_id=1, source_target_pairs={{0,4},{1,5},{2,6},{3,7},{4,0},{5,1},{6,2},{7,3},{8,12},{9,13},{10,... | collective-permute-start | bytes 393224 | tf_op jit(solution)/shard_map/ppermute | solution.py:288
  32.4 0.5 %collective-permute-start.12 = (f32[2,16,8,128]{3,2,1,0:T(8,128)S(1)}, f32[2,16,8,128]{3,2,1,0:T(8,128)S(1)}, u32[]{:S(2)}, u32[]{:S(2)}) collective-permute-start(f32[2,16,8,128]{3,2,1,0:T(8,128)S(1)} %get-tuple-element.40), channel_id=1, source_target_pairs={{0,2},{1,3},{2,0},{3,1},{4,6},{5,7},{6,4},{7,5},{8,10},{9,11},{10,... | collective-permute-start | bytes 393224 | tf_op jit(solution)/shard_map/ppermute | solution.py:288
  33.0 2.7 %collective-permute-start.14 = (f32[2,16,8,128]{3,2,1,0:T(8,128)S(1)}, f32[2,16,8,128]{3,2,1,0:T(8,128)S(1)}, u32[]{:S(2)}, u32[]{:S(2)}) collective-permute-start(f32[2,16,8,128]{3,2,1,0:T(8,128)S(1)} %get-tuple-element.42), channel_id=1, source_target_pairs={{0,5},{1,4},{2,7},{3,6},{4,1},{5,0},{6,3},{7,2},{8,13},{9,12},{10,... | collective-permute-start | bytes 393224 | tf_op jit(solution)/shard_map/ppermute | solution.py:288
  35.6 0.4 %collective-permute-done.10.rest_1_ = f32[2,16,8,128]{3,2,1,0:T(8,128)S(1)} collective-permute-done((f32[2,16,8,128]{3,2,1,0:T(8,128)S(1)}, f32[2,16,8,128]{3,2,1,0:T(8,128)S(1)}, u32[]{:S(2)}, u32[]{:S(2)}) %collective-permute-start.10) | collective-permute-done | bytes 131104 | tf_op jit(solution)/shard_map/ppermute | solution.py:288
  36.1 4.2 %collective-permute-done.11.rest_2_ = f32[2,16,8,128]{3,2,1,0:T(8,128)S(1)} collective-permute-done((f32[2,16,8,128]{3,2,1,0:T(8,128)S(1)}, f32[2,16,8,128]{3,2,1,0:T(8,128)S(1)}, u32[]{:S(2)}, u32[]{:S(2)}) %collective-permute-start.11) | collective-permute-done | bytes 131104 | tf_op jit(solution)/shard_map/ppermute | solution.py:288
  40.3 2.3 %collective-permute-done.14.rest_5_ = f32[2,16,8,128]{3,2,1,0:T(8,128)S(1)} collective-permute-done((f32[2,16,8,128]{3,2,1,0:T(8,128)S(1)}, f32[2,16,8,128]{3,2,1,0:T(8,128)S(1)}, u32[]{:S(2)}, u32[]{:S(2)}) %collective-permute-start.14) | collective-permute-done | bytes 131104 | tf_op jit(solution)/shard_map/ppermute | solution.py:288
  42.6 1.6 %finish.1 = f32[2,2,128,512]{3,2,1,0:T(8,128)} custom-call(bf16[256,256]{1,0:T(8,128)(2,1)S(1)} %copy-done.3, bf16[256,256]{1,0:T(8,128)(2,1)S(1)} %copy-done.2, bf16[256,256]{1,0:T(8,128)(2,1)S(1)} %copy-done.1, bf16[256,256]{1,0:T(8,128)(2,1)S(1)} %copy-done, f32[2,16,8,128]{3,2,1,0:T(8,128)S(1)} %get-tuple-element.37.rest_0_, ...), custom_call_target="tpu_custom_call" | custom-call | tf_op jit(solution)/shard_map/finish/pallas_call | solution.py:461
  (24 shorter events, 0.1 us)
Async XLA Ops:
  3.0 7.9 %collective-permute-start = (f32[2,16,8,128]{3,2,1,0:T(8,128)S(1)}, f32[2,16,8,128]{3,2,1,0:T(8,128)S(1)}, u32[]{:S(2)}, u32[]{:S(2)}) collective-permute-start(f32[2,16,8,128]{3,2,1,0:T(8,128)S(1)} %get-tuple-element.26), channel_id=1, source_target_pairs={{0,6},{1,7},{2,4},{3,5},{4,2},{5,3},{6,0},{7,1},{8,14},{9,15},{10,... | collective-permute-start | bytes 393224 | tf_op jit(solution)/shard_map/ppermute | solution.py:288
  7.0 9.0 %collective-permute-start.1 = (f32[2,16,8,128]{3,2,1,0:T(8,128)S(1)}, f32[2,16,8,128]{3,2,1,0:T(8,128)S(1)}, u32[]{:S(2)}, u32[]{:S(2)}) collective-permute-start(f32[2,16,8,128]{3,2,1,0:T(8,128)S(1)} %get-tuple-element.27), channel_id=1, source_target_pairs={{0,4},{1,5},{2,6},{3,7},{4,0},{5,1},{6,2},{7,3},{8,12},{9,13},{10,... | collective-permute-start | bytes 393224 | tf_op jit(solution)/shard_map/ppermute | solution.py:288
  7.5 8.5 %collective-permute-start.2 = (f32[2,16,8,128]{3,2,1,0:T(8,128)S(1)}, f32[2,16,8,128]{3,2,1,0:T(8,128)S(1)}, u32[]{:S(2)}, u32[]{:S(2)}) collective-permute-start(f32[2,16,8,128]{3,2,1,0:T(8,128)S(1)} %get-tuple-element.28), channel_id=1, source_target_pairs={{0,2},{1,3},{2,0},{3,1},{4,6},{5,7},{6,4},{7,5},{8,10},{9,11},{10,... | collective-permute-start | bytes 393224 | tf_op jit(solution)/shard_map/ppermute | solution.py:288
  7.6 8.9 %collective-permute-start.3 = (f32[2,16,8,128]{3,2,1,0:T(8,128)S(1)}, f32[2,16,8,128]{3,2,1,0:T(8,128)S(1)}, u32[]{:S(2)}, u32[]{:S(2)}) collective-permute-start(f32[2,16,8,128]{3,2,1,0:T(8,128)S(1)} %get-tuple-element.29), channel_id=1, source_target_pairs={{0,7},{1,6},{2,5},{3,4},{4,3},{5,2},{6,1},{7,0},{8,15},{9,14},{10,... | collective-permute-start | bytes 393224 | tf_op jit(solution)/shard_map/ppermute | solution.py:288
  9.1 9.7 %collective-permute-start.4 = (f32[2,16,8,128]{3,2,1,0:T(8,128)S(1)}, f32[2,16,8,128]{3,2,1,0:T(8,128)S(1)}, u32[]{:S(2)}, u32[]{:S(2)}) collective-permute-start(f32[2,16,8,128]{3,2,1,0:T(8,128)S(1)} %get-tuple-element.30), channel_id=1, source_target_pairs={{0,5},{1,4},{2,7},{3,6},{4,1},{5,0},{6,3},{7,2},{8,13},{9,12},{10,... | collective-permute-start | bytes 393224 | tf_op jit(solution)/shard_map/ppermute | solution.py:288
  10.9 7.9 %copy-start.4 = (f32[4,128]{1,0:T(4,128)S(1)}, f32[4,128]{1,0:T(4,128)}, u32[]{:S(2)}) copy-start(f32[4,128]{1,0:T(4,128)} %constant.26.clone.eig_ref) | copy-start | bytes 6148
  10.9 7.9 %collective-permute-start.5 = (f32[2,16,8,128]{3,2,1,0:T(8,128)S(1)}, f32[2,16,8,128]{3,2,1,0:T(8,128)S(1)}, u32[]{:S(2)}, u32[]{:S(2)}) collective-permute-start(f32[2,16,8,128]{3,2,1,0:T(8,128)S(1)} %get-tuple-element.31), channel_id=1, source_target_pairs={{0,3},{1,2},{2,1},{3,0},{4,7},{5,6},{6,5},{7,4},{8,11},{9,10},{10,... | collective-permute-start | bytes 393224 | tf_op jit(solution)/shard_map/ppermute | solution.py:288
  16.0 2.8 %collective-permute-start.6 = (f32[2,16,8,128]{3,2,1,0:T(8,128)S(1)}, f32[2,16,8,128]{3,2,1,0:T(8,128)S(1)}, u32[]{:S(2)}, u32[]{:S(2)}) collective-permute-start(f32[2,16,8,128]{3,2,1,0:T(8,128)S(1)} %get-tuple-element.32), channel_id=1, source_target_pairs={{0,1},{1,0},{2,3},{3,2},{4,5},{5,4},{6,7},{7,6},{8,9},{9,8},{10,11... | collective-permute-start | bytes 393224 | tf_op jit(solution)/shard_map/ppermute | solution.py:288
  19.8 5.6 %collective-permute-start.9 = (f32[2,16,128]{2,1,0:T(8,128)S(1)}, f32[2,16,128]{2,1,0:T(8,128)S(1)}, u32[]{:S(2)}, u32[]{:S(2)}) collective-permute-start(f32[2,16,128]{2,1,0:T(8,128)S(1)} %get-tuple-element.36.rest_0_), channel_id=1, source_target_pairs={{0,24},{8,16},{16,8},{24,0},{1,25},{9,17},{17,9},{25,1},{2,26},{10... | collective-permute-start | bytes 49160 | tf_op jit(solution)/shard_map/ppermute | solution.py:288
  23.7 4.6 %collective-permute-start.8 = (f32[2,16,128]{2,1,0:T(8,128)S(1)}, f32[2,16,128]{2,1,0:T(8,128)S(1)}, u32[]{:S(2)}, u32[]{:S(2)}) collective-permute-start(f32[2,16,128]{2,1,0:T(8,128)S(1)} %get-tuple-element.36.rest_0_), channel_id=1, source_target_pairs={{0,16},{8,24},{16,0},{24,8},{1,17},{9,25},{17,1},{25,9},{2,18},{10... | collective-permute-start | bytes 49160 | tf_op jit(solution)/shard_map/ppermute | solution.py:288
  23.7 4.6 %collective-permute-start.7 = (f32[2,16,128]{2,1,0:T(8,128)S(1)}, f32[2,16,128]{2,1,0:T(8,128)S(1)}, u32[]{:S(2)}, u32[]{:S(2)}) collective-permute-start(f32[2,16,128]{2,1,0:T(8,128)S(1)} %get-tuple-element.36.rest_0_), channel_id=1, source_target_pairs={{0,8},{8,0},{16,24},{24,16},{1,9},{9,1},{17,25},{25,17},{2,10},{10... | collective-permute-start | bytes 49160 | tf_op jit(solution)/shard_map/ppermute | solution.py:288
  28.3 14.2 %copy-start = (bf16[256,256]{1,0:T(8,128)(2,1)S(1)}, bf16[256,256]{1,0:T(8,128)(2,1)}, u32[]{:S(2)}) copy-start(bf16[256,256]{1,0:T(8,128)(2,1)} %constant.25.clone.ol) | copy-start | bytes 393220
  28.3 14.2 %copy-start.1 = (bf16[256,256]{1,0:T(8,128)(2,1)S(1)}, bf16[256,256]{1,0:T(8,128)(2,1)}, u32[]{:S(2)}) copy-start(bf16[256,256]{1,0:T(8,128)(2,1)} %constant.24.clone.oh) | copy-start | bytes 393220
  28.3 14.2 %copy-start.2 = (bf16[256,256]{1,0:T(8,128)(2,1)S(1)}, bf16[256,256]{1,0:T(8,128)(2,1)}, u32[]{:S(2)}) copy-start(bf16[256,256]{1,0:T(8,128)(2,1)} %constant.23.clone.el) | copy-start | bytes 393220
  28.3 14.2 %copy-start.3 = (bf16[256,256]{1,0:T(8,128)(2,1)S(1)}, bf16[256,256]{1,0:T(8,128)(2,1)}, u32[]{:S(2)}) copy-start(bf16[256,256]{1,0:T(8,128)(2,1)} %constant.22.clone.eh) | copy-start | bytes 393220
  29.4 6.7 %collective-permute-start.10 = (f32[2,16,8,128]{3,2,1,0:T(8,128)S(1)}, f32[2,16,8,128]{3,2,1,0:T(8,128)S(1)}, u32[]{:S(2)}, u32[]{:S(2)}) collective-permute-start(f32[2,16,8,128]{3,2,1,0:T(8,128)S(1)} %get-tuple-element.38), channel_id=1, source_target_pairs={{0,6},{1,7},{2,4},{3,5},{4,2},{5,3},{6,0},{7,1},{8,14},{9,15},{10,... | collective-permute-start | bytes 393224 | tf_op jit(solution)/shard_map/ppermute | solution.py:288
  30.6 9.7 %collective-permute-start.11 = (f32[2,16,8,128]{3,2,1,0:T(8,128)S(1)}, f32[2,16,8,128]{3,2,1,0:T(8,128)S(1)}, u32[]{:S(2)}, u32[]{:S(2)}) collective-permute-start(f32[2,16,8,128]{3,2,1,0:T(8,128)S(1)} %get-tuple-element.39), channel_id=1, source_target_pairs={{0,4},{1,5},{2,6},{3,7},{4,0},{5,1},{6,2},{7,3},{8,12},{9,13},{10,... | collective-permute-start | bytes 393224 | tf_op jit(solution)/shard_map/ppermute | solution.py:288
  32.4 7.8 %collective-permute-start.12 = (f32[2,16,8,128]{3,2,1,0:T(8,128)S(1)}, f32[2,16,8,128]{3,2,1,0:T(8,128)S(1)}, u32[]{:S(2)}, u32[]{:S(2)}) collective-permute-start(f32[2,16,8,128]{3,2,1,0:T(8,128)S(1)} %get-tuple-element.40), channel_id=1, source_target_pairs={{0,2},{1,3},{2,0},{3,1},{4,6},{5,7},{6,4},{7,5},{8,10},{9,11},{10,... | collective-permute-start | bytes 393224 | tf_op jit(solution)/shard_map/ppermute | solution.py:288
  32.9 7.3 %collective-permute-start.13 = (f32[2,16,8,128]{3,2,1,0:T(8,128)S(1)}, f32[2,16,8,128]{3,2,1,0:T(8,128)S(1)}, u32[]{:S(2)}, u32[]{:S(2)}) collective-permute-start(f32[2,16,8,128]{3,2,1,0:T(8,128)S(1)} %get-tuple-element.41), channel_id=1, source_target_pairs={{0,7},{1,6},{2,5},{3,4},{4,3},{5,2},{6,1},{7,0},{8,15},{9,14},{10,... | collective-permute-start | bytes 393224 | tf_op jit(solution)/shard_map/ppermute | solution.py:288
  33.0 9.6 %collective-permute-start.14 = (f32[2,16,8,128]{3,2,1,0:T(8,128)S(1)}, f32[2,16,8,128]{3,2,1,0:T(8,128)S(1)}, u32[]{:S(2)}, u32[]{:S(2)}) collective-permute-start(f32[2,16,8,128]{3,2,1,0:T(8,128)S(1)} %get-tuple-element.42), channel_id=1, source_target_pairs={{0,5},{1,4},{2,7},{3,6},{4,1},{5,0},{6,3},{7,2},{8,13},{9,12},{10,... | collective-permute-start | bytes 393224 | tf_op jit(solution)/shard_map/ppermute | solution.py:288
  36.1 6.5 %collective-permute-start.15 = (f32[2,16,8,128]{3,2,1,0:T(8,128)S(1)}, f32[2,16,8,128]{3,2,1,0:T(8,128)S(1)}, u32[]{:S(2)}, u32[]{:S(2)}) collective-permute-start(f32[2,16,8,128]{3,2,1,0:T(8,128)S(1)} %get-tuple-element.43), channel_id=1, source_target_pairs={{0,3},{1,2},{2,1},{3,0},{4,7},{5,6},{6,5},{7,4},{8,11},{9,10},{10,... | collective-permute-start | bytes 393224 | tf_op jit(solution)/shard_map/ppermute | solution.py:288
  40.2 2.3 %collective-permute-start.16 = (f32[2,16,8,128]{3,2,1,0:T(8,128)S(1)}, f32[2,16,8,128]{3,2,1,0:T(8,128)S(1)}, u32[]{:S(2)}, u32[]{:S(2)}) collective-permute-start(f32[2,16,8,128]{3,2,1,0:T(8,128)S(1)} %get-tuple-element.44), channel_id=1, source_target_pairs={{0,1},{1,0},{2,3},{3,2},{4,5},{5,4},{6,7},{7,6},{8,9},{9,8},{10,11... | collective-permute-start | bytes 393224 | tf_op jit(solution)/shard_map/ppermute | solution.py:288

commit v3 on v2

--- a/solution.py
+++ b/solution.py
@@ -1,3 +1,4 @@
+import functools
 import math
 
 import numpy as np
@@ -152,6 +153,7 @@
     back_tables = [jnp.asarray(np.ascontiguousarray(t.T)) for t in (even_hi, even_lo, odd_hi, odd_lo)]
     eig_table = jnp.asarray(eig.reshape(chunks, lanes))
     f32 = jnp.float32
+    cover = pl.CostEstimate(flops=8 * 10**9, transcendentals=0, bytes_accessed=24 * 10**6)
     params = pltpu.CompilerParams(vmem_limit_bytes=VMEM_LIMIT)
     piece = (depth, steps, SUB, lanes)
     grain_run = min(steps, 8)
@@ -161,124 +163,196 @@
     hbm = pl.BlockSpec(memory_space=pltpu.HBM)
     shared = 2 if depth % 2 == 0 else 1
 
-    def source_kernel(rates_hbm, f_hbm, id_hbm, mask_hbm, eh_hbm, el_hbm, oh_hbm, ol_hbm, *rest):
-        outs = rest[:devices_z]
-        f_buf, id_buf, mask_buf, sums, diffs, modes, eh, el, oh, ol, rates = rest[devices_z:-3]
-        f_sems, tile_sems, table_sems = rest[-3:]
+    grain_runs = max(steps // 8, 1)
+    mask_runs = max(steps // 16, 1)
+    ahead = (
+        jax.ShapeDtypeStruct((depth, tiles, 2, local_x, LANES), f32),
+        jax.ShapeDtypeStruct((2, depth // shared, tiles, grain_runs, SUB, LANES), f32),
+        jax.ShapeDtypeStruct((tiles, mask_runs, SUB, LANES), f32),
+    ) + tuple(jax.ShapeDtypeStruct((half, half), jnp.bfloat16) for _ in range(4))
+
+    def fill(heat, tile, f_buf, rate_buf, sink_buf, sums, diffs):
+        for xi in range(steps):
+            at = pl.ds(xi, SUB, stride=steps)
+            for layer in range(depth):
+                rhs = []
+                for t in (tile, tile + tiles // 2):
+                    rate = rate_buf[int(heat), layer // shared, t, xi // 8]
+                    c = f_buf[layer, t, 0, at, :]
+                    h = f_buf[layer, t, 1, at, :]
+                    if heat:
+                        c2 = c * c
+                        value = h + rate * c2 / (1.0 + c2)
+                        if layer == 0:
+                            value = value - sink_buf[t, xi // 16] * (h + 1.0)
+                    else:
+                        value = c + rate * jnp.tanh(h - c)
+                    rhs.append(value)
+                rows = pl.ds((layer * steps + xi) * SUB, SUB)
+                cols = pl.ds(tile * LANES, LANES)
+                sums[rows, cols] = rhs[0] + rhs[1]
+                diffs[rows, cols] = rhs[0] - rhs[1]
+
+    def forward_y(g, tables_y, sums, diffs, modes, outs):
+        eh, el, oh, ol = tables_y
+        for parity, (src, hi, lo) in enumerate(((sums, eh, el), (diffs, oh, ol))):
+            both = dot3(src[...], hi[...], lo[...], ((1,), (0,)))
+            for chunk in range(chunks // 2):
+                part = both[:, chunk * lanes : (chunk + 1) * lanes]
+                modes[parity * (chunks // 2) + chunk] = part.reshape(piece)
+        for j in range(chunks):
+            outs[j][...] = modes[(g // 2) ^ j]
+
+    def first_kernel(rates_hbm, f_hbm, id_hbm, mask_hbm, *rest):
+        tables_hbm, outs = rest[:4], rest[4 : 4 + chunks]
+        f_buf, rate_buf, sink_buf = rest[4 + chunks : 7 + chunks]
+        tables_y = rest[7 + chunks : 11 + chunks]
+        id_buf, mask_buf, sums, diffs, modes, rates = rest[11 + chunks : -4]
+        f_sems, id_sems, mask_sems, table_sems = rest[-4:]
         g = lax.axis_index("gz")
-        field_copies = [
-            pltpu.make_async_copy(
-                f_hbm.at[:, layer, :, pl.ds(t * LANES, LANES)],
-                f_buf.at[layer, t],
-                f_sems.at[layer, t],
-            )
-            for layer in range(depth)
+        field = g % 2
+        rate_copy = pltpu.make_async_copy(rates_hbm, rates, table_sems.at[4])
+        id_copies = [
+            [
+                pltpu.make_async_copy(
+                    id_hbm.at[group * shared, :, pl.ds(t * LANES, LANES)],
+                    id_buf.at[group, t],
+                    id_sems.at[group, t],
+                )
+                for group in range(depth // shared)
+            ]
             for t in range(tiles)
         ]
-        tile_copies = []
-        for t in range(tiles):
-            cols = pl.ds(t * LANES, LANES)
-            for group in range(depth // shared):
-                tile_copies.append(
-                    pltpu.make_async_copy(
-                        id_hbm.at[group * shared, :, cols],
-                        id_buf.at[group, t],
-                        tile_sems.at[0, group, t],
-                    )
+        mask_copies = [
+            pltpu.make_async_copy(
+                mask_hbm.at[:, pl.ds(t * LANES, LANES)], mask_buf.at[t], mask_sems.at[t]
+            )
+            for t in range(tiles)
+        ]
+        field_copies = [
+            [
+                pltpu.make_async_copy(
+                    f_hbm.at[:, layer, :, pl.ds(t * LANES, LANES)],
+                    f_buf.at[layer, t],
+                    f_sems.at[layer, t],
                 )
-            tile_copies.append(
-                pltpu.make_async_copy(mask_hbm.at[:, cols], mask_buf.at[t], tile_sems.at[1, 0, t])
-            )
+                for layer in range(depth)
+            ]
+            for t in range(tiles)
+        ]
         table_copies = [
-            pltpu.make_async_copy(src, dst, table_sems.at[i])
-            for i, (src, dst) in enumerate(
-                ((eh_hbm, eh), (el_hbm, el), (oh_hbm, oh), (ol_hbm, ol))
-            )
+            pltpu.make_async_copy(tables_hbm[i], tables_y[i], table_sems.at[i]) for i in range(4)
         ]
-        tile_copies.append(pltpu.make_async_copy(rates_hbm, rates, table_sems.at[4]))
-        for copy in tile_copies + field_copies + table_copies:
+        rate_copy.start()
+        for copies in id_copies:
+            for copy in copies:
+                copy.start()
+
+        @pl.when(g == 0)
+        def _():
+            for copy in mask_copies:
+                copy.start()
+
+        for tile in range(tiles // 2):
+            for t in (tile, tile + tiles // 2):
+                for copy in field_copies[t]:
+                    copy.start()
+        for copy in table_copies:
             copy.start()
-        for copy in tile_copies:
+        rate_copy.wait()
+        for copies in id_copies:
+            for copy in copies:
+                copy.wait()
+        for group in range(depth // shared):
+            for t in range(tiles):
+                for run in range(grain_runs):
+                    ids = id_buf[group, t, pl.ds(run * 8, SUB, stride=steps), :]
+                    found = [jnp.zeros(ids.shape, f32)] * 2
+                    for grain in range(grain_count):
+                        hit = ids == grain
+                        found = [jnp.where(hit, rates[f, grain], found[f]) for f in range(2)]
+                    for f in range(2):
+                        rate_buf[f, group, t, run] = found[f]
+
+        @pl.when(g == 0)
+        def _():
+            for copy in mask_copies:
+                copy.wait()
+            for t in range(tiles):
+                for run in range(mask_runs):
+                    mask = mask_buf[t, pl.ds(run * 16, SUB, stride=steps), :]
+                    sink_buf[t, run] = mask.astype(f32) * heat_loss
+
+        @pl.when(g != 0)
+        def _():
+            sink_buf[...] = jnp.zeros_like(sink_buf)
+
+        for tile in range(tiles // 2):
+            for t in (tile, tile + tiles // 2):
+                for copy in field_copies[t]:
+                    copy.wait()
+            for heat in (False, True):
+                pl.when(field == int(heat))(
+                    functools.partial(fill, heat, tile, f_buf, rate_buf, sink_buf, sums, diffs)
+                )
+        for copy in table_copies:
             copy.wait()
-        for layer in range(depth):
-            first = jnp.where(g * depth + layer == 0, heat_loss, 0.0)
-            for copy in field_copies[layer * tiles : (layer + 1) * tiles]:
-                copy.wait()
-            for tile in range(tiles // 2):
-                pair = (tile, tile + tiles // 2)
-                rates_c, rates_h, sinks = [None] * 2, [None] * 2, [None] * 2
-                for xi in range(steps):
-                    at = pl.ds(xi, SUB, stride=steps)
-                    rhs = [[None] * 2, [None] * 2]
-                    for side in range(2):
-                        t = pair[side]
-                        if xi % grain_run == 0:
-                            ids = id_buf[layer // shared, t, at, :]
-                            rate_c = jnp.zeros(ids.shape, f32)
-                            rate_h = jnp.zeros(ids.shape, f32)
-                            for grain in range(grain_count):
-                                hit = ids == grain
-                                rate_c = jnp.where(hit, rates[0, grain], rate_c)
-                                rate_h = jnp.where(hit, rates[1, grain], rate_h)
-                            rates_c[side], rates_h[side] = rate_c, rate_h
-                        if xi % mask_run == 0:
-                            sinks[side] = mask_buf[t, at, :].astype(f32) * first
-                        c = f_buf[layer, t, 0, at, :]
-                        h = f_buf[layer, t, 1, at, :]
-                        square = c * c
-                        rhs[0][side] = c + rates_c[side] * jnp.tanh(h - c)
-                        rhs[1][side] = (
-                            h + rates_h[side] * square / (1.0 + square) - sinks[side] * (h + 1.0)
-                        )
-                    for f in range(2):
-                        rows = pl.ds((f * steps + xi) * SUB, SUB)
-                        cols = pl.ds(tile * LANES, LANES)
-                        sums[layer, rows, cols] = rhs[f][0] + rhs[f][1]
-                        diffs[layer, rows, cols] = rhs[f][0] - rhs[f][1]
-            if layer == 0:
-                for copy in table_copies:
-                    copy.wait()
-            for parity, (src, hi, lo) in enumerate(((sums, eh, el), (diffs, oh, ol))):
-                both = dot3(src[layer], hi[...], lo[...], ((1,), (0,)))
-                for f in range(2):
-                    for chunk in range(chunks // 2):
-                        part = both[
-                            f * local_x : (f + 1) * local_x, chunk * lanes : (chunk + 1) * lanes
-                        ]
-                        place = 2 * (chunk + parity * (chunks // 2)) + f
-                        modes[place, layer] = part.reshape(steps, SUB, lanes)
-        for k in range(devices_z):
-            outs[k][...] = modes[g ^ k]
-
-    square = (half, half)
-    pieces = pl.pallas_call(
-        source_kernel,
+        forward_y(g, tables_y, sums, diffs, modes, outs)
+
+    def second_kernel(f_buf, rate_buf, sink_buf, *rest):
+        tables_y, outs = rest[:4], rest[4 : 4 + chunks]
+        sums, diffs, modes = rest[4 + chunks :]
+        g = lax.axis_index("gz")
+        for heat in (False, True):
+
+            @pl.when(1 - g % 2 == int(heat))
+            def _(heat=heat):
+                for tile in range(tiles // 2):
+                    fill(heat, tile, f_buf, rate_buf, sink_buf, sums, diffs)
+
+        forward_y(g, tables_y, sums, diffs, modes, outs)
+
+    piece_shapes = [jax.ShapeDtypeStruct(piece, f32)] * chunks
+    work_scratch = [
+        pltpu.VMEM((depth * local_x, half), f32),
+        pltpu.VMEM((depth * local_x, half), f32),
+        pltpu.VMEM((chunks,) + piece, f32),
+    ]
+    first_out = pl.pallas_call(
+        first_kernel,
         in_specs=[hbm] * 8,
-        out_specs=[vmem] * devices_z,
-        out_shape=[jax.ShapeDtypeStruct(piece, f32)] * devices_z,
+        out_specs=[vmem] * (chunks + len(ahead)),
+        out_shape=piece_shapes + list(ahead),
         scratch_shapes=[
-            pltpu.VMEM((depth, tiles, 2, local_x, LANES), f32),
             pltpu.VMEM((depth // shared, tiles, local_x, LANES), jnp.int32),
             pltpu.VMEM((tiles, local_x, LANES), jnp.int32),
-            pltpu.VMEM((depth, 2 * local_x, half), f32),
-            pltpu.VMEM((depth, 2 * local_x, half), f32),
-            pltpu.VMEM((devices_z,) + piece, f32),
-        ]
-        + [pltpu.VMEM(square, jnp.bfloat16)] * 4
-        + [
+            *work_scratch,
             pltpu.SMEM((2, grain_count), f32),
             pltpu.SemaphoreType.DMA((depth, tiles)),
-            pltpu.SemaphoreType.DMA((2, depth // shared, tiles)),
+            pltpu.SemaphoreType.DMA((depth // shared, tiles)),
+            pltpu.SemaphoreType.DMA((tiles,)),
             pltpu.SemaphoreType.DMA((5,)),
         ],
         compiler_params=params,
-        name="sources",
+        name="sources_own",
     )(
         *(
             pltpu.with_memory_space_constraint(a, pltpu.HBM)
             for a in (grain_rates.T, fields, grain_ids, die_mask, *tables)
-        ),
+        )
     )
+    own_pieces = first_out[:chunks]
+    other_pieces = pl.pallas_call(
+        second_kernel,
+        in_specs=[vmem] * len(ahead),
+        out_specs=[vmem] * chunks,
+        out_shape=piece_shapes,
+        scratch_shapes=work_scratch,
+        compiler_params=params,
+        cost_estimate=cover,
+        name="sources_other",
+    )(*first_out[chunks:])
+    pieces = [(own_pieces, other_pieces)[k % 2][k // 2] for k in range(devices_z)]
 
     def exchange(arrays, axis, order):
         count = lax.axis_size(axis)
@@ -288,7 +362,9 @@
             out.append(lax.ppermute(arrays[k], axis, route) if k else arrays[k])
         return out
 
-    order_z = [0] + sorted(range(1, devices_z), key=lambda k: (k & 1, -k))
+    order_own = [0] + list(range(1, chunks))[::-1]
+    order_other = list(range(chunks))[::-1]
+    order_z = [2 * j for j in order_own] + [2 * j + 1 for j in order_other]
     order_x = list(range(devices_x))
 
     gathered = exchange(pieces, "gz", order_z)
@@ -424,53 +500,80 @@
 
     returned = exchange(solved, "gz", order_z)
 
-    def final_kernel(eh, el, oh, ol, *rest):
-        ins = rest[:devices_z]
-        out_ref, modes, buf, out_sems = rest[devices_z:]
+    def backward_y(tables_y, order, ins, modes, buf, done):
+        eh, el, oh, ol = tables_y
         g = lax.axis_index("gz")
-        for i, k in enumerate(order_z):
-            modes[g ^ k] = ins[i][...]
+        for i, j in enumerate(order):
+            modes[(g // 2) ^ j] = ins[i][...]
+        dims = ((1,), (0,))
+        parts = [modes[chunk].reshape(depth * local_x, lanes) for chunk in range(chunks)]
+        low = dot3(jnp.concatenate(parts[: chunks // 2], axis=1), eh[...], el[...], dims)
+        high = dot3(jnp.concatenate(parts[chunks // 2 :], axis=1), oh[...], ol[...], dims)
+        for side, value in enumerate((low + high, low - high)):
+            for layer in range(depth):
+                for col in range(tiles // 2):
+                    t = side * (tiles // 2) + col
+                    for xi in range(steps):
+                        at = (layer * steps + xi) * SUB
+                        buf[layer, t, pl.ds(xi, SUB, stride=steps), :] = value[
+                            at : at + SUB, col * LANES : (col + 1) * LANES
+                        ]
+                    done(layer, t)
+
+    def own_kernel(*refs):
+        buf, modes = refs[4 + chunks :]
+        backward_y(refs[:4], order_own, refs[4 : 4 + chunks], modes, buf, lambda layer, t: None)
+
+    def other_kernel(own_buf, *refs):
+        out_ref, modes, buf, own_sems, sems = refs[4 + chunks :]
+        mine = lax.axis_index("gz") % 2
         copies = []
-        dims = ((1,), (0,))
-        for f in range(2):
-            parts = [
-                modes[2 * chunk + f].reshape(depth * local_x, lanes) for chunk in range(chunks)
-            ]
-            low = dot3(jnp.concatenate(parts[: chunks // 2], axis=1), eh[...], el[...], dims)
-            high = dot3(jnp.concatenate(parts[chunks // 2 :], axis=1), oh[...], ol[...], dims)
-            for side, value in enumerate((low + high, low - high)):
-                for layer in range(depth):
-                    for col in range(tiles // 2):
-                        t = side * (tiles // 2) + col
-                        for xi in range(steps):
-                            at = (layer * steps + xi) * SUB
-                            buf[f, layer, t, pl.ds(xi, SUB, stride=steps), :] = value[
-                                at : at + SUB, col * LANES : (col + 1) * LANES
-                            ]
-                        copies.append(
-                            pltpu.make_async_copy(
-                                buf.at[f, layer, t],
-                                out_ref.at[f, layer, :, pl.ds(t * LANES, LANES)],
-                                out_sems.at[f, layer, t],
-                            )
-                        )
-                        copies[-1].start()
+
+        def send(source, field, layer, t, sem):
+            copies.append(
+                pltpu.make_async_copy(
+                    source.at[layer, t], out_ref.at[field, layer, :, pl.ds(t * LANES, LANES)], sem
+                )
+            )
+            copies[-1].start()
+
+        for layer in range(depth):
+            for t in range(tiles):
+                send(own_buf, mine, layer, t, own_sems.at[layer, t])
+        backward_y(
+            refs[:4],
+            order_other,
+            refs[4 : 4 + chunks],
+            modes,
+            buf,
+            lambda layer, t: send(buf, 1 - mine, layer, t, sems.at[layer, t]),
+        )
         for copy in copies:
             copy.wait()
 
+    by_source = dict(zip(order_z, returned))
+    buffer = (depth, tiles, local_x, LANES)
+    modes_scratch = pltpu.VMEM((chunks,) + piece, f32)
+    own_buf = pl.pallas_call(
+        own_kernel,
+        in_specs=[vmem] * (4 + chunks),
+        out_specs=vmem,
+        out_shape=jax.ShapeDtypeStruct(buffer, f32),
+        scratch_shapes=[modes_scratch],
+        compiler_params=params,
+        cost_estimate=cover,
+        name="finish_own",
+    )(*back_tables, *(by_source[2 * j] for j in order_own))
+    tile_sems = pltpu.SemaphoreType.DMA((depth, tiles))
     return pl.pallas_call(
-        final_kernel,
-        in_specs=[vmem] * (4 + devices_z),
+        other_kernel,
+        in_specs=[vmem] * (5 + chunks),
         out_specs=hbm,
         out_shape=jax.ShapeDtypeStruct((2, depth, local_x, span_y), f32),
-        scratch_shapes=[
-            pltpu.VMEM((devices_z,) + piece, f32),
-            pltpu.VMEM((2, depth, tiles, local_x, LANES), f32),
-            pltpu.SemaphoreType.DMA((2, depth, tiles)),
-        ],
+        scratch_shapes=[modes_scratch, pltpu.VMEM(buffer, f32), tile_sems, tile_sems],
         compiler_params=params,
-        name="finish",
-    )(*back_tables, *returned)
+        name="finish_other",
+    )(own_buf, *back_tables, *(by_source[2 * j + 1] for j in order_other))
 
 
 def solution(mesh):

time: 44.4 us -> 43.2 us (0.973)
  waiting for transfers between devices: 19 us -> 17.3 us
    ppermute x17, waiting for transfers between devices: 19 us -> 17.3 us  [exchange(): out.append(lax.ppermute(arrays[k], axis, route) if k else arrays[k])]
    pallas_call x2 -> x4, Pallas kernels: 4.64 us -> 4.84 us  [the longest x1 2.25 us: on_device_fn(): pl.pallas_call(first_kernel, in_specs=[hbm] * 8, out_specs=[vmem] * (chun...]
  transfers between devices with their start and end apart: 17 -> 17, of which waited for: 9 -> 8; matrix products, arithmetic and copies ran while one was open for 0% -> 0% of each run, Pallas kernels for 0% -> 3%
where the time goes in v3:
time: 43.2 us; the launch traced here: 43 us
  starting transfers between devices  18.7 us (43%)
  waiting for transfers between devices  17.3 us (40%)
  Pallas kernels  6.89 us (16%)
    ppermute x17, starting transfers between devices, exchange(): out.append(lax.ppermute(arrays[k], axis, route) if k else arrays[k])  18.7 us
    ppermute x17, waiting for transfers between devices, exchange(): out.append(lax.ppermute(arrays[k], axis, route) if k else arrays[k])  17.3 us
    pallas_call x1, Pallas kernels, on_device_fn(): pl.pallas_call(first_kernel, in_specs=[hbm] * 8, out_specs=[vmem] * (chun...  2.25 us
    pallas_call x1, Pallas kernels, on_device_fn(): pl.pallas_call(other_kernel, in_specs=[vmem] * (5 + chunks), out_specs=hb...  1.28 us
    pallas_call x1, Pallas kernels, on_device_fn(): pl.pallas_call(solve_kernel, in_specs=[vmem] * (4 + devices_x), out_specs...  1.03 us
    pallas_call x1, Pallas kernels, on_device_fn(): pl.pallas_call(gather_kernel, in_specs=[vmem] * (1 + devices_z), out_spec...  1.02 us
  transfers between devices with their start and end apart: 17, of which 8 were waited for; matrix products, arithmetic and copies ran while one was open for 0% of the time, Pallas kernels for 3%

profile of v3, /device:TPU:0, one launch (start us, length us, event | category | flops | bytes accessed | tf_op | source)
XLA Modules:
  0.0 43.0 jit_solution(16720717066686858781)
XLA Ops:
  0.0 2.2 %sources_own.1 = (f32[2,16,8,128]{3,2,1,0:T(8,128)S(1)}, f32[2,16,8,128]{3,2,1,0:T(8,128)S(1)}, f32[2,16,8,128]{3,2,1,0:T(8,128)S(1)}, f32[2,16,8,128]{3,2,1,0:T...) custom-call(f32[2,32]{1,0:T(2,128)} %bitcast.1, ...), custom_call_target="tpu_custom_call" | custom-call | tf_op jit(solution)/shard_map/sources_own/pallas_call | solution.py:321
  2.3 3.9 %collective-permute-start = (f32[2,16,8,128]{3,2,1,0:T(8,128)S(1)}, f32[2,16,8,128]{3,2,1,0:T(8,128)S(1)}, u32[]{:S(2)}, u32[]{:S(2)}) collective-permute-start(f32[2,16,8,128]{3,2,1,0:T(8,128)S(1)} %get-tuple-element.33), channel_id=1, source_target_pairs={{0,6},{1,7},{2,4},{3,5},{4,2},{5,3},{6,0},{7,1},{8,14},{9,15},{10,... | collective-permute-start | bytes 393224 | tf_op jit(solution)/shard_map/ppermute | solution.py:362
  6.1 0.5 %collective-permute-start.1 = (f32[2,16,8,128]{3,2,1,0:T(8,128)S(1)}, f32[2,16,8,128]{3,2,1,0:T(8,128)S(1)}, u32[]{:S(2)}, u32[]{:S(2)}) collective-permute-start(f32[2,16,8,128]{3,2,1,0:T(8,128)S(1)} %get-tuple-element.34), channel_id=1, source_target_pairs={{0,4},{1,5},{2,6},{3,7},{4,0},{5,1},{6,2},{7,3},{8,12},{9,13},{10,... | collective-permute-start | bytes 393224 | tf_op jit(solution)/shard_map/ppermute | solution.py:362
  6.8 0.7 %sources_other.1 = (f32[2,16,8,128]{3,2,1,0:T(8,128)S(1)}, f32[2,16,8,128]{3,2,1,0:T(8,128)S(1)}, f32[2,16,8,128]{3,2,1,0:T(8,128)S(1)}, f32[2,16,8,128]{3,2,1,0:T(8,128)S(1)}) custom-call(f32[2,4,2,128,128]{4,3,2,1,0:T(8,128)S(1)} %get-tuple-element.36.f_buf, f32[2,1,4,2,8,128]{5,4,3,2,1,0:T(8,128)S(1)} %get-tuple-element.37.rate_buf, ...), custom_call_target="tpu_custom_call" | custom-call | flops 8000000000 | bytes 24000000 | tf_op jit(solution)/shard_map/sources_other/pallas_call | solution.py:345
  7.5 1.5 %collective-permute-start.3 = (f32[2,16,8,128]{3,2,1,0:T(8,128)S(1)}, f32[2,16,8,128]{3,2,1,0:T(8,128)S(1)}, u32[]{:S(2)}, u32[]{:S(2)}) collective-permute-start(f32[2,16,8,128]{3,2,1,0:T(8,128)S(1)} %get-tuple-element.43), channel_id=1, source_target_pairs={{0,7},{1,6},{2,5},{3,4},{4,3},{5,2},{6,1},{7,0},{8,15},{9,14},{10,... | collective-permute-start | bytes 393224 | tf_op jit(solution)/shard_map/ppermute | solution.py:362
  9.0 1.6 %collective-permute-start.4 = (f32[2,16,8,128]{3,2,1,0:T(8,128)S(1)}, f32[2,16,8,128]{3,2,1,0:T(8,128)S(1)}, u32[]{:S(2)}, u32[]{:S(2)}) collective-permute-start(f32[2,16,8,128]{3,2,1,0:T(8,128)S(1)} %get-tuple-element.44), channel_id=1, source_target_pairs={{0,5},{1,4},{2,7},{3,6},{4,1},{5,0},{6,3},{7,2},{8,13},{9,12},{10,... | collective-permute-start | bytes 393224 | tf_op jit(solution)/shard_map/ppermute | solution.py:362
  10.8 2.8 %collective-permute-done.1.rest_2_ = f32[2,16,8,128]{3,2,1,0:T(8,128)S(1)} collective-permute-done((f32[2,16,8,128]{3,2,1,0:T(8,128)S(1)}, f32[2,16,8,128]{3,2,1,0:T(8,128)S(1)}, u32[]{:S(2)}, u32[]{:S(2)}) %collective-permute-start.1) | collective-permute-done | bytes 131104 | tf_op jit(solution)/shard_map/ppermute | solution.py:362
  13.6 1.7 %collective-permute-done.3.rest_4_ = f32[2,16,8,128]{3,2,1,0:T(8,128)S(1)} collective-permute-done((f32[2,16,8,128]{3,2,1,0:T(8,128)S(1)}, f32[2,16,8,128]{3,2,1,0:T(8,128)S(1)}, u32[]{:S(2)}, u32[]{:S(2)}) %collective-permute-start.3) | collective-permute-done | bytes 131104 | tf_op jit(solution)/shard_map/ppermute | solution.py:362
  15.4 2.5 %collective-permute-done.4.rest_5_ = f32[2,16,8,128]{3,2,1,0:T(8,128)S(1)} collective-permute-done((f32[2,16,8,128]{3,2,1,0:T(8,128)S(1)}, f32[2,16,8,128]{3,2,1,0:T(8,128)S(1)}, u32[]{:S(2)}, u32[]{:S(2)}) %collective-permute-start.4) | collective-permute-done | bytes 131104 | tf_op jit(solution)/shard_map/ppermute | solution.py:362
  17.9 1.0 %gather.1 = (f32[16,16,8,128]{3,2,1,0:T(8,128)S(1)}, f32[16,8,128]{2,1,0:T(8,128)S(1)}, f32[16,8,128]{2,1,0:T(8,128)S(1)}, f32[2,16,128]{2,1,0:T(8,128)S(1)}) custom-call(f32[4,128]{1,0:T(4,128)S(1)} %copy-done.4, f32[2,16,8,128]{3,2,1,0:T(8,128)S(1)} %get-tuple-element.32.rest_0_, f32[2,16,8,128]{3,2,1,0:T(8,128)S(1)} %collective-permute-done.rest_1_, ...), custom_call_target="tpu_custom_call" | custom-call | tf_op jit(solution)/shard_map/gather/pallas_call | solution.py:419
  18.9 4.0 %collective-permute-start.9 = (f32[2,16,128]{2,1,0:T(8,128)S(1)}, f32[2,16,128]{2,1,0:T(8,128)S(1)}, u32[]{:S(2)}, u32[]{:S(2)}) collective-permute-start(f32[2,16,128]{2,1,0:T(8,128)S(1)} %get-tuple-element.50.rest_0_), channel_id=1, source_target_pairs={{0,24},{8,16},{16,8},{24,0},{1,25},{9,17},{17,9},{25,1},{2,26},{10... | collective-permute-start | bytes 49160 | tf_op jit(solution)/shard_map/ppermute | solution.py:362
  22.9 0.6 %collective-permute-start.7 = (f32[2,16,128]{2,1,0:T(8,128)S(1)}, f32[2,16,128]{2,1,0:T(8,128)S(1)}, u32[]{:S(2)}, u32[]{:S(2)}) collective-permute-start(f32[2,16,128]{2,1,0:T(8,128)S(1)} %get-tuple-element.50.rest_0_), channel_id=1, source_target_pairs={{0,8},{8,0},{16,24},{24,16},{1,9},{9,1},{17,25},{25,17},{2,10},{10... | collective-permute-start | bytes 49160 | tf_op jit(solution)/shard_map/ppermute | solution.py:362
  23.5 1.1 %collective-permute-done.9.rest_3_ = f32[2,16,128]{2,1,0:T(8,128)S(1)} collective-permute-done((f32[2,16,128]{2,1,0:T(8,128)S(1)}, f32[2,16,128]{2,1,0:T(8,128)S(1)}, u32[]{:S(2)}, u32[]{:S(2)}) %collective-permute-start.9) | collective-permute-done | bytes 16416 | tf_op jit(solution)/shard_map/ppermute | solution.py:362
  24.6 2.9 %collective-permute-done.8.rest_2_ = f32[2,16,128]{2,1,0:T(8,128)S(1)} collective-permute-done((f32[2,16,128]{2,1,0:T(8,128)S(1)}, f32[2,16,128]{2,1,0:T(8,128)S(1)}, u32[]{:S(2)}, u32[]{:S(2)}) %collective-permute-start.8) | collective-permute-done | bytes 16416 | tf_op jit(solution)/shard_map/ppermute | solution.py:362
  27.5 1.0 %solve.1 = (f32[2,16,8,128]{3,2,1,0:T(8,128)S(1)}, f32[2,16,8,128]{3,2,1,0:T(8,128)S(1)}, f32[2,16,8,128]{3,2,1,0:T(8,128)S(1)}, f32[2,16,8,128]{3,2,1,0:T(8,128...) custom-call(f32[4,128]{1,0:T(4,128)S(1)} %copy-done.4, ...), custom_call_target="tpu_custom_call" | custom-call | tf_op jit(solution)/shard_map/solve/pallas_call | solution.py:487
  28.6 1.2 %collective-permute-start.10 = (f32[2,16,8,128]{3,2,1,0:T(8,128)S(1)}, f32[2,16,8,128]{3,2,1,0:T(8,128)S(1)}, u32[]{:S(2)}, u32[]{:S(2)}) collective-permute-start(f32[2,16,8,128]{3,2,1,0:T(8,128)S(1)} %get-tuple-element.52), channel_id=1, source_target_pairs={{0,6},{1,7},{2,4},{3,5},{4,2},{5,3},{6,0},{7,1},{8,14},{9,15},{10,... | collective-permute-start | bytes 393224 | tf_op jit(solution)/shard_map/ppermute | solution.py:362
  29.7 1.9 %collective-permute-start.11 = (f32[2,16,8,128]{3,2,1,0:T(8,128)S(1)}, f32[2,16,8,128]{3,2,1,0:T(8,128)S(1)}, u32[]{:S(2)}, u32[]{:S(2)}) collective-permute-start(f32[2,16,8,128]{3,2,1,0:T(8,128)S(1)} %get-tuple-element.53), channel_id=1, source_target_pairs={{0,4},{1,5},{2,6},{3,7},{4,0},{5,1},{6,2},{7,3},{8,12},{9,13},{10,... | collective-permute-start | bytes 393224 | tf_op jit(solution)/shard_map/ppermute | solution.py:362
  31.6 0.5 %collective-permute-start.12 = (f32[2,16,8,128]{3,2,1,0:T(8,128)S(1)}, f32[2,16,8,128]{3,2,1,0:T(8,128)S(1)}, u32[]{:S(2)}, u32[]{:S(2)}) collective-permute-start(f32[2,16,8,128]{3,2,1,0:T(8,128)S(1)} %get-tuple-element.54), channel_id=1, source_target_pairs={{0,2},{1,3},{2,0},{3,1},{4,6},{5,7},{6,4},{7,5},{8,10},{9,11},{10,... | collective-permute-start | bytes 393224 | tf_op jit(solution)/shard_map/ppermute | solution.py:362
  32.1 2.7 %collective-permute-start.14 = (f32[2,16,8,128]{3,2,1,0:T(8,128)S(1)}, f32[2,16,8,128]{3,2,1,0:T(8,128)S(1)}, u32[]{:S(2)}, u32[]{:S(2)}) collective-permute-start(f32[2,16,8,128]{3,2,1,0:T(8,128)S(1)} %get-tuple-element.56), channel_id=1, source_target_pairs={{0,5},{1,4},{2,7},{3,6},{4,1},{5,0},{6,3},{7,2},{8,13},{9,12},{10,... | collective-permute-start | bytes 393224 | tf_op jit(solution)/shard_map/ppermute | solution.py:362
  34.8 0.4 %collective-permute-done.10.refs_5_ = f32[2,16,8,128]{3,2,1,0:T(8,128)S(1)} collective-permute-done((f32[2,16,8,128]{3,2,1,0:T(8,128)S(1)}, f32[2,16,8,128]{3,2,1,0:T(8,128)S(1)}, u32[]{:S(2)}, u32[]{:S(2)}) %collective-permute-start.10) | collective-permute-done | bytes 131104 | tf_op jit(solution)/shard_map/ppermute | solution.py:362
  35.3 4.2 %collective-permute-done.11.refs_6_ = f32[2,16,8,128]{3,2,1,0:T(8,128)S(1)} collective-permute-done((f32[2,16,8,128]{3,2,1,0:T(8,128)S(1)}, f32[2,16,8,128]{3,2,1,0:T(8,128)S(1)}, u32[]{:S(2)}, u32[]{:S(2)}) %collective-permute-start.11) | collective-permute-done | bytes 131104 | tf_op jit(solution)/shard_map/ppermute | solution.py:362
  39.5 0.6 %finish_own.1.own_buf = f32[2,4,128,128]{3,2,1,0:T(8,128)S(1)} custom-call(bf16[256,256]{1,0:T(8,128)(2,1)S(1)} %copy-done.3, bf16[256,256]{1,0:T(8,128)(2,1)S(1)} %copy-done.2, bf16[256,256]{1,0:T(8,128)(2,1)S(1)} %copy-done.1, bf16[256,256]{1,0:T(8,128)(2,1)S(1)} %copy-done, f32[2,16,8,128]{3,2,1,0:T(8,128)S(1)} %get-tuple-element.51.refs_4_, ...), custom_call_target="tpu_custom_call" | custom-call | flops 8000000000 | bytes 24000000 | tf_op jit(solution)/shard_map/finish_own/pallas_call | solution.py:557
  40.0 1.7 %collective-permute-done.14.refs_5_ = f32[2,16,8,128]{3,2,1,0:T(8,128)S(1)} collective-permute-done((f32[2,16,8,128]{3,2,1,0:T(8,128)S(1)}, f32[2,16,8,128]{3,2,1,0:T(8,128)S(1)}, u32[]{:S(2)}, u32[]{:S(2)}) %collective-permute-start.14) | collective-permute-done | bytes 131104 | tf_op jit(solution)/shard_map/ppermute | solution.py:362
  41.8 1.3 %finish_other.1 = f32[2,2,128,512]{3,2,1,0:T(8,128)} custom-call(f32[2,4,128,128]{3,2,1,0:T(8,128)S(1)} %finish_own.1.own_buf, bf16[256,256]{1,0:T(8,128)(2,1)S(1)} %copy-done.3, bf16[256,256]{1,0:T(8,128)(2,1)S(1)} %copy-done.2, bf16[256,256]{1,0:T(8,128)(2,1)S(1)} %copy-done.1, bf16[256,256]{1,0:T(8,128)(2,1)S(1)} %copy-done, ...), custom_call_target="tpu_custom_call" | custom-call | tf_op jit(solution)/shard_map/finish_other/pallas_call | solution.py:568
  (26 shorter events, 0.3 us)
Async XLA Ops:
  2.3 8.4 %collective-permute-start = (f32[2,16,8,128]{3,2,1,0:T(8,128)S(1)}, f32[2,16,8,128]{3,2,1,0:T(8,128)S(1)}, u32[]{:S(2)}, u32[]{:S(2)}) collective-permute-start(f32[2,16,8,128]{3,2,1,0:T(8,128)S(1)} %get-tuple-element.33), channel_id=1, source_target_pairs={{0,6},{1,7},{2,4},{3,5},{4,2},{5,3},{6,0},{7,1},{8,14},{9,15},{10,... | collective-permute-start | bytes 393224 | tf_op jit(solution)/shard_map/ppermute | solution.py:362
  6.1 7.5 %collective-permute-start.1 = (f32[2,16,8,128]{3,2,1,0:T(8,128)S(1)}, f32[2,16,8,128]{3,2,1,0:T(8,128)S(1)}, u32[]{:S(2)}, u32[]{:S(2)}) collective-permute-start(f32[2,16,8,128]{3,2,1,0:T(8,128)S(1)} %get-tuple-element.34), channel_id=1, source_target_pairs={{0,4},{1,5},{2,6},{3,7},{4,0},{5,1},{6,2},{7,3},{8,12},{9,13},{10,... | collective-permute-start | bytes 393224 | tf_op jit(solution)/shard_map/ppermute | solution.py:362
  6.6 7.0 %collective-permute-start.2 = (f32[2,16,8,128]{3,2,1,0:T(8,128)S(1)}, f32[2,16,8,128]{3,2,1,0:T(8,128)S(1)}, u32[]{:S(2)}, u32[]{:S(2)}) collective-permute-start(f32[2,16,8,128]{3,2,1,0:T(8,128)S(1)} %get-tuple-element.35), channel_id=1, source_target_pairs={{0,2},{1,3},{2,0},{3,1},{4,6},{5,7},{6,4},{7,5},{8,10},{9,11},{10,... | collective-permute-start | bytes 393224 | tf_op jit(solution)/shard_map/ppermute | solution.py:362
  7.5 7.8 %collective-permute-start.3 = (f32[2,16,8,128]{3,2,1,0:T(8,128)S(1)}, f32[2,16,8,128]{3,2,1,0:T(8,128)S(1)}, u32[]{:S(2)}, u32[]{:S(2)}) collective-permute-start(f32[2,16,8,128]{3,2,1,0:T(8,128)S(1)} %get-tuple-element.43), channel_id=1, source_target_pairs={{0,7},{1,6},{2,5},{3,4},{4,3},{5,2},{6,1},{7,0},{8,15},{9,14},{10,... | collective-permute-start | bytes 393224 | tf_op jit(solution)/shard_map/ppermute | solution.py:362
  9.0 8.8 %collective-permute-start.4 = (f32[2,16,8,128]{3,2,1,0:T(8,128)S(1)}, f32[2,16,8,128]{3,2,1,0:T(8,128)S(1)}, u32[]{:S(2)}, u32[]{:S(2)}) collective-permute-start(f32[2,16,8,128]{3,2,1,0:T(8,128)S(1)} %get-tuple-element.44), channel_id=1, source_target_pairs={{0,5},{1,4},{2,7},{3,6},{4,1},{5,0},{6,3},{7,2},{8,13},{9,12},{10,... | collective-permute-start | bytes 393224 | tf_op jit(solution)/shard_map/ppermute | solution.py:362
  10.7 7.2 %copy-start.4 = (f32[4,128]{1,0:T(4,128)S(1)}, f32[4,128]{1,0:T(4,128)}, u32[]{:S(2)}) copy-start(f32[4,128]{1,0:T(4,128)} %constant.26.clone.eig_ref) | copy-start | bytes 6148
  10.7 7.2 %collective-permute-start.5 = (f32[2,16,8,128]{3,2,1,0:T(8,128)S(1)}, f32[2,16,8,128]{3,2,1,0:T(8,128)S(1)}, u32[]{:S(2)}, u32[]{:S(2)}) collective-permute-start(f32[2,16,8,128]{3,2,1,0:T(8,128)S(1)} %get-tuple-element.45), channel_id=1, source_target_pairs={{0,3},{1,2},{2,1},{3,0},{4,7},{5,6},{6,5},{7,4},{8,11},{9,10},{10,... | collective-permute-start | bytes 393224 | tf_op jit(solution)/shard_map/ppermute | solution.py:362
  13.6 4.2 %collective-permute-start.6 = (f32[2,16,8,128]{3,2,1,0:T(8,128)S(1)}, f32[2,16,8,128]{3,2,1,0:T(8,128)S(1)}, u32[]{:S(2)}, u32[]{:S(2)}) collective-permute-start(f32[2,16,8,128]{3,2,1,0:T(8,128)S(1)} %get-tuple-element.46), channel_id=1, source_target_pairs={{0,1},{1,0},{2,3},{3,2},{4,5},{5,4},{6,7},{7,6},{8,9},{9,8},{10,11... | collective-permute-start | bytes 393224 | tf_op jit(solution)/shard_map/ppermute | solution.py:362
  18.9 5.7 %collective-permute-start.9 = (f32[2,16,128]{2,1,0:T(8,128)S(1)}, f32[2,16,128]{2,1,0:T(8,128)S(1)}, u32[]{:S(2)}, u32[]{:S(2)}) collective-permute-start(f32[2,16,128]{2,1,0:T(8,128)S(1)} %get-tuple-element.50.rest_0_), channel_id=1, source_target_pairs={{0,24},{8,16},{16,8},{24,0},{1,25},{9,17},{17,9},{25,1},{2,26},{10... | collective-permute-start | bytes 49160 | tf_op jit(solution)/shard_map/ppermute | solution.py:362
  22.9 4.6 %collective-permute-start.8 = (f32[2,16,128]{2,1,0:T(8,128)S(1)}, f32[2,16,128]{2,1,0:T(8,128)S(1)}, u32[]{:S(2)}, u32[]{:S(2)}) collective-permute-start(f32[2,16,128]{2,1,0:T(8,128)S(1)} %get-tuple-element.50.rest_0_), channel_id=1, source_target_pairs={{0,16},{8,24},{16,0},{24,8},{1,17},{9,25},{17,1},{25,9},{2,18},{10... | collective-permute-start | bytes 49160 | tf_op jit(solution)/shard_map/ppermute | solution.py:362
  22.9 4.6 %collective-permute-start.7 = (f32[2,16,128]{2,1,0:T(8,128)S(1)}, f32[2,16,128]{2,1,0:T(8,128)S(1)}, u32[]{:S(2)}, u32[]{:S(2)}) collective-permute-start(f32[2,16,128]{2,1,0:T(8,128)S(1)} %get-tuple-element.50.rest_0_), channel_id=1, source_target_pairs={{0,8},{8,0},{16,24},{24,16},{1,9},{9,1},{17,25},{25,17},{2,10},{10... | collective-permute-start | bytes 49160 | tf_op jit(solution)/shard_map/ppermute | solution.py:362
  27.5 11.9 %copy-start = (bf16[256,256]{1,0:T(8,128)(2,1)S(1)}, bf16[256,256]{1,0:T(8,128)(2,1)}, u32[]{:S(2)}) copy-start(bf16[256,256]{1,0:T(8,128)(2,1)} %constant.25.clone.refs_3_) | copy-start | bytes 393220
  27.5 11.9 %copy-start.1 = (bf16[256,256]{1,0:T(8,128)(2,1)S(1)}, bf16[256,256]{1,0:T(8,128)(2,1)}, u32[]{:S(2)}) copy-start(bf16[256,256]{1,0:T(8,128)(2,1)} %constant.24.clone.refs_2_) | copy-start | bytes 393220
  27.5 11.9 %copy-start.2 = (bf16[256,256]{1,0:T(8,128)(2,1)S(1)}, bf16[256,256]{1,0:T(8,128)(2,1)}, u32[]{:S(2)}) copy-start(bf16[256,256]{1,0:T(8,128)(2,1)} %constant.23.clone.refs_1_) | copy-start | bytes 393220
  27.5 11.9 %copy-start.3 = (bf16[256,256]{1,0:T(8,128)(2,1)S(1)}, bf16[256,256]{1,0:T(8,128)(2,1)}, u32[]{:S(2)}) copy-start(bf16[256,256]{1,0:T(8,128)(2,1)} %constant.22.clone.refs_0_) | copy-start | bytes 393220
  28.6 6.7 %collective-permute-start.10 = (f32[2,16,8,128]{3,2,1,0:T(8,128)S(1)}, f32[2,16,8,128]{3,2,1,0:T(8,128)S(1)}, u32[]{:S(2)}, u32[]{:S(2)}) collective-permute-start(f32[2,16,8,128]{3,2,1,0:T(8,128)S(1)} %get-tuple-element.52), channel_id=1, source_target_pairs={{0,6},{1,7},{2,4},{3,5},{4,2},{5,3},{6,0},{7,1},{8,14},{9,15},{10,... | collective-permute-start | bytes 393224 | tf_op jit(solution)/shard_map/ppermute | solution.py:362
  29.7 9.7 %collective-permute-start.11 = (f32[2,16,8,128]{3,2,1,0:T(8,128)S(1)}, f32[2,16,8,128]{3,2,1,0:T(8,128)S(1)}, u32[]{:S(2)}, u32[]{:S(2)}) collective-permute-start(f32[2,16,8,128]{3,2,1,0:T(8,128)S(1)} %get-tuple-element.53), channel_id=1, source_target_pairs={{0,4},{1,5},{2,6},{3,7},{4,0},{5,1},{6,2},{7,3},{8,12},{9,13},{10,... | collective-permute-start | bytes 393224 | tf_op jit(solution)/shard_map/ppermute | solution.py:362
  31.6 7.8 %collective-permute-start.12 = (f32[2,16,8,128]{3,2,1,0:T(8,128)S(1)}, f32[2,16,8,128]{3,2,1,0:T(8,128)S(1)}, u32[]{:S(2)}, u32[]{:S(2)}) collective-permute-start(f32[2,16,8,128]{3,2,1,0:T(8,128)S(1)} %get-tuple-element.54), channel_id=1, source_target_pairs={{0,2},{1,3},{2,0},{3,1},{4,6},{5,7},{6,4},{7,5},{8,10},{9,11},{10,... | collective-permute-start | bytes 393224 | tf_op jit(solution)/shard_map/ppermute | solution.py:362
  32.1 7.9 %collective-permute-start.13 = (f32[2,16,8,128]{3,2,1,0:T(8,128)S(1)}, f32[2,16,8,128]{3,2,1,0:T(8,128)S(1)}, u32[]{:S(2)}, u32[]{:S(2)}) collective-permute-start(f32[2,16,8,128]{3,2,1,0:T(8,128)S(1)} %get-tuple-element.55), channel_id=1, source_target_pairs={{0,7},{1,6},{2,5},{3,4},{4,3},{5,2},{6,1},{7,0},{8,15},{9,14},{10,... | collective-permute-start | bytes 393224 | tf_op jit(solution)/shard_map/ppermute | solution.py:362
  32.1 9.6 %collective-permute-start.14 = (f32[2,16,8,128]{3,2,1,0:T(8,128)S(1)}, f32[2,16,8,128]{3,2,1,0:T(8,128)S(1)}, u32[]{:S(2)}, u32[]{:S(2)}) collective-permute-start(f32[2,16,8,128]{3,2,1,0:T(8,128)S(1)} %get-tuple-element.56), channel_id=1, source_target_pairs={{0,5},{1,4},{2,7},{3,6},{4,1},{5,0},{6,3},{7,2},{8,13},{9,12},{10,... | collective-permute-start | bytes 393224 | tf_op jit(solution)/shard_map/ppermute | solution.py:362
  35.3 6.5 %collective-permute-start.15 = (f32[2,16,8,128]{3,2,1,0:T(8,128)S(1)}, f32[2,16,8,128]{3,2,1,0:T(8,128)S(1)}, u32[]{:S(2)}, u32[]{:S(2)}) collective-permute-start(f32[2,16,8,128]{3,2,1,0:T(8,128)S(1)} %get-tuple-element.57), channel_id=1, source_target_pairs={{0,3},{1,2},{2,1},{3,0},{4,7},{5,6},{6,5},{7,4},{8,11},{9,10},{10,... | collective-permute-start | bytes 393224 | tf_op jit(solution)/shard_map/ppermute | solution.py:362
  39.4 2.3 %collective-permute-start.16 = (f32[2,16,8,128]{3,2,1,0:T(8,128)S(1)}, f32[2,16,8,128]{3,2,1,0:T(8,128)S(1)}, u32[]{:S(2)}, u32[]{:S(2)}) collective-permute-start(f32[2,16,8,128]{3,2,1,0:T(8,128)S(1)} %get-tuple-element.58), channel_id=1, source_target_pairs={{0,1},{1,0},{2,3},{3,2},{4,5},{5,4},{6,7},{7,6},{8,9},{9,8},{10,11... | collective-permute-start | bytes 393224 | tf_op jit(solution)/shard_map/ppermute | solution.py:362

commit v4 on v3

--- a/solution.py
+++ b/solution.py
@@ -171,6 +171,10 @@
         jax.ShapeDtypeStruct((tiles, mask_runs, SUB, LANES), f32),
     ) + tuple(jax.ShapeDtypeStruct((half, half), jnp.bfloat16) for _ in range(4))
 
+    layer_eig = [4.0 * math.sin(math.pi * k / (2 * layers)) ** 2 for k in range(layers)]
+    per_run = jax.ShapeDtypeStruct((layers, SUB, lanes), f32)
+    factor_shapes = [per_run] * 4 + [jax.ShapeDtypeStruct((devices_x, layers, lanes), f32)]
+
     def fill(heat, tile, f_buf, rate_buf, sink_buf, sums, diffs):
         for xi in range(steps):
             at = pl.ds(xi, SUB, stride=steps)
@@ -203,11 +207,12 @@
         for j in range(chunks):
             outs[j][...] = modes[(g // 2) ^ j]
 
-    def first_kernel(rates_hbm, f_hbm, id_hbm, mask_hbm, *rest):
+    def first_kernel(rates_hbm, eig_hbm, f_hbm, id_hbm, mask_hbm, *rest):
         tables_hbm, outs = rest[:4], rest[4 : 4 + chunks]
         f_buf, rate_buf, sink_buf = rest[4 + chunks : 7 + chunks]
         tables_y = rest[7 + chunks : 11 + chunks]
-        id_buf, mask_buf, sums, diffs, modes, rates = rest[11 + chunks : -4]
+        decay_ref, gain_ref, up_ref, down_ref, weight_ref = rest[11 + chunks : 16 + chunks]
+        id_buf, mask_buf, sums, diffs, modes, rates, eig_ref = rest[16 + chunks : -4]
         f_sems, id_sems, mask_sems, table_sems = rest[-4:]
         g = lax.axis_index("gz")
         field = g % 2
@@ -243,6 +248,8 @@
         table_copies = [
             pltpu.make_async_copy(tables_hbm[i], tables_y[i], table_sems.at[i]) for i in range(4)
         ]
+        eig_copy = pltpu.make_async_copy(eig_hbm, eig_ref, table_sems.at[5])
+        eig_copy.start()
         rate_copy.start()
         for copies in id_copies:
             for copy in copies:
@@ -259,6 +266,25 @@
                     copy.start()
         for copy in table_copies:
             copy.start()
+        eig_copy.wait()
+        spread = jnp.where(g % 2 == 0, spread_solute, spread_heat).astype(f32)
+        eig_one = eig_ref[pl.ds(g // 2, 1), :]
+        eig_rows = jnp.broadcast_to(eig_one, (SUB, lanes))
+        row = lax.broadcasted_iota(jnp.int32, (SUB, lanes), 0)
+        for k in range(layers):
+            decay, root = line_factors(eig_rows, spread, layer_eig[k])
+            step_decay = power(decay, steps)
+            decay_ref[k] = decay
+            gain_ref[k] = ((1.0 if k == 0 else 2.0) / layers) / root
+            up_ref[k] = sublane_powers(step_decay, row, False)
+            down_ref[k] = sublane_powers(step_decay, row, True)
+            block_decay = power(decay[:1], local_x)
+            weight = jnp.ones_like(block_decay)
+            for m in range(devices_x):
+                weight_ref[m, pl.ds(k, 1), :] = weight
+                weight = weight * block_decay
+            for m in range(devices_x):
+                weight_ref[m, pl.ds(k, 1), :] = weight_ref[m, pl.ds(k, 1), :] / (1.0 - weight)
         rate_copy.wait()
         for copies in id_copies:
             for copy in copies:
@@ -320,25 +346,26 @@
     ]
     first_out = pl.pallas_call(
         first_kernel,
-        in_specs=[hbm] * 8,
-        out_specs=[vmem] * (chunks + len(ahead)),
-        out_shape=piece_shapes + list(ahead),
+        in_specs=[hbm] * 9,
+        out_specs=[vmem] * (chunks + len(ahead) + len(factor_shapes)),
+        out_shape=piece_shapes + list(ahead) + factor_shapes,
         scratch_shapes=[
             pltpu.VMEM((depth // shared, tiles, local_x, LANES), jnp.int32),
             pltpu.VMEM((tiles, local_x, LANES), jnp.int32),
             *work_scratch,
             pltpu.SMEM((2, grain_count), f32),
+            pltpu.VMEM((chunks, lanes), f32),
             pltpu.SemaphoreType.DMA((depth, tiles)),
             pltpu.SemaphoreType.DMA((depth // shared, tiles)),
             pltpu.SemaphoreType.DMA((tiles,)),
-            pltpu.SemaphoreType.DMA((5,)),
+            pltpu.SemaphoreType.DMA((6,)),
         ],
         compiler_params=params,
         name="sources_own",
     )(
         *(
             pltpu.with_memory_space_constraint(a, pltpu.HBM)
-            for a in (grain_rates.T, fields, grain_ids, die_mask, *tables)
+            for a in (grain_rates.T, eig_table, fields, grain_ids, die_mask, *tables)
         )
     )
     own_pieces = first_out[:chunks]
@@ -351,7 +378,8 @@
         compiler_params=params,
         cost_estimate=cover,
         name="sources_other",
-    )(*first_out[chunks:])
+    )(*first_out[chunks : chunks + len(ahead)])
+    decays, gains, ups, downs, weights = first_out[chunks + len(ahead) :]
     pieces = [(own_pieces, other_pieces)[k % 2][k // 2] for k in range(devices_z)]
 
     def exchange(arrays, axis, order):
@@ -369,18 +397,10 @@
 
     gathered = exchange(pieces, "gz", order_z)
 
-    def line_setup(eig_ref):
+    def gather_kernel(decay_ref, up_ref, down_ref, *rest):
+        ins = rest[:devices_z]
+        hat_ref, left_ref, right_ref, ends, field = rest[devices_z:]
         g = lax.axis_index("gz")
-        spread = jnp.where(g % 2 == 0, spread_solute, spread_heat).astype(f32)
-        eig_rows = jnp.broadcast_to(eig_ref[pl.ds(g // 2, 1), :], (SUB, lanes))
-        return g, spread, eig_rows
-
-    layer_eig = [4.0 * math.sin(math.pi * k / (2 * layers)) ** 2 for k in range(layers)]
-
-    def gather_kernel(eig_ref, *rest):
-        ins = rest[: devices_z]
-        hat_ref, from_left, from_right, ends, field = rest[devices_z:]
-        g, spread, eig_rows = line_setup(eig_ref)
         for i, k in enumerate(order_z):
             field[pl.ds((g ^ k) * depth, depth)] = ins[i][...]
 
@@ -390,23 +410,40 @@
                 hat_ref[k, xi] = hat[k]
             return carry
 
-        lax.fori_loop(0, steps, transform, 0)
-        row = lax.broadcasted_iota(jnp.int32, (SUB, lanes), 0)
+        lax.fori_loop(0, steps, transform, 0, unroll=4)
         for k in range(layers):
-            decay, _ = line_factors(eig_rows, spread, layer_eig[k])
+            decay = decay_ref[k]
             left = hat_ref[k, 0]
             right = hat_ref[k, steps - 1]
             for xi in range(1, steps):
                 left = hat_ref[k, xi] + decay * left
                 right = hat_ref[k, steps - 1 - xi] + decay * right
-            step_decay = power(decay, steps)
-            up = sublane_powers(step_decay, row, False)
-            down = sublane_powers(step_decay, row, True)
-            ends[0, pl.ds(k, 1), :] = jnp.sum(left * down, axis=0, keepdims=True)
-            ends[1, pl.ds(k, 1), :] = jnp.sum(right * up, axis=0, keepdims=True)
-            left = jnp.where(row >= 1, pltpu.roll(left, 1, 0), 0.0)
-            right = jnp.where(row < SUB - 1, pltpu.roll(right, SUB - 1, 0), 0.0)
-            factor = step_decay
+            ends[0, pl.ds(k, 1), :] = jnp.sum(left * down_ref[k], axis=0, keepdims=True)
+            ends[1, pl.ds(k, 1), :] = jnp.sum(right * up_ref[k], axis=0, keepdims=True)
+            left_ref[k] = left
+            right_ref[k] = right
+
+    hat, lefts, rights, ends = pl.pallas_call(
+        gather_kernel,
+        in_specs=[vmem] * (3 + devices_z),
+        out_specs=[vmem] * 4,
+        out_shape=[
+            jax.ShapeDtypeStruct((layers, steps, SUB, lanes), f32),
+            per_run,
+            per_run,
+            jax.ShapeDtypeStruct((2, layers, lanes), f32),
+        ],
+        scratch_shapes=[pltpu.VMEM((layers, steps, SUB, lanes), f32)],
+        compiler_params=params,
+        name="gather",
+    )(decays, ups, downs, *gathered)
+
+    def carry_kernel(decay_ref, left_ref, right_ref, from_left, from_right):
+        row = lax.broadcasted_iota(jnp.int32, (SUB, lanes), 0)
+        for k in range(layers):
+            factor = power(decay_ref[k], steps)
+            left = jnp.where(row >= 1, pltpu.roll(left_ref[k], 1, 0), 0.0)
+            right = jnp.where(row < SUB - 1, pltpu.roll(right_ref[k], SUB - 1, 0), 0.0)
             for shift in (1, 2, 4):
                 left = left + factor * jnp.where(row >= shift, pltpu.roll(left, shift, 0), 0.0)
                 right = right + factor * jnp.where(
@@ -416,56 +453,37 @@
             from_left[k] = left
             from_right[k] = right
 
-    hat, from_left, from_right, ends = pl.pallas_call(
-        gather_kernel,
-        in_specs=[vmem] * (1 + devices_z),
-        out_specs=[vmem] * 4,
-        out_shape=[
-            jax.ShapeDtypeStruct((layers, steps, SUB, lanes), f32),
-            jax.ShapeDtypeStruct((layers, SUB, lanes), f32),
-            jax.ShapeDtypeStruct((layers, SUB, lanes), f32),
-            jax.ShapeDtypeStruct((2, layers, lanes), f32),
-        ],
-        scratch_shapes=[
-            pltpu.VMEM((layers, steps, SUB, lanes), f32),
-        ],
+    from_left, from_right = pl.pallas_call(
+        carry_kernel,
+        in_specs=[vmem] * 3,
+        out_specs=[vmem] * 2,
+        out_shape=[per_run] * 2,
         compiler_params=params,
-        name="gather",
-    )(eig_table, *gathered)
+        cost_estimate=cover,
+        name="carry",
+    )(decays, lefts, rights)
 
     all_ends = exchange([ends] * devices_x, "gx", order_x)
 
-    def solve_kernel(eig_ref, hat_ref, left_ref, right_ref, *rest):
-        end_refs = rest[: devices_x]
+    def solve_kernel(decay_ref, gain_ref, up_ref, down_ref, weight_ref, hat_ref, left_ref, right_ref, *rest):
+        end_refs = rest[:devices_x]
         outs = rest[devices_x : devices_x + devices_z]
         near, work, entry = rest[devices_x + devices_z :]
-        g, spread, eig_rows = line_setup(eig_ref)
+        g = lax.axis_index("gz")
         place = lax.axis_index("gx")
         for i, k in enumerate(order_x):
             near[place ^ k] = end_refs[i][...]
-        row = lax.broadcasted_iota(jnp.int32, (SUB, lanes), 0)
-        eig_one = eig_ref[pl.ds(g // 2, 1), :]
-        kz = lax.broadcasted_iota(jnp.int32, (layers, lanes), 0).astype(f32)
-        eig_z = 4.0 * jnp.sin(kz * (math.pi / (2 * layers))) ** 2
-        decay_all, _ = line_factors(eig_one, spread, eig_z)
-        block_decay = power(decay_all, local_x)
-        total_left = near[(place + devices_x - 1) % devices_x, 0]
-        total_right = near[(place + 1) % devices_x, 1]
-        weight = block_decay
-        for m in range(2, devices_x + 1):
-            total_left = total_left + weight * near[(place + devices_x - m) % devices_x, 0]
-            total_right = total_right + weight * near[(place + m) % devices_x, 1]
-            weight = weight * block_decay
-        entry[0] = total_left / (1.0 - weight)
-        entry[1] = total_right / (1.0 - weight)
+        for direction in range(2):
+            total = None
+            for m in range(1, devices_x + 1):
+                shift = m if direction else devices_x - m
+                value = weight_ref[m - 1] * near[(place + shift) % devices_x, direction]
+                total = value if total is None else total + value
+            entry[direction] = total
         for k in range(layers):
-            decay, root = line_factors(eig_rows, spread, layer_eig[k])
-            gain = ((1.0 if k == 0 else 2.0) / layers) / root
-            step_decay = power(decay, steps)
-            up = sublane_powers(step_decay, row, False)
-            down = sublane_powers(step_decay, row, True)
-            left = left_ref[k] + up * entry[0, pl.ds(k, 1), :]
-            right = right_ref[k] + down * entry[1, pl.ds(k, 1), :]
+            decay, gain = decay_ref[k], gain_ref[k]
+            left = left_ref[k] + up_ref[k] * entry[0, pl.ds(k, 1), :]
+            right = right_ref[k] + down_ref[k] * entry[1, pl.ds(k, 1), :]
             for xi in range(steps):
                 left = hat_ref[k, xi] + decay * left
                 work[k, xi] = left
@@ -480,13 +498,13 @@
                 work[z, xi] = values[z]
             return carry
 
-        lax.fori_loop(0, steps, back, 0)
+        lax.fori_loop(0, steps, back, 0, unroll=4)
         for k in range(devices_z):
             outs[k][...] = work[pl.ds((g ^ k) * depth, depth)]
 
     solved = pl.pallas_call(
         solve_kernel,
-        in_specs=[vmem] * (4 + devices_x),
+        in_specs=[vmem] * (8 + devices_x),
         out_specs=[vmem] * devices_z,
         out_shape=[jax.ShapeDtypeStruct(piece, f32)] * devices_z,
         scratch_shapes=[
@@ -496,7 +514,7 @@
         ],
         compiler_params=params,
         name="solve",
-    )(eig_table, hat, from_left, from_right, *all_ends)
+    )(decays, gains, ups, downs, weights, hat, from_left, from_right, *all_ends)
 
     returned = exchange(solved, "gz", order_z)
 

time: 43.2 us -> 42.6 us (0.986)
  Pallas kernels: 6.89 us -> 6.4 us
    pallas_call x3 -> x4, Pallas kernels: 4.3 us -> 3.81 us  [the longest x1 2.27 us: on_device_fn(): pl.pallas_call(first_kernel, in_specs=[hbm] * 9, out_specs=[vmem] * (chun...]
where the time goes in v4:
time: 42.6 us; the launch traced here: 42.5 us
  starting transfers between devices  18.7 us (44%)
  waiting for transfers between devices  17.3 us (41%)
  Pallas kernels  6.4 us (15%)
    ppermute x17, starting transfers between devices, exchange(): out.append(lax.ppermute(arrays[k], axis, route) if k else arrays[k])  18.7 us
    ppermute x17, waiting for transfers between devices, exchange(): out.append(lax.ppermute(arrays[k], axis, route) if k else arrays[k])  17.3 us
    pallas_call x1, Pallas kernels, on_device_fn(): pl.pallas_call(first_kernel, in_specs=[hbm] * 9, out_specs=[vmem] * (chun...  2.27 us
    pallas_call x1, Pallas kernels, on_device_fn(): pl.pallas_call(other_kernel, in_specs=[vmem] * (5 + chunks), out_specs=hb...  1.28 us
  transfers between devices with their start and end apart: 17, of which 8 were waited for; matrix products, arithmetic and copies ran while one was open for 0% of the time, Pallas kernels for 3%

profile of v4, /device:TPU:0, one launch (start us, length us, event | category | flops | bytes accessed | tf_op | source)
XLA Modules:
  0.0 42.5 jit_solution(12605677742725964384)
XLA Ops:
  0.0 2.3 %sources_own.1 = (f32[2,16,8,128]{3,2,1,0:T(8,128)S(1)}, f32[2,16,8,128]{3,2,1,0:T(8,128)S(1)}, f32[2,16,8,128]{3,2,1,0:T(8,128)S(1)}, f32[2,16,8,128]{3,2,1,0:T...) custom-call(f32[2,32]{1,0:T(2,128)} %bitcast.1, ...), custom_call_target="tpu_custom_call" | custom-call | tf_op jit(solution)/shard_map/sources_own/pallas_call | solution.py:347
  2.3 3.9 %collective-permute-start = (f32[2,16,8,128]{3,2,1,0:T(8,128)S(1)}, f32[2,16,8,128]{3,2,1,0:T(8,128)S(1)}, u32[]{:S(2)}, u32[]{:S(2)}) collective-permute-start(f32[2,16,8,128]{3,2,1,0:T(8,128)S(1)} %get-tuple-element.45), channel_id=1, source_target_pairs={{0,6},{1,7},{2,4},{3,5},{4,2},{5,3},{6,0},{7,1},{8,14},{9,15},{10,... | collective-permute-start | bytes 393224 | tf_op jit(solution)/shard_map/ppermute | solution.py:390
  6.2 0.5 %collective-permute-start.1 = (f32[2,16,8,128]{3,2,1,0:T(8,128)S(1)}, f32[2,16,8,128]{3,2,1,0:T(8,128)S(1)}, u32[]{:S(2)}, u32[]{:S(2)}) collective-permute-start(f32[2,16,8,128]{3,2,1,0:T(8,128)S(1)} %get-tuple-element.46), channel_id=1, source_target_pairs={{0,4},{1,5},{2,6},{3,7},{4,0},{5,1},{6,2},{7,3},{8,12},{9,13},{10,... | collective-permute-start | bytes 393224 | tf_op jit(solution)/shard_map/ppermute | solution.py:390
  6.8 0.7 %sources_other.1 = (f32[2,16,8,128]{3,2,1,0:T(8,128)S(1)}, f32[2,16,8,128]{3,2,1,0:T(8,128)S(1)}, f32[2,16,8,128]{3,2,1,0:T(8,128)S(1)}, f32[2,16,8,128]{3,2,1,0:T(8,128)S(1)}) custom-call(f32[2,4,2,128,128]{4,3,2,1,0:T(8,128)S(1)} %get-tuple-element.48.f_buf, f32[2,1,4,2,8,128]{5,4,3,2,1,0:T(8,128)S(1)} %get-tuple-element.49.rate_buf, ...), custom_call_target="tpu_custom_call" | custom-call | flops 8000000000 | bytes 24000000 | tf_op jit(solution)/shard_map/sources_other/pallas_call | solution.py:372
  7.6 1.5 %collective-permute-start.3 = (f32[2,16,8,128]{3,2,1,0:T(8,128)S(1)}, f32[2,16,8,128]{3,2,1,0:T(8,128)S(1)}, u32[]{:S(2)}, u32[]{:S(2)}) collective-permute-start(f32[2,16,8,128]{3,2,1,0:T(8,128)S(1)} %get-tuple-element.55), channel_id=1, source_target_pairs={{0,7},{1,6},{2,5},{3,4},{4,3},{5,2},{6,1},{7,0},{8,15},{9,14},{10,... | collective-permute-start | bytes 393224 | tf_op jit(solution)/shard_map/ppermute | solution.py:390
  9.1 1.6 %collective-permute-start.4 = (f32[2,16,8,128]{3,2,1,0:T(8,128)S(1)}, f32[2,16,8,128]{3,2,1,0:T(8,128)S(1)}, u32[]{:S(2)}, u32[]{:S(2)}) collective-permute-start(f32[2,16,8,128]{3,2,1,0:T(8,128)S(1)} %get-tuple-element.56), channel_id=1, source_target_pairs={{0,5},{1,4},{2,7},{3,6},{4,1},{5,0},{6,3},{7,2},{8,13},{9,12},{10,... | collective-permute-start | bytes 393224 | tf_op jit(solution)/shard_map/ppermute | solution.py:390
  10.8 2.8 %collective-permute-done.1.rest_2_ = f32[2,16,8,128]{3,2,1,0:T(8,128)S(1)} collective-permute-done((f32[2,16,8,128]{3,2,1,0:T(8,128)S(1)}, f32[2,16,8,128]{3,2,1,0:T(8,128)S(1)}, u32[]{:S(2)}, u32[]{:S(2)}) %collective-permute-start.1) | collective-permute-done | bytes 131104 | tf_op jit(solution)/shard_map/ppermute | solution.py:390
  13.7 1.7 %collective-permute-done.3.rest_4_ = f32[2,16,8,128]{3,2,1,0:T(8,128)S(1)} collective-permute-done((f32[2,16,8,128]{3,2,1,0:T(8,128)S(1)}, f32[2,16,8,128]{3,2,1,0:T(8,128)S(1)}, u32[]{:S(2)}, u32[]{:S(2)}) %collective-permute-start.3) | collective-permute-done | bytes 131104 | tf_op jit(solution)/shard_map/ppermute | solution.py:390
  15.4 2.5 %collective-permute-done.4.rest_5_ = f32[2,16,8,128]{3,2,1,0:T(8,128)S(1)} collective-permute-done((f32[2,16,8,128]{3,2,1,0:T(8,128)S(1)}, f32[2,16,8,128]{3,2,1,0:T(8,128)S(1)}, u32[]{:S(2)}, u32[]{:S(2)}) %collective-permute-start.4) | collective-permute-done | bytes 131104 | tf_op jit(solution)/shard_map/ppermute | solution.py:390
  17.9 0.7 %gather.1 = (f32[16,16,8,128]{3,2,1,0:T(8,128)S(1)}, f32[16,8,128]{2,1,0:T(8,128)S(1)}, f32[16,8,128]{2,1,0:T(8,128)S(1)}, f32[2,16,128]{2,1,0:T(8,128)S(1)}) custom-call(f32[16,8,128]{2,1,0:T(8,128)S(1)} %get-tuple-element.39.decay_ref, f32[16,8,128]{2,1,0:T(8,128)S(1)} %get-tuple-element.41.up_ref, f32[16,8,128]{2,1,0:T(8,128)S(1)} %get-tuple-element.42.down_ref, ...), custom_call_target="tpu_custom_call" | custom-call | tf_op jit(solution)/shard_map/gather/pallas_call | solution.py:426
  18.6 4.0 %collective-permute-start.9 = (f32[2,16,128]{2,1,0:T(8,128)S(1)}, f32[2,16,128]{2,1,0:T(8,128)S(1)}, u32[]{:S(2)}, u32[]{:S(2)}) collective-permute-start(f32[2,16,128]{2,1,0:T(8,128)S(1)} %get-tuple-element.64.rest_0_), channel_id=1, source_target_pairs={{0,24},{8,16},{16,8},{24,0},{1,25},{9,17},{17,9},{25,1},{2,26},{10... | collective-permute-start | bytes 49160 | tf_op jit(solution)/shard_map/ppermute | solution.py:390
  22.6 0.6 %collective-permute-start.7 = (f32[2,16,128]{2,1,0:T(8,128)S(1)}, f32[2,16,128]{2,1,0:T(8,128)S(1)}, u32[]{:S(2)}, u32[]{:S(2)}) collective-permute-start(f32[2,16,128]{2,1,0:T(8,128)S(1)} %get-tuple-element.64.rest_0_), channel_id=1, source_target_pairs={{0,8},{8,0},{16,24},{24,16},{1,9},{9,1},{17,25},{25,17},{2,10},{10... | collective-permute-start | bytes 49160 | tf_op jit(solution)/shard_map/ppermute | solution.py:390
  23.3 1.0 %collective-permute-done.9.rest_3_ = f32[2,16,128]{2,1,0:T(8,128)S(1)} collective-permute-done((f32[2,16,128]{2,1,0:T(8,128)S(1)}, f32[2,16,128]{2,1,0:T(8,128)S(1)}, u32[]{:S(2)}, u32[]{:S(2)}) %collective-permute-start.9) | collective-permute-done | bytes 16416 | tf_op jit(solution)/shard_map/ppermute | solution.py:390
  24.3 2.9 %collective-permute-done.8.rest_2_ = f32[2,16,128]{2,1,0:T(8,128)S(1)} collective-permute-done((f32[2,16,128]{2,1,0:T(8,128)S(1)}, f32[2,16,128]{2,1,0:T(8,128)S(1)}, u32[]{:S(2)}, u32[]{:S(2)}) %collective-permute-start.8) | collective-permute-done | bytes 16416 | tf_op jit(solution)/shard_map/ppermute | solution.py:390
  27.2 0.8 %solve.1 = (f32[2,16,8,128]{3,2,1,0:T(8,128)S(1)}, f32[2,16,8,128]{3,2,1,0:T(8,128)S(1)}, f32[2,16,8,128]{3,2,1,0:T(8,128)S(1)}, f32[2,16,8,128]{3,2,1,0:T(8,128...) custom-call(f32[16,8,128]{2,1,0:T(8,128)S(1)} %get-tuple-element.39., ...), custom_call_target="tpu_custom_call" | custom-call | tf_op jit(solution)/shard_map/solve/pallas_call | solution.py:505
  28.0 1.2 %collective-permute-start.10 = (f32[2,16,8,128]{3,2,1,0:T(8,128)S(1)}, f32[2,16,8,128]{3,2,1,0:T(8,128)S(1)}, u32[]{:S(2)}, u32[]{:S(2)}) collective-permute-start(f32[2,16,8,128]{3,2,1,0:T(8,128)S(1)} %get-tuple-element.66), channel_id=1, source_target_pairs={{0,6},{1,7},{2,4},{3,5},{4,2},{5,3},{6,0},{7,1},{8,14},{9,15},{10,... | collective-permute-start | bytes 393224 | tf_op jit(solution)/shard_map/ppermute | solution.py:390
  29.2 1.9 %collective-permute-start.11 = (f32[2,16,8,128]{3,2,1,0:T(8,128)S(1)}, f32[2,16,8,128]{3,2,1,0:T(8,128)S(1)}, u32[]{:S(2)}, u32[]{:S(2)}) collective-permute-start(f32[2,16,8,128]{3,2,1,0:T(8,128)S(1)} %get-tuple-element.67), channel_id=1, source_target_pairs={{0,4},{1,5},{2,6},{3,7},{4,0},{5,1},{6,2},{7,3},{8,12},{9,13},{10,... | collective-permute-start | bytes 393224 | tf_op jit(solution)/shard_map/ppermute | solution.py:390
  31.0 0.5 %collective-permute-start.12 = (f32[2,16,8,128]{3,2,1,0:T(8,128)S(1)}, f32[2,16,8,128]{3,2,1,0:T(8,128)S(1)}, u32[]{:S(2)}, u32[]{:S(2)}) collective-permute-start(f32[2,16,8,128]{3,2,1,0:T(8,128)S(1)} %get-tuple-element.68), channel_id=1, source_target_pairs={{0,2},{1,3},{2,0},{3,1},{4,6},{5,7},{6,4},{7,5},{8,10},{9,11},{10,... | collective-permute-start | bytes 393224 | tf_op jit(solution)/shard_map/ppermute | solution.py:390
  31.6 2.7 %collective-permute-start.14 = (f32[2,16,8,128]{3,2,1,0:T(8,128)S(1)}, f32[2,16,8,128]{3,2,1,0:T(8,128)S(1)}, u32[]{:S(2)}, u32[]{:S(2)}) collective-permute-start(f32[2,16,8,128]{3,2,1,0:T(8,128)S(1)} %get-tuple-element.70), channel_id=1, source_target_pairs={{0,5},{1,4},{2,7},{3,6},{4,1},{5,0},{6,3},{7,2},{8,13},{9,12},{10,... | collective-permute-start | bytes 393224 | tf_op jit(solution)/shard_map/ppermute | solution.py:390
  34.2 0.4 %collective-permute-done.10.refs_5_ = f32[2,16,8,128]{3,2,1,0:T(8,128)S(1)} collective-permute-done((f32[2,16,8,128]{3,2,1,0:T(8,128)S(1)}, f32[2,16,8,128]{3,2,1,0:T(8,128)S(1)}, u32[]{:S(2)}, u32[]{:S(2)}) %collective-permute-start.10) | collective-permute-done | bytes 131104 | tf_op jit(solution)/shard_map/ppermute | solution.py:390
  34.7 4.2 %collective-permute-done.11.refs_6_ = f32[2,16,8,128]{3,2,1,0:T(8,128)S(1)} collective-permute-done((f32[2,16,8,128]{3,2,1,0:T(8,128)S(1)}, f32[2,16,8,128]{3,2,1,0:T(8,128)S(1)}, u32[]{:S(2)}, u32[]{:S(2)}) %collective-permute-start.11) | collective-permute-done | bytes 131104 | tf_op jit(solution)/shard_map/ppermute | solution.py:390
  38.9 0.6 %finish_own.1.own_buf = f32[2,4,128,128]{3,2,1,0:T(8,128)S(1)} custom-call(bf16[256,256]{1,0:T(8,128)(2,1)S(1)} %copy-done.3, bf16[256,256]{1,0:T(8,128)(2,1)S(1)} %copy-done.2, bf16[256,256]{1,0:T(8,128)(2,1)S(1)} %copy-done.1, bf16[256,256]{1,0:T(8,128)(2,1)S(1)} %copy-done, f32[2,16,8,128]{3,2,1,0:T(8,128)S(1)} %get-tuple-element.65.refs_4_, ...), custom_call_target="tpu_custom_call" | custom-call | flops 8000000000 | bytes 24000000 | tf_op jit(solution)/shard_map/finish_own/pallas_call | solution.py:575
  39.5 1.7 %collective-permute-done.14.refs_5_ = f32[2,16,8,128]{3,2,1,0:T(8,128)S(1)} collective-permute-done((f32[2,16,8,128]{3,2,1,0:T(8,128)S(1)}, f32[2,16,8,128]{3,2,1,0:T(8,128)S(1)}, u32[]{:S(2)}, u32[]{:S(2)}) %collective-permute-start.14) | collective-permute-done | bytes 131104 | tf_op jit(solution)/shard_map/ppermute | solution.py:390
  41.2 1.3 %finish_other.1 = f32[2,2,128,512]{3,2,1,0:T(8,128)} custom-call(f32[2,4,128,128]{3,2,1,0:T(8,128)S(1)} %finish_own.1.own_buf, bf16[256,256]{1,0:T(8,128)(2,1)S(1)} %copy-done.3, bf16[256,256]{1,0:T(8,128)(2,1)S(1)} %copy-done.2, bf16[256,256]{1,0:T(8,128)(2,1)S(1)} %copy-done.1, bf16[256,256]{1,0:T(8,128)(2,1)S(1)} %copy-done, ...), custom_call_target="tpu_custom_call" | custom-call | tf_op jit(solution)/shard_map/finish_other/pallas_call | solution.py:586
  (25 shorter events, 0.4 us)
Async XLA Ops:
  2.3 8.4 %collective-permute-start = (f32[2,16,8,128]{3,2,1,0:T(8,128)S(1)}, f32[2,16,8,128]{3,2,1,0:T(8,128)S(1)}, u32[]{:S(2)}, u32[]{:S(2)}) collective-permute-start(f32[2,16,8,128]{3,2,1,0:T(8,128)S(1)} %get-tuple-element.45), channel_id=1, source_target_pairs={{0,6},{1,7},{2,4},{3,5},{4,2},{5,3},{6,0},{7,1},{8,14},{9,15},{10,... | collective-permute-start | bytes 393224 | tf_op jit(solution)/shard_map/ppermute | solution.py:390
  6.2 7.5 %collective-permute-start.1 = (f32[2,16,8,128]{3,2,1,0:T(8,128)S(1)}, f32[2,16,8,128]{3,2,1,0:T(8,128)S(1)}, u32[]{:S(2)}, u32[]{:S(2)}) collective-permute-start(f32[2,16,8,128]{3,2,1,0:T(8,128)S(1)} %get-tuple-element.46), channel_id=1, source_target_pairs={{0,4},{1,5},{2,6},{3,7},{4,0},{5,1},{6,2},{7,3},{8,12},{9,13},{10,... | collective-permute-start | bytes 393224 | tf_op jit(solution)/shard_map/ppermute | solution.py:390
  6.7 7.0 %collective-permute-start.2 = (f32[2,16,8,128]{3,2,1,0:T(8,128)S(1)}, f32[2,16,8,128]{3,2,1,0:T(8,128)S(1)}, u32[]{:S(2)}, u32[]{:S(2)}) collective-permute-start(f32[2,16,8,128]{3,2,1,0:T(8,128)S(1)} %get-tuple-element.47), channel_id=1, source_target_pairs={{0,2},{1,3},{2,0},{3,1},{4,6},{5,7},{6,4},{7,5},{8,10},{9,11},{10,... | collective-permute-start | bytes 393224 | tf_op jit(solution)/shard_map/ppermute | solution.py:390
  7.6 7.8 %collective-permute-start.3 = (f32[2,16,8,128]{3,2,1,0:T(8,128)S(1)}, f32[2,16,8,128]{3,2,1,0:T(8,128)S(1)}, u32[]{:S(2)}, u32[]{:S(2)}) collective-permute-start(f32[2,16,8,128]{3,2,1,0:T(8,128)S(1)} %get-tuple-element.55), channel_id=1, source_target_pairs={{0,7},{1,6},{2,5},{3,4},{4,3},{5,2},{6,1},{7,0},{8,15},{9,14},{10,... | collective-permute-start | bytes 393224 | tf_op jit(solution)/shard_map/ppermute | solution.py:390
  9.1 8.8 %collective-permute-start.4 = (f32[2,16,8,128]{3,2,1,0:T(8,128)S(1)}, f32[2,16,8,128]{3,2,1,0:T(8,128)S(1)}, u32[]{:S(2)}, u32[]{:S(2)}) collective-permute-start(f32[2,16,8,128]{3,2,1,0:T(8,128)S(1)} %get-tuple-element.56), channel_id=1, source_target_pairs={{0,5},{1,4},{2,7},{3,6},{4,1},{5,0},{6,3},{7,2},{8,13},{9,12},{10,... | collective-permute-start | bytes 393224 | tf_op jit(solution)/shard_map/ppermute | solution.py:390
  10.7 7.2 %collective-permute-start.5 = (f32[2,16,8,128]{3,2,1,0:T(8,128)S(1)}, f32[2,16,8,128]{3,2,1,0:T(8,128)S(1)}, u32[]{:S(2)}, u32[]{:S(2)}) collective-permute-start(f32[2,16,8,128]{3,2,1,0:T(8,128)S(1)} %get-tuple-element.57), channel_id=1, source_target_pairs={{0,3},{1,2},{2,1},{3,0},{4,7},{5,6},{6,5},{7,4},{8,11},{9,10},{10,... | collective-permute-start | bytes 393224 | tf_op jit(solution)/shard_map/ppermute | solution.py:390
  13.7 4.2 %collective-permute-start.6 = (f32[2,16,8,128]{3,2,1,0:T(8,128)S(1)}, f32[2,16,8,128]{3,2,1,0:T(8,128)S(1)}, u32[]{:S(2)}, u32[]{:S(2)}) collective-permute-start(f32[2,16,8,128]{3,2,1,0:T(8,128)S(1)} %get-tuple-element.58), channel_id=1, source_target_pairs={{0,1},{1,0},{2,3},{3,2},{4,5},{5,4},{6,7},{7,6},{8,9},{9,8},{10,11... | collective-permute-start | bytes 393224 | tf_op jit(solution)/shard_map/ppermute | solution.py:390
  18.6 5.7 %collective-permute-start.9 = (f32[2,16,128]{2,1,0:T(8,128)S(1)}, f32[2,16,128]{2,1,0:T(8,128)S(1)}, u32[]{:S(2)}, u32[]{:S(2)}) collective-permute-start(f32[2,16,128]{2,1,0:T(8,128)S(1)} %get-tuple-element.64.rest_0_), channel_id=1, source_target_pairs={{0,24},{8,16},{16,8},{24,0},{1,25},{9,17},{17,9},{25,1},{2,26},{10... | collective-permute-start | bytes 49160 | tf_op jit(solution)/shard_map/ppermute | solution.py:390
  22.6 4.6 %collective-permute-start.8 = (f32[2,16,128]{2,1,0:T(8,128)S(1)}, f32[2,16,128]{2,1,0:T(8,128)S(1)}, u32[]{:S(2)}, u32[]{:S(2)}) collective-permute-start(f32[2,16,128]{2,1,0:T(8,128)S(1)} %get-tuple-element.64.rest_0_), channel_id=1, source_target_pairs={{0,16},{8,24},{16,0},{24,8},{1,17},{9,25},{17,1},{25,9},{2,18},{10... | collective-permute-start | bytes 49160 | tf_op jit(solution)/shard_map/ppermute | solution.py:390
  22.6 4.6 %collective-permute-start.7 = (f32[2,16,128]{2,1,0:T(8,128)S(1)}, f32[2,16,128]{2,1,0:T(8,128)S(1)}, u32[]{:S(2)}, u32[]{:S(2)}) collective-permute-start(f32[2,16,128]{2,1,0:T(8,128)S(1)} %get-tuple-element.64.rest_0_), channel_id=1, source_target_pairs={{0,8},{8,0},{16,24},{24,16},{1,9},{9,1},{17,25},{25,17},{2,10},{10... | collective-permute-start | bytes 49160 | tf_op jit(solution)/shard_map/ppermute | solution.py:390
  27.2 11.7 %copy-start = (bf16[256,256]{1,0:T(8,128)(2,1)S(1)}, bf16[256,256]{1,0:T(8,128)(2,1)}, u32[]{:S(2)}) copy-start(bf16[256,256]{1,0:T(8,128)(2,1)} %constant.25.clone.refs_3_) | copy-start | bytes 393220
  27.2 11.7 %copy-start.1 = (bf16[256,256]{1,0:T(8,128)(2,1)S(1)}, bf16[256,256]{1,0:T(8,128)(2,1)}, u32[]{:S(2)}) copy-start(bf16[256,256]{1,0:T(8,128)(2,1)} %constant.24.clone.refs_2_) | copy-start | bytes 393220
  27.2 11.7 %copy-start.2 = (bf16[256,256]{1,0:T(8,128)(2,1)S(1)}, bf16[256,256]{1,0:T(8,128)(2,1)}, u32[]{:S(2)}) copy-start(bf16[256,256]{1,0:T(8,128)(2,1)} %constant.23.clone.refs_1_) | copy-start | bytes 393220
  27.2 11.7 %copy-start.3 = (bf16[256,256]{1,0:T(8,128)(2,1)S(1)}, bf16[256,256]{1,0:T(8,128)(2,1)}, u32[]{:S(2)}) copy-start(bf16[256,256]{1,0:T(8,128)(2,1)} %constant.22.clone.refs_0_) | copy-start | bytes 393220
  28.0 6.7 %collective-permute-start.10 = (f32[2,16,8,128]{3,2,1,0:T(8,128)S(1)}, f32[2,16,8,128]{3,2,1,0:T(8,128)S(1)}, u32[]{:S(2)}, u32[]{:S(2)}) collective-permute-start(f32[2,16,8,128]{3,2,1,0:T(8,128)S(1)} %get-tuple-element.66), channel_id=1, source_target_pairs={{0,6},{1,7},{2,4},{3,5},{4,2},{5,3},{6,0},{7,1},{8,14},{9,15},{10,... | collective-permute-start | bytes 393224 | tf_op jit(solution)/shard_map/ppermute | solution.py:390
  29.2 9.7 %collective-permute-start.11 = (f32[2,16,8,128]{3,2,1,0:T(8,128)S(1)}, f32[2,16,8,128]{3,2,1,0:T(8,128)S(1)}, u32[]{:S(2)}, u32[]{:S(2)}) collective-permute-start(f32[2,16,8,128]{3,2,1,0:T(8,128)S(1)} %get-tuple-element.67), channel_id=1, source_target_pairs={{0,4},{1,5},{2,6},{3,7},{4,0},{5,1},{6,2},{7,3},{8,12},{9,13},{10,... | collective-permute-start | bytes 393224 | tf_op jit(solution)/shard_map/ppermute | solution.py:390
  31.0 7.8 %collective-permute-start.12 = (f32[2,16,8,128]{3,2,1,0:T(8,128)S(1)}, f32[2,16,8,128]{3,2,1,0:T(8,128)S(1)}, u32[]{:S(2)}, u32[]{:S(2)}) collective-permute-start(f32[2,16,8,128]{3,2,1,0:T(8,128)S(1)} %get-tuple-element.68), channel_id=1, source_target_pairs={{0,2},{1,3},{2,0},{3,1},{4,6},{5,7},{6,4},{7,5},{8,10},{9,11},{10,... | collective-permute-start | bytes 393224 | tf_op jit(solution)/shard_map/ppermute | solution.py:390
  31.6 7.9 %collective-permute-start.13 = (f32[2,16,8,128]{3,2,1,0:T(8,128)S(1)}, f32[2,16,8,128]{3,2,1,0:T(8,128)S(1)}, u32[]{:S(2)}, u32[]{:S(2)}) collective-permute-start(f32[2,16,8,128]{3,2,1,0:T(8,128)S(1)} %get-tuple-element.69), channel_id=1, source_target_pairs={{0,7},{1,6},{2,5},{3,4},{4,3},{5,2},{6,1},{7,0},{8,15},{9,14},{10,... | collective-permute-start | bytes 393224 | tf_op jit(solution)/shard_map/ppermute | solution.py:390
  31.6 9.6 %collective-permute-start.14 = (f32[2,16,8,128]{3,2,1,0:T(8,128)S(1)}, f32[2,16,8,128]{3,2,1,0:T(8,128)S(1)}, u32[]{:S(2)}, u32[]{:S(2)}) collective-permute-start(f32[2,16,8,128]{3,2,1,0:T(8,128)S(1)} %get-tuple-element.70), channel_id=1, source_target_pairs={{0,5},{1,4},{2,7},{3,6},{4,1},{5,0},{6,3},{7,2},{8,13},{9,12},{10,... | collective-permute-start | bytes 393224 | tf_op jit(solution)/shard_map/ppermute | solution.py:390
  34.7 6.5 %collective-permute-start.15 = (f32[2,16,8,128]{3,2,1,0:T(8,128)S(1)}, f32[2,16,8,128]{3,2,1,0:T(8,128)S(1)}, u32[]{:S(2)}, u32[]{:S(2)}) collective-permute-start(f32[2,16,8,128]{3,2,1,0:T(8,128)S(1)} %get-tuple-element.71), channel_id=1, source_target_pairs={{0,3},{1,2},{2,1},{3,0},{4,7},{5,6},{6,5},{7,4},{8,11},{9,10},{10,... | collective-permute-start | bytes 393224 | tf_op jit(solution)/shard_map/ppermute | solution.py:390
  38.9 2.3 %collective-permute-start.16 = (f32[2,16,8,128]{3,2,1,0:T(8,128)S(1)}, f32[2,16,8,128]{3,2,1,0:T(8,128)S(1)}, u32[]{:S(2)}, u32[]{:S(2)}) collective-permute-start(f32[2,16,8,128]{3,2,1,0:T(8,128)S(1)} %get-tuple-element.72), channel_id=1, source_target_pairs={{0,1},{1,0},{2,3},{3,2},{4,5},{5,4},{6,7},{7,6},{8,9},{9,8},{10,11... | collective-permute-start | bytes 393224 | tf_op jit(solution)/shard_map/ppermute | solution.py:390

commit v5 on v4

--- a/solution.py
+++ b/solution.py
@@ -524,15 +524,15 @@
         for i, j in enumerate(order):
             modes[(g // 2) ^ j] = ins[i][...]
         dims = ((1,), (0,))
-        parts = [modes[chunk].reshape(depth * local_x, lanes) for chunk in range(chunks)]
-        low = dot3(jnp.concatenate(parts[: chunks // 2], axis=1), eh[...], el[...], dims)
-        high = dot3(jnp.concatenate(parts[chunks // 2 :], axis=1), oh[...], ol[...], dims)
-        for side, value in enumerate((low + high, low - high)):
-            for layer in range(depth):
+        for layer in range(depth):
+            parts = [modes[chunk, layer].reshape(local_x, lanes) for chunk in range(chunks)]
+            low = dot3(jnp.concatenate(parts[: chunks // 2], axis=1), eh[...], el[...], dims)
+            high = dot3(jnp.concatenate(parts[chunks // 2 :], axis=1), oh[...], ol[...], dims)
+            for side, value in enumerate((low + high, low - high)):
                 for col in range(tiles // 2):
                     t = side * (tiles // 2) + col
                     for xi in range(steps):
-                        at = (layer * steps + xi) * SUB
+                        at = xi * SUB
                         buf[layer, t, pl.ds(xi, SUB, stride=steps), :] = value[
                             at : at + SUB, col * LANES : (col + 1) * LANES
                         ]

time: 42.6 us -> 42.6 us (level)
  no operation moved by 1% of the time
where the time goes in v5:
time: 42.6 us; the launch traced here: 42.5 us
  starting transfers between devices  18.7 us (44%)
  waiting for transfers between devices  17.3 us (41%)
  Pallas kernels  6.37 us (15%)
    ppermute x17, starting transfers between devices, exchange(): out.append(lax.ppermute(arrays[k], axis, route) if k else arrays[k])  18.7 us
    ppermute x17, waiting for transfers between devices, exchange(): out.append(lax.ppermute(arrays[k], axis, route) if k else arrays[k])  17.3 us
    pallas_call x1, Pallas kernels, on_device_fn(): pl.pallas_call(first_kernel, in_specs=[hbm] * 9, out_specs=[vmem] * (chun...  2.27 us
    pallas_call x1, Pallas kernels, on_device_fn(): pl.pallas_call(other_kernel, in_specs=[vmem] * (5 + chunks), out_specs=hb...  1.31 us
  transfers between devices with their start and end apart: 17, of which 8 were waited for; matrix products, arithmetic and copies ran while one was open for 0% of the time, Pallas kernels for 3%

profile of v5, /device:TPU:0, one launch (start us, length us, event | category | flops | bytes accessed | tf_op | source)
XLA Modules:
  0.0 42.5 jit_solution(3302143395629750325)
XLA Ops:
  0.0 2.3 %sources_own.1 = (f32[2,16,8,128]{3,2,1,0:T(8,128)S(1)}, f32[2,16,8,128]{3,2,1,0:T(8,128)S(1)}, f32[2,16,8,128]{3,2,1,0:T(8,128)S(1)}, f32[2,16,8,128]{3,2,1,0:T...) custom-call(f32[2,32]{1,0:T(2,128)} %bitcast.1, ...), custom_call_target="tpu_custom_call" | custom-call | tf_op jit(solution)/shard_map/sources_own/pallas_call | solution.py:347
  2.3 3.9 %collective-permute-start = (f32[2,16,8,128]{3,2,1,0:T(8,128)S(1)}, f32[2,16,8,128]{3,2,1,0:T(8,128)S(1)}, u32[]{:S(2)}, u32[]{:S(2)}) collective-permute-start(f32[2,16,8,128]{3,2,1,0:T(8,128)S(1)} %get-tuple-element.45), channel_id=1, source_target_pairs={{0,6},{1,7},{2,4},{3,5},{4,2},{5,3},{6,0},{7,1},{8,14},{9,15},{10,... | collective-permute-start | bytes 393224 | tf_op jit(solution)/shard_map/ppermute | solution.py:390
  6.2 0.5 %collective-permute-start.1 = (f32[2,16,8,128]{3,2,1,0:T(8,128)S(1)}, f32[2,16,8,128]{3,2,1,0:T(8,128)S(1)}, u32[]{:S(2)}, u32[]{:S(2)}) collective-permute-start(f32[2,16,8,128]{3,2,1,0:T(8,128)S(1)} %get-tuple-element.46), channel_id=1, source_target_pairs={{0,4},{1,5},{2,6},{3,7},{4,0},{5,1},{6,2},{7,3},{8,12},{9,13},{10,... | collective-permute-start | bytes 393224 | tf_op jit(solution)/shard_map/ppermute | solution.py:390
  6.8 0.7 %sources_other.1 = (f32[2,16,8,128]{3,2,1,0:T(8,128)S(1)}, f32[2,16,8,128]{3,2,1,0:T(8,128)S(1)}, f32[2,16,8,128]{3,2,1,0:T(8,128)S(1)}, f32[2,16,8,128]{3,2,1,0:T(8,128)S(1)}) custom-call(f32[2,4,2,128,128]{4,3,2,1,0:T(8,128)S(1)} %get-tuple-element.48.f_buf, f32[2,1,4,2,8,128]{5,4,3,2,1,0:T(8,128)S(1)} %get-tuple-element.49.rate_buf, ...), custom_call_target="tpu_custom_call" | custom-call | flops 8000000000 | bytes 24000000 | tf_op jit(solution)/shard_map/sources_other/pallas_call | solution.py:372
  7.6 1.5 %collective-permute-start.3 = (f32[2,16,8,128]{3,2,1,0:T(8,128)S(1)}, f32[2,16,8,128]{3,2,1,0:T(8,128)S(1)}, u32[]{:S(2)}, u32[]{:S(2)}) collective-permute-start(f32[2,16,8,128]{3,2,1,0:T(8,128)S(1)} %get-tuple-element.55), channel_id=1, source_target_pairs={{0,7},{1,6},{2,5},{3,4},{4,3},{5,2},{6,1},{7,0},{8,15},{9,14},{10,... | collective-permute-start | bytes 393224 | tf_op jit(solution)/shard_map/ppermute | solution.py:390
  9.1 1.6 %collective-permute-start.4 = (f32[2,16,8,128]{3,2,1,0:T(8,128)S(1)}, f32[2,16,8,128]{3,2,1,0:T(8,128)S(1)}, u32[]{:S(2)}, u32[]{:S(2)}) collective-permute-start(f32[2,16,8,128]{3,2,1,0:T(8,128)S(1)} %get-tuple-element.56), channel_id=1, source_target_pairs={{0,5},{1,4},{2,7},{3,6},{4,1},{5,0},{6,3},{7,2},{8,13},{9,12},{10,... | collective-permute-start | bytes 393224 | tf_op jit(solution)/shard_map/ppermute | solution.py:390
  10.8 2.8 %collective-permute-done.1.rest_2_ = f32[2,16,8,128]{3,2,1,0:T(8,128)S(1)} collective-permute-done((f32[2,16,8,128]{3,2,1,0:T(8,128)S(1)}, f32[2,16,8,128]{3,2,1,0:T(8,128)S(1)}, u32[]{:S(2)}, u32[]{:S(2)}) %collective-permute-start.1) | collective-permute-done | bytes 131104 | tf_op jit(solution)/shard_map/ppermute | solution.py:390
  13.7 1.7 %collective-permute-done.3.rest_4_ = f32[2,16,8,128]{3,2,1,0:T(8,128)S(1)} collective-permute-done((f32[2,16,8,128]{3,2,1,0:T(8,128)S(1)}, f32[2,16,8,128]{3,2,1,0:T(8,128)S(1)}, u32[]{:S(2)}, u32[]{:S(2)}) %collective-permute-start.3) | collective-permute-done | bytes 131104 | tf_op jit(solution)/shard_map/ppermute | solution.py:390
  15.4 2.5 %collective-permute-done.4.rest_5_ = f32[2,16,8,128]{3,2,1,0:T(8,128)S(1)} collective-permute-done((f32[2,16,8,128]{3,2,1,0:T(8,128)S(1)}, f32[2,16,8,128]{3,2,1,0:T(8,128)S(1)}, u32[]{:S(2)}, u32[]{:S(2)}) %collective-permute-start.4) | collective-permute-done | bytes 131104 | tf_op jit(solution)/shard_map/ppermute | solution.py:390
  17.9 0.7 %gather.1 = (f32[16,16,8,128]{3,2,1,0:T(8,128)S(1)}, f32[16,8,128]{2,1,0:T(8,128)S(1)}, f32[16,8,128]{2,1,0:T(8,128)S(1)}, f32[2,16,128]{2,1,0:T(8,128)S(1)}) custom-call(f32[16,8,128]{2,1,0:T(8,128)S(1)} %get-tuple-element.39.decay_ref, f32[16,8,128]{2,1,0:T(8,128)S(1)} %get-tuple-element.41.up_ref, f32[16,8,128]{2,1,0:T(8,128)S(1)} %get-tuple-element.42.down_ref, ...), custom_call_target="tpu_custom_call" | custom-call | tf_op jit(solution)/shard_map/gather/pallas_call | solution.py:426
  18.6 4.0 %collective-permute-start.9 = (f32[2,16,128]{2,1,0:T(8,128)S(1)}, f32[2,16,128]{2,1,0:T(8,128)S(1)}, u32[]{:S(2)}, u32[]{:S(2)}) collective-permute-start(f32[2,16,128]{2,1,0:T(8,128)S(1)} %get-tuple-element.64.rest_0_), channel_id=1, source_target_pairs={{0,24},{8,16},{16,8},{24,0},{1,25},{9,17},{17,9},{25,1},{2,26},{10... | collective-permute-start | bytes 49160 | tf_op jit(solution)/shard_map/ppermute | solution.py:390
  22.6 0.6 %collective-permute-start.7 = (f32[2,16,128]{2,1,0:T(8,128)S(1)}, f32[2,16,128]{2,1,0:T(8,128)S(1)}, u32[]{:S(2)}, u32[]{:S(2)}) collective-permute-start(f32[2,16,128]{2,1,0:T(8,128)S(1)} %get-tuple-element.64.rest_0_), channel_id=1, source_target_pairs={{0,8},{8,0},{16,24},{24,16},{1,9},{9,1},{17,25},{25,17},{2,10},{10... | collective-permute-start | bytes 49160 | tf_op jit(solution)/shard_map/ppermute | solution.py:390
  23.3 1.0 %collective-permute-done.9.rest_3_ = f32[2,16,128]{2,1,0:T(8,128)S(1)} collective-permute-done((f32[2,16,128]{2,1,0:T(8,128)S(1)}, f32[2,16,128]{2,1,0:T(8,128)S(1)}, u32[]{:S(2)}, u32[]{:S(2)}) %collective-permute-start.9) | collective-permute-done | bytes 16416 | tf_op jit(solution)/shard_map/ppermute | solution.py:390
  24.3 2.9 %collective-permute-done.8.rest_2_ = f32[2,16,128]{2,1,0:T(8,128)S(1)} collective-permute-done((f32[2,16,128]{2,1,0:T(8,128)S(1)}, f32[2,16,128]{2,1,0:T(8,128)S(1)}, u32[]{:S(2)}, u32[]{:S(2)}) %collective-permute-start.8) | collective-permute-done | bytes 16416 | tf_op jit(solution)/shard_map/ppermute | solution.py:390
  27.2 0.8 %solve.1 = (f32[2,16,8,128]{3,2,1,0:T(8,128)S(1)}, f32[2,16,8,128]{3,2,1,0:T(8,128)S(1)}, f32[2,16,8,128]{3,2,1,0:T(8,128)S(1)}, f32[2,16,8,128]{3,2,1,0:T(8,128...) custom-call(f32[16,8,128]{2,1,0:T(8,128)S(1)} %get-tuple-element.39., ...), custom_call_target="tpu_custom_call" | custom-call | tf_op jit(solution)/shard_map/solve/pallas_call | solution.py:505
  28.0 1.2 %collective-permute-start.10 = (f32[2,16,8,128]{3,2,1,0:T(8,128)S(1)}, f32[2,16,8,128]{3,2,1,0:T(8,128)S(1)}, u32[]{:S(2)}, u32[]{:S(2)}) collective-permute-start(f32[2,16,8,128]{3,2,1,0:T(8,128)S(1)} %get-tuple-element.66), channel_id=1, source_target_pairs={{0,6},{1,7},{2,4},{3,5},{4,2},{5,3},{6,0},{7,1},{8,14},{9,15},{10,... | collective-permute-start | bytes 393224 | tf_op jit(solution)/shard_map/ppermute | solution.py:390
  29.2 1.9 %collective-permute-start.11 = (f32[2,16,8,128]{3,2,1,0:T(8,128)S(1)}, f32[2,16,8,128]{3,2,1,0:T(8,128)S(1)}, u32[]{:S(2)}, u32[]{:S(2)}) collective-permute-start(f32[2,16,8,128]{3,2,1,0:T(8,128)S(1)} %get-tuple-element.67), channel_id=1, source_target_pairs={{0,4},{1,5},{2,6},{3,7},{4,0},{5,1},{6,2},{7,3},{8,12},{9,13},{10,... | collective-permute-start | bytes 393224 | tf_op jit(solution)/shard_map/ppermute | solution.py:390
  31.0 0.5 %collective-permute-start.12 = (f32[2,16,8,128]{3,2,1,0:T(8,128)S(1)}, f32[2,16,8,128]{3,2,1,0:T(8,128)S(1)}, u32[]{:S(2)}, u32[]{:S(2)}) collective-permute-start(f32[2,16,8,128]{3,2,1,0:T(8,128)S(1)} %get-tuple-element.68), channel_id=1, source_target_pairs={{0,2},{1,3},{2,0},{3,1},{4,6},{5,7},{6,4},{7,5},{8,10},{9,11},{10,... | collective-permute-start | bytes 393224 | tf_op jit(solution)/shard_map/ppermute | solution.py:390
  31.6 2.7 %collective-permute-start.14 = (f32[2,16,8,128]{3,2,1,0:T(8,128)S(1)}, f32[2,16,8,128]{3,2,1,0:T(8,128)S(1)}, u32[]{:S(2)}, u32[]{:S(2)}) collective-permute-start(f32[2,16,8,128]{3,2,1,0:T(8,128)S(1)} %get-tuple-element.70), channel_id=1, source_target_pairs={{0,5},{1,4},{2,7},{3,6},{4,1},{5,0},{6,3},{7,2},{8,13},{9,12},{10,... | collective-permute-start | bytes 393224 | tf_op jit(solution)/shard_map/ppermute | solution.py:390
  34.2 0.4 %collective-permute-done.10.refs_5_ = f32[2,16,8,128]{3,2,1,0:T(8,128)S(1)} collective-permute-done((f32[2,16,8,128]{3,2,1,0:T(8,128)S(1)}, f32[2,16,8,128]{3,2,1,0:T(8,128)S(1)}, u32[]{:S(2)}, u32[]{:S(2)}) %collective-permute-start.10) | collective-permute-done | bytes 131104 | tf_op jit(solution)/shard_map/ppermute | solution.py:390
  34.7 4.2 %collective-permute-done.11.refs_6_ = f32[2,16,8,128]{3,2,1,0:T(8,128)S(1)} collective-permute-done((f32[2,16,8,128]{3,2,1,0:T(8,128)S(1)}, f32[2,16,8,128]{3,2,1,0:T(8,128)S(1)}, u32[]{:S(2)}, u32[]{:S(2)}) %collective-permute-start.11) | collective-permute-done | bytes 131104 | tf_op jit(solution)/shard_map/ppermute | solution.py:390
  38.9 0.5 %finish_own.1.own_buf = f32[2,4,128,128]{3,2,1,0:T(8,128)S(1)} custom-call(bf16[256,256]{1,0:T(8,128)(2,1)S(1)} %copy-done.3, bf16[256,256]{1,0:T(8,128)(2,1)S(1)} %copy-done.2, bf16[256,256]{1,0:T(8,128)(2,1)S(1)} %copy-done.1, bf16[256,256]{1,0:T(8,128)(2,1)S(1)} %copy-done, f32[2,16,8,128]{3,2,1,0:T(8,128)S(1)} %get-tuple-element.65.refs_4_, ...), custom_call_target="tpu_custom_call" | custom-call | flops 8000000000 | bytes 24000000 | tf_op jit(solution)/shard_map/finish_own/pallas_call | solution.py:575
  39.4 1.8 %collective-permute-done.14.refs_5_ = f32[2,16,8,128]{3,2,1,0:T(8,128)S(1)} collective-permute-done((f32[2,16,8,128]{3,2,1,0:T(8,128)S(1)}, f32[2,16,8,128]{3,2,1,0:T(8,128)S(1)}, u32[]{:S(2)}, u32[]{:S(2)}) %collective-permute-start.14) | collective-permute-done | bytes 131104 | tf_op jit(solution)/shard_map/ppermute | solution.py:390
  41.2 1.3 %finish_other.1 = f32[2,2,128,512]{3,2,1,0:T(8,128)} custom-call(f32[2,4,128,128]{3,2,1,0:T(8,128)S(1)} %finish_own.1.own_buf, bf16[256,256]{1,0:T(8,128)(2,1)S(1)} %copy-done.3, bf16[256,256]{1,0:T(8,128)(2,1)S(1)} %copy-done.2, bf16[256,256]{1,0:T(8,128)(2,1)S(1)} %copy-done.1, bf16[256,256]{1,0:T(8,128)(2,1)S(1)} %copy-done, ...), custom_call_target="tpu_custom_call" | custom-call | tf_op jit(solution)/shard_map/finish_other/pallas_call | solution.py:586
  (25 shorter events, 0.4 us)
Async XLA Ops:
  2.3 8.4 %collective-permute-start = (f32[2,16,8,128]{3,2,1,0:T(8,128)S(1)}, f32[2,16,8,128]{3,2,1,0:T(8,128)S(1)}, u32[]{:S(2)}, u32[]{:S(2)}) collective-permute-start(f32[2,16,8,128]{3,2,1,0:T(8,128)S(1)} %get-tuple-element.45), channel_id=1, source_target_pairs={{0,6},{1,7},{2,4},{3,5},{4,2},{5,3},{6,0},{7,1},{8,14},{9,15},{10,... | collective-permute-start | bytes 393224 | tf_op jit(solution)/shard_map/ppermute | solution.py:390
  6.2 7.5 %collective-permute-start.1 = (f32[2,16,8,128]{3,2,1,0:T(8,128)S(1)}, f32[2,16,8,128]{3,2,1,0:T(8,128)S(1)}, u32[]{:S(2)}, u32[]{:S(2)}) collective-permute-start(f32[2,16,8,128]{3,2,1,0:T(8,128)S(1)} %get-tuple-element.46), channel_id=1, source_target_pairs={{0,4},{1,5},{2,6},{3,7},{4,0},{5,1},{6,2},{7,3},{8,12},{9,13},{10,... | collective-permute-start | bytes 393224 | tf_op jit(solution)/shard_map/ppermute | solution.py:390
  6.7 7.0 %collective-permute-start.2 = (f32[2,16,8,128]{3,2,1,0:T(8,128)S(1)}, f32[2,16,8,128]{3,2,1,0:T(8,128)S(1)}, u32[]{:S(2)}, u32[]{:S(2)}) collective-permute-start(f32[2,16,8,128]{3,2,1,0:T(8,128)S(1)} %get-tuple-element.47), channel_id=1, source_target_pairs={{0,2},{1,3},{2,0},{3,1},{4,6},{5,7},{6,4},{7,5},{8,10},{9,11},{10,... | collective-permute-start | bytes 393224 | tf_op jit(solution)/shard_map/ppermute | solution.py:390
  7.6 7.8 %collective-permute-start.3 = (f32[2,16,8,128]{3,2,1,0:T(8,128)S(1)}, f32[2,16,8,128]{3,2,1,0:T(8,128)S(1)}, u32[]{:S(2)}, u32[]{:S(2)}) collective-permute-start(f32[2,16,8,128]{3,2,1,0:T(8,128)S(1)} %get-tuple-element.55), channel_id=1, source_target_pairs={{0,7},{1,6},{2,5},{3,4},{4,3},{5,2},{6,1},{7,0},{8,15},{9,14},{10,... | collective-permute-start | bytes 393224 | tf_op jit(solution)/shard_map/ppermute | solution.py:390
  9.1 8.8 %collective-permute-start.4 = (f32[2,16,8,128]{3,2,1,0:T(8,128)S(1)}, f32[2,16,8,128]{3,2,1,0:T(8,128)S(1)}, u32[]{:S(2)}, u32[]{:S(2)}) collective-permute-start(f32[2,16,8,128]{3,2,1,0:T(8,128)S(1)} %get-tuple-element.56), channel_id=1, source_target_pairs={{0,5},{1,4},{2,7},{3,6},{4,1},{5,0},{6,3},{7,2},{8,13},{9,12},{10,... | collective-permute-start | bytes 393224 | tf_op jit(solution)/shard_map/ppermute | solution.py:390
  10.7 7.2 %collective-permute-start.5 = (f32[2,16,8,128]{3,2,1,0:T(8,128)S(1)}, f32[2,16,8,128]{3,2,1,0:T(8,128)S(1)}, u32[]{:S(2)}, u32[]{:S(2)}) collective-permute-start(f32[2,16,8,128]{3,2,1,0:T(8,128)S(1)} %get-tuple-element.57), channel_id=1, source_target_pairs={{0,3},{1,2},{2,1},{3,0},{4,7},{5,6},{6,5},{7,4},{8,11},{9,10},{10,... | collective-permute-start | bytes 393224 | tf_op jit(solution)/shard_map/ppermute | solution.py:390
  13.7 4.2 %collective-permute-start.6 = (f32[2,16,8,128]{3,2,1,0:T(8,128)S(1)}, f32[2,16,8,128]{3,2,1,0:T(8,128)S(1)}, u32[]{:S(2)}, u32[]{:S(2)}) collective-permute-start(f32[2,16,8,128]{3,2,1,0:T(8,128)S(1)} %get-tuple-element.58), channel_id=1, source_target_pairs={{0,1},{1,0},{2,3},{3,2},{4,5},{5,4},{6,7},{7,6},{8,9},{9,8},{10,11... | collective-permute-start | bytes 393224 | tf_op jit(solution)/shard_map/ppermute | solution.py:390
  18.6 5.7 %collective-permute-start.9 = (f32[2,16,128]{2,1,0:T(8,128)S(1)}, f32[2,16,128]{2,1,0:T(8,128)S(1)}, u32[]{:S(2)}, u32[]{:S(2)}) collective-permute-start(f32[2,16,128]{2,1,0:T(8,128)S(1)} %get-tuple-element.64.rest_0_), channel_id=1, source_target_pairs={{0,24},{8,16},{16,8},{24,0},{1,25},{9,17},{17,9},{25,1},{2,26},{10... | collective-permute-start | bytes 49160 | tf_op jit(solution)/shard_map/ppermute | solution.py:390
  22.6 4.6 %collective-permute-start.8 = (f32[2,16,128]{2,1,0:T(8,128)S(1)}, f32[2,16,128]{2,1,0:T(8,128)S(1)}, u32[]{:S(2)}, u32[]{:S(2)}) collective-permute-start(f32[2,16,128]{2,1,0:T(8,128)S(1)} %get-tuple-element.64.rest_0_), channel_id=1, source_target_pairs={{0,16},{8,24},{16,0},{24,8},{1,17},{9,25},{17,1},{25,9},{2,18},{10... | collective-permute-start | bytes 49160 | tf_op jit(solution)/shard_map/ppermute | solution.py:390
  22.6 4.6 %collective-permute-start.7 = (f32[2,16,128]{2,1,0:T(8,128)S(1)}, f32[2,16,128]{2,1,0:T(8,128)S(1)}, u32[]{:S(2)}, u32[]{:S(2)}) collective-permute-start(f32[2,16,128]{2,1,0:T(8,128)S(1)} %get-tuple-element.64.rest_0_), channel_id=1, source_target_pairs={{0,8},{8,0},{16,24},{24,16},{1,9},{9,1},{17,25},{25,17},{2,10},{10... | collective-permute-start | bytes 49160 | tf_op jit(solution)/shard_map/ppermute | solution.py:390
  27.2 11.7 %copy-start = (bf16[256,256]{1,0:T(8,128)(2,1)S(1)}, bf16[256,256]{1,0:T(8,128)(2,1)}, u32[]{:S(2)}) copy-start(bf16[256,256]{1,0:T(8,128)(2,1)} %constant.25.clone.refs_3_) | copy-start | bytes 393220
  27.2 11.7 %copy-start.1 = (bf16[256,256]{1,0:T(8,128)(2,1)S(1)}, bf16[256,256]{1,0:T(8,128)(2,1)}, u32[]{:S(2)}) copy-start(bf16[256,256]{1,0:T(8,128)(2,1)} %constant.24.clone.refs_2_) | copy-start | bytes 393220
  27.2 11.7 %copy-start.2 = (bf16[256,256]{1,0:T(8,128)(2,1)S(1)}, bf16[256,256]{1,0:T(8,128)(2,1)}, u32[]{:S(2)}) copy-start(bf16[256,256]{1,0:T(8,128)(2,1)} %constant.23.clone.refs_1_) | copy-start | bytes 393220
  27.2 11.7 %copy-start.3 = (bf16[256,256]{1,0:T(8,128)(2,1)S(1)}, bf16[256,256]{1,0:T(8,128)(2,1)}, u32[]{:S(2)}) copy-start(bf16[256,256]{1,0:T(8,128)(2,1)} %constant.22.clone.refs_0_) | copy-start | bytes 393220
  28.0 6.7 %collective-permute-start.10 = (f32[2,16,8,128]{3,2,1,0:T(8,128)S(1)}, f32[2,16,8,128]{3,2,1,0:T(8,128)S(1)}, u32[]{:S(2)}, u32[]{:S(2)}) collective-permute-start(f32[2,16,8,128]{3,2,1,0:T(8,128)S(1)} %get-tuple-element.66), channel_id=1, source_target_pairs={{0,6},{1,7},{2,4},{3,5},{4,2},{5,3},{6,0},{7,1},{8,14},{9,15},{10,... | collective-permute-start | bytes 393224 | tf_op jit(solution)/shard_map/ppermute | solution.py:390
  29.2 9.7 %collective-permute-start.11 = (f32[2,16,8,128]{3,2,1,0:T(8,128)S(1)}, f32[2,16,8,128]{3,2,1,0:T(8,128)S(1)}, u32[]{:S(2)}, u32[]{:S(2)}) collective-permute-start(f32[2,16,8,128]{3,2,1,0:T(8,128)S(1)} %get-tuple-element.67), channel_id=1, source_target_pairs={{0,4},{1,5},{2,6},{3,7},{4,0},{5,1},{6,2},{7,3},{8,12},{9,13},{10,... | collective-permute-start | bytes 393224 | tf_op jit(solution)/shard_map/ppermute | solution.py:390
  31.0 7.8 %collective-permute-start.12 = (f32[2,16,8,128]{3,2,1,0:T(8,128)S(1)}, f32[2,16,8,128]{3,2,1,0:T(8,128)S(1)}, u32[]{:S(2)}, u32[]{:S(2)}) collective-permute-start(f32[2,16,8,128]{3,2,1,0:T(8,128)S(1)} %get-tuple-element.68), channel_id=1, source_target_pairs={{0,2},{1,3},{2,0},{3,1},{4,6},{5,7},{6,4},{7,5},{8,10},{9,11},{10,... | collective-permute-start | bytes 393224 | tf_op jit(solution)/shard_map/ppermute | solution.py:390
  31.6 7.8 %collective-permute-start.13 = (f32[2,16,8,128]{3,2,1,0:T(8,128)S(1)}, f32[2,16,8,128]{3,2,1,0:T(8,128)S(1)}, u32[]{:S(2)}, u32[]{:S(2)}) collective-permute-start(f32[2,16,8,128]{3,2,1,0:T(8,128)S(1)} %get-tuple-element.69), channel_id=1, source_target_pairs={{0,7},{1,6},{2,5},{3,4},{4,3},{5,2},{6,1},{7,0},{8,15},{9,14},{10,... | collective-permute-start | bytes 393224 | tf_op jit(solution)/shard_map/ppermute | solution.py:390
  31.6 9.6 %collective-permute-start.14 = (f32[2,16,8,128]{3,2,1,0:T(8,128)S(1)}, f32[2,16,8,128]{3,2,1,0:T(8,128)S(1)}, u32[]{:S(2)}, u32[]{:S(2)}) collective-permute-start(f32[2,16,8,128]{3,2,1,0:T(8,128)S(1)} %get-tuple-element.70), channel_id=1, source_target_pairs={{0,5},{1,4},{2,7},{3,6},{4,1},{5,0},{6,3},{7,2},{8,13},{9,12},{10,... | collective-permute-start | bytes 393224 | tf_op jit(solution)/shard_map/ppermute | solution.py:390
  34.7 6.5 %collective-permute-start.15 = (f32[2,16,8,128]{3,2,1,0:T(8,128)S(1)}, f32[2,16,8,128]{3,2,1,0:T(8,128)S(1)}, u32[]{:S(2)}, u32[]{:S(2)}) collective-permute-start(f32[2,16,8,128]{3,2,1,0:T(8,128)S(1)} %get-tuple-element.71), channel_id=1, source_target_pairs={{0,3},{1,2},{2,1},{3,0},{4,7},{5,6},{6,5},{7,4},{8,11},{9,10},{10,... | collective-permute-start | bytes 393224 | tf_op jit(solution)/shard_map/ppermute | solution.py:390
  38.9 2.3 %collective-permute-start.16 = (f32[2,16,8,128]{3,2,1,0:T(8,128)S(1)}, f32[2,16,8,128]{3,2,1,0:T(8,128)S(1)}, u32[]{:S(2)}, u32[]{:S(2)}) collective-permute-start(f32[2,16,8,128]{3,2,1,0:T(8,128)S(1)} %get-tuple-element.72), channel_id=1, source_target_pairs={{0,1},{1,0},{2,3},{3,2},{4,5},{5,4},{6,7},{7,6},{8,9},{9,8},{10,11... | collective-permute-start | bytes 393224 | tf_op jit(solution)/shard_map/ppermute | solution.py:390

commit v6 on v4

--- a/solution.py
+++ b/solution.py
@@ -390,7 +390,7 @@
             out.append(lax.ppermute(arrays[k], axis, route) if k else arrays[k])
         return out
 
-    order_own = [0] + list(range(1, chunks))[::-1]
+    order_own = [0, chunks - 1] + list(range(1, chunks - 1))
     order_other = list(range(chunks))[::-1]
     order_z = [2 * j for j in order_own] + [2 * j + 1 for j in order_other]
     order_x = list(range(devices_x))

time: 42.6 us -> 42.5 us (level)
  transfers between devices with their start and end apart: 17 -> 17, of which waited for: 8 -> 11; matrix products, arithmetic and copies ran while one was open for 0% -> 0% of each run, Pallas kernels for 3% -> 3%
where the time goes in v6:
time: 42.5 us; the launch traced here: 42.3 us
  starting transfers between devices  18.5 us (44%)
  waiting for transfers between devices  17.4 us (41%)
  Pallas kernels  6.4 us (15%)
    ppermute x17, starting transfers between devices, exchange(): out.append(lax.ppermute(arrays[k], axis, route) if k else arrays[k])  18.5 us
    ppermute x17, waiting for transfers between devices, exchange(): out.append(lax.ppermute(arrays[k], axis, route) if k else arrays[k])  17.4 us
    pallas_call x1, Pallas kernels, on_device_fn(): pl.pallas_call(first_kernel, in_specs=[hbm] * 9, out_specs=[vmem] * (chun...  2.27 us
    pallas_call x1, Pallas kernels, on_device_fn(): pl.pallas_call(other_kernel, in_specs=[vmem] * (5 + chunks), out_specs=hb...  1.28 us
  transfers between devices with their start and end apart: 17, of which 11 were waited for; matrix products, arithmetic and copies ran while one was open for 0% of the time, Pallas kernels for 3%

profile of v6, /device:TPU:0, one launch (start us, length us, event | category | flops | bytes accessed | tf_op | source)
XLA Modules:
  0.0 42.3 jit_solution(17838758533975648559)
XLA Ops:
  0.0 2.3 %sources_own.1 = (f32[2,16,8,128]{3,2,1,0:T(8,128)S(1)}, f32[2,16,8,128]{3,2,1,0:T(8,128)S(1)}, f32[2,16,8,128]{3,2,1,0:T(8,128)S(1)}, f32[2,16,8,128]{3,2,1,0:T...) custom-call(f32[2,32]{1,0:T(2,128)} %bitcast.1, ...), custom_call_target="tpu_custom_call" | custom-call | tf_op jit(solution)/shard_map/sources_own/pallas_call | solution.py:347
  2.3 3.9 %collective-permute-start = (f32[2,16,8,128]{3,2,1,0:T(8,128)S(1)}, f32[2,16,8,128]{3,2,1,0:T(8,128)S(1)}, u32[]{:S(2)}, u32[]{:S(2)}) collective-permute-start(f32[2,16,8,128]{3,2,1,0:T(8,128)S(1)} %get-tuple-element.45), channel_id=1, source_target_pairs={{0,6},{1,7},{2,4},{3,5},{4,2},{5,3},{6,0},{7,1},{8,14},{9,15},{10,... | collective-permute-start | bytes 393224 | tf_op jit(solution)/shard_map/ppermute | solution.py:390
  6.2 0.5 %collective-permute-start.1 = (f32[2,16,8,128]{3,2,1,0:T(8,128)S(1)}, f32[2,16,8,128]{3,2,1,0:T(8,128)S(1)}, u32[]{:S(2)}, u32[]{:S(2)}) collective-permute-start(f32[2,16,8,128]{3,2,1,0:T(8,128)S(1)} %get-tuple-element.46), channel_id=1, source_target_pairs={{0,2},{1,3},{2,0},{3,1},{4,6},{5,7},{6,4},{7,5},{8,10},{9,11},{10,... | collective-permute-start | bytes 393224 | tf_op jit(solution)/shard_map/ppermute | solution.py:390
  6.8 0.7 %sources_other.1 = (f32[2,16,8,128]{3,2,1,0:T(8,128)S(1)}, f32[2,16,8,128]{3,2,1,0:T(8,128)S(1)}, f32[2,16,8,128]{3,2,1,0:T(8,128)S(1)}, f32[2,16,8,128]{3,2,1,0:T(8,128)S(1)}) custom-call(f32[2,4,2,128,128]{4,3,2,1,0:T(8,128)S(1)} %get-tuple-element.48.f_buf, f32[2,1,4,2,8,128]{5,4,3,2,1,0:T(8,128)S(1)} %get-tuple-element.49.rate_buf, ...), custom_call_target="tpu_custom_call" | custom-call | flops 8000000000 | bytes 24000000 | tf_op jit(solution)/shard_map/sources_other/pallas_call | solution.py:372
  7.6 1.5 %collective-permute-start.3 = (f32[2,16,8,128]{3,2,1,0:T(8,128)S(1)}, f32[2,16,8,128]{3,2,1,0:T(8,128)S(1)}, u32[]{:S(2)}, u32[]{:S(2)}) collective-permute-start(f32[2,16,8,128]{3,2,1,0:T(8,128)S(1)} %get-tuple-element.55), channel_id=1, source_target_pairs={{0,7},{1,6},{2,5},{3,4},{4,3},{5,2},{6,1},{7,0},{8,15},{9,14},{10,... | collective-permute-start | bytes 393224 | tf_op jit(solution)/shard_map/ppermute | solution.py:390
  9.1 1.6 %collective-permute-start.4 = (f32[2,16,8,128]{3,2,1,0:T(8,128)S(1)}, f32[2,16,8,128]{3,2,1,0:T(8,128)S(1)}, u32[]{:S(2)}, u32[]{:S(2)}) collective-permute-start(f32[2,16,8,128]{3,2,1,0:T(8,128)S(1)} %get-tuple-element.56), channel_id=1, source_target_pairs={{0,5},{1,4},{2,7},{3,6},{4,1},{5,0},{6,3},{7,2},{8,13},{9,12},{10,... | collective-permute-start | bytes 393224 | tf_op jit(solution)/shard_map/ppermute | solution.py:390
  10.8 2.6 %collective-permute-done.1.rest_2_ = f32[2,16,8,128]{3,2,1,0:T(8,128)S(1)} collective-permute-done((f32[2,16,8,128]{3,2,1,0:T(8,128)S(1)}, f32[2,16,8,128]{3,2,1,0:T(8,128)S(1)}, u32[]{:S(2)}, u32[]{:S(2)}) %collective-permute-start.1) | collective-permute-done | bytes 131104 | tf_op jit(solution)/shard_map/ppermute | solution.py:390
  13.4 2.4 %collective-permute-done.2.rest_3_ = f32[2,16,8,128]{3,2,1,0:T(8,128)S(1)} collective-permute-done((f32[2,16,8,128]{3,2,1,0:T(8,128)S(1)}, f32[2,16,8,128]{3,2,1,0:T(8,128)S(1)}, u32[]{:S(2)}, u32[]{:S(2)}) %collective-permute-start.2) | collective-permute-done | bytes 131104 | tf_op jit(solution)/shard_map/ppermute | solution.py:390
  15.9 1.7 %collective-permute-done.4.rest_5_ = f32[2,16,8,128]{3,2,1,0:T(8,128)S(1)} collective-permute-done((f32[2,16,8,128]{3,2,1,0:T(8,128)S(1)}, f32[2,16,8,128]{3,2,1,0:T(8,128)S(1)}, u32[]{:S(2)}, u32[]{:S(2)}) %collective-permute-start.4) | collective-permute-done | bytes 131104 | tf_op jit(solution)/shard_map/ppermute | solution.py:390
  17.7 0.7 %gather.1 = (f32[16,16,8,128]{3,2,1,0:T(8,128)S(1)}, f32[16,8,128]{2,1,0:T(8,128)S(1)}, f32[16,8,128]{2,1,0:T(8,128)S(1)}, f32[2,16,128]{2,1,0:T(8,128)S(1)}) custom-call(f32[16,8,128]{2,1,0:T(8,128)S(1)} %get-tuple-element.39.decay_ref, f32[16,8,128]{2,1,0:T(8,128)S(1)} %get-tuple-element.41.up_ref, f32[16,8,128]{2,1,0:T(8,128)S(1)} %get-tuple-element.42.down_ref, ...), custom_call_target="tpu_custom_call" | custom-call | tf_op jit(solution)/shard_map/gather/pallas_call | solution.py:426
  18.4 3.7 %collective-permute-start.9 = (f32[2,16,128]{2,1,0:T(8,128)S(1)}, f32[2,16,128]{2,1,0:T(8,128)S(1)}, u32[]{:S(2)}, u32[]{:S(2)}) collective-permute-start(f32[2,16,128]{2,1,0:T(8,128)S(1)} %get-tuple-element.64.rest_0_), channel_id=1, source_target_pairs={{0,24},{8,16},{16,8},{24,0},{1,25},{9,17},{17,9},{25,1},{2,26},{10... | collective-permute-start | bytes 49160 | tf_op jit(solution)/shard_map/ppermute | solution.py:390
  22.1 0.8 %collective-permute-start.7 = (f32[2,16,128]{2,1,0:T(8,128)S(1)}, f32[2,16,128]{2,1,0:T(8,128)S(1)}, u32[]{:S(2)}, u32[]{:S(2)}) collective-permute-start(f32[2,16,128]{2,1,0:T(8,128)S(1)} %get-tuple-element.64.rest_0_), channel_id=1, source_target_pairs={{0,8},{8,0},{16,24},{24,16},{1,9},{9,1},{17,25},{25,17},{2,10},{10... | collective-permute-start | bytes 49160 | tf_op jit(solution)/shard_map/ppermute | solution.py:390
  23.0 1.0 %collective-permute-done.9.rest_3_ = f32[2,16,128]{2,1,0:T(8,128)S(1)} collective-permute-done((f32[2,16,128]{2,1,0:T(8,128)S(1)}, f32[2,16,128]{2,1,0:T(8,128)S(1)}, u32[]{:S(2)}, u32[]{:S(2)}) %collective-permute-start.9) | collective-permute-done | bytes 16416 | tf_op jit(solution)/shard_map/ppermute | solution.py:390
  24.0 2.7 %collective-permute-done.8.rest_2_ = f32[2,16,128]{2,1,0:T(8,128)S(1)} collective-permute-done((f32[2,16,128]{2,1,0:T(8,128)S(1)}, f32[2,16,128]{2,1,0:T(8,128)S(1)}, u32[]{:S(2)}, u32[]{:S(2)}) %collective-permute-start.8) | collective-permute-done | bytes 16416 | tf_op jit(solution)/shard_map/ppermute | solution.py:390
  26.8 0.8 %solve.1 = (f32[2,16,8,128]{3,2,1,0:T(8,128)S(1)}, f32[2,16,8,128]{3,2,1,0:T(8,128)S(1)}, f32[2,16,8,128]{3,2,1,0:T(8,128)S(1)}, f32[2,16,8,128]{3,2,1,0:T(8,128...) custom-call(f32[16,8,128]{2,1,0:T(8,128)S(1)} %get-tuple-element.39., ...), custom_call_target="tpu_custom_call" | custom-call | tf_op jit(solution)/shard_map/solve/pallas_call | solution.py:505
  27.6 2.8 %collective-permute-start.10 = (f32[2,16,8,128]{3,2,1,0:T(8,128)S(1)}, f32[2,16,8,128]{3,2,1,0:T(8,128)S(1)}, u32[]{:S(2)}, u32[]{:S(2)}) collective-permute-start(f32[2,16,8,128]{3,2,1,0:T(8,128)S(1)} %get-tuple-element.66), channel_id=1, source_target_pairs={{0,6},{1,7},{2,4},{3,5},{4,2},{5,3},{6,0},{7,1},{8,14},{9,15},{10,... | collective-permute-start | bytes 393224 | tf_op jit(solution)/shard_map/ppermute | solution.py:390
  30.4 0.5 %collective-permute-start.11 = (f32[2,16,8,128]{3,2,1,0:T(8,128)S(1)}, f32[2,16,8,128]{3,2,1,0:T(8,128)S(1)}, u32[]{:S(2)}, u32[]{:S(2)}) collective-permute-start(f32[2,16,8,128]{3,2,1,0:T(8,128)S(1)} %get-tuple-element.67), channel_id=1, source_target_pairs={{0,2},{1,3},{2,0},{3,1},{4,6},{5,7},{6,4},{7,5},{8,10},{9,11},{10,... | collective-permute-start | bytes 393224 | tf_op jit(solution)/shard_map/ppermute | solution.py:390
  31.3 2.4 %collective-permute-start.14 = (f32[2,16,8,128]{3,2,1,0:T(8,128)S(1)}, f32[2,16,8,128]{3,2,1,0:T(8,128)S(1)}, u32[]{:S(2)}, u32[]{:S(2)}) collective-permute-start(f32[2,16,8,128]{3,2,1,0:T(8,128)S(1)} %get-tuple-element.70), channel_id=1, source_target_pairs={{0,5},{1,4},{2,7},{3,6},{4,1},{5,0},{6,3},{7,2},{8,13},{9,12},{10,... | collective-permute-start | bytes 393224 | tf_op jit(solution)/shard_map/ppermute | solution.py:390
  33.7 0.7 %collective-permute-done.10.refs_5_ = f32[2,16,8,128]{3,2,1,0:T(8,128)S(1)} collective-permute-done((f32[2,16,8,128]{3,2,1,0:T(8,128)S(1)}, f32[2,16,8,128]{3,2,1,0:T(8,128)S(1)}, u32[]{:S(2)}, u32[]{:S(2)}) %collective-permute-start.10) | collective-permute-done | bytes 131104 | tf_op jit(solution)/shard_map/ppermute | solution.py:390
  34.4 1.7 %collective-permute-done.11.refs_6_ = f32[2,16,8,128]{3,2,1,0:T(8,128)S(1)} collective-permute-done((f32[2,16,8,128]{3,2,1,0:T(8,128)S(1)}, f32[2,16,8,128]{3,2,1,0:T(8,128)S(1)}, u32[]{:S(2)}, u32[]{:S(2)}) %collective-permute-start.11) | collective-permute-done | bytes 131104 | tf_op jit(solution)/shard_map/ppermute | solution.py:390
  36.1 3.5 %collective-permute-done.12.refs_7_ = f32[2,16,8,128]{3,2,1,0:T(8,128)S(1)} collective-permute-done((f32[2,16,8,128]{3,2,1,0:T(8,128)S(1)}, f32[2,16,8,128]{3,2,1,0:T(8,128)S(1)}, u32[]{:S(2)}, u32[]{:S(2)}) %collective-permute-start.12) | collective-permute-done | bytes 131104 | tf_op jit(solution)/shard_map/ppermute | solution.py:390
  39.6 0.6 %finish_own.1.own_buf = f32[2,4,128,128]{3,2,1,0:T(8,128)S(1)} custom-call(bf16[256,256]{1,0:T(8,128)(2,1)S(1)} %copy-done.3, bf16[256,256]{1,0:T(8,128)(2,1)S(1)} %copy-done.2, bf16[256,256]{1,0:T(8,128)(2,1)S(1)} %copy-done.1, bf16[256,256]{1,0:T(8,128)(2,1)S(1)} %copy-done, f32[2,16,8,128]{3,2,1,0:T(8,128)S(1)} %get-tuple-element.65.refs_4_, ...), custom_call_target="tpu_custom_call" | custom-call | flops 8000000000 | bytes 24000000 | tf_op jit(solution)/shard_map/finish_own/pallas_call | solution.py:575
  40.5 0.5 %collective-permute-done.15.refs_6_ = f32[2,16,8,128]{3,2,1,0:T(8,128)S(1)} collective-permute-done((f32[2,16,8,128]{3,2,1,0:T(8,128)S(1)}, f32[2,16,8,128]{3,2,1,0:T(8,128)S(1)}, u32[]{:S(2)}, u32[]{:S(2)}) %collective-permute-start.15) | collective-permute-done | bytes 131104 | tf_op jit(solution)/shard_map/ppermute | solution.py:390
  41.1 1.3 %finish_other.1 = f32[2,2,128,512]{3,2,1,0:T(8,128)} custom-call(f32[2,4,128,128]{3,2,1,0:T(8,128)S(1)} %finish_own.1.own_buf, bf16[256,256]{1,0:T(8,128)(2,1)S(1)} %copy-done.3, bf16[256,256]{1,0:T(8,128)(2,1)S(1)} %copy-done.2, bf16[256,256]{1,0:T(8,128)(2,1)S(1)} %copy-done.1, bf16[256,256]{1,0:T(8,128)(2,1)S(1)} %copy-done, ...), custom_call_target="tpu_custom_call" | custom-call | tf_op jit(solution)/shard_map/finish_other/pallas_call | solution.py:586
  (25 shorter events, 1.3 us)
Async XLA Ops:
  2.3 8.4 %collective-permute-start = (f32[2,16,8,128]{3,2,1,0:T(8,128)S(1)}, f32[2,16,8,128]{3,2,1,0:T(8,128)S(1)}, u32[]{:S(2)}, u32[]{:S(2)}) collective-permute-start(f32[2,16,8,128]{3,2,1,0:T(8,128)S(1)} %get-tuple-element.45), channel_id=1, source_target_pairs={{0,6},{1,7},{2,4},{3,5},{4,2},{5,3},{6,0},{7,1},{8,14},{9,15},{10,... | collective-permute-start | bytes 393224 | tf_op jit(solution)/shard_map/ppermute | solution.py:390
  6.2 7.3 %collective-permute-start.1 = (f32[2,16,8,128]{3,2,1,0:T(8,128)S(1)}, f32[2,16,8,128]{3,2,1,0:T(8,128)S(1)}, u32[]{:S(2)}, u32[]{:S(2)}) collective-permute-start(f32[2,16,8,128]{3,2,1,0:T(8,128)S(1)} %get-tuple-element.46), channel_id=1, source_target_pairs={{0,2},{1,3},{2,0},{3,1},{4,6},{5,7},{6,4},{7,5},{8,10},{9,11},{10,... | collective-permute-start | bytes 393224 | tf_op jit(solution)/shard_map/ppermute | solution.py:390
  6.7 9.2 %collective-permute-start.2 = (f32[2,16,8,128]{3,2,1,0:T(8,128)S(1)}, f32[2,16,8,128]{3,2,1,0:T(8,128)S(1)}, u32[]{:S(2)}, u32[]{:S(2)}) collective-permute-start(f32[2,16,8,128]{3,2,1,0:T(8,128)S(1)} %get-tuple-element.47), channel_id=1, source_target_pairs={{0,4},{1,5},{2,6},{3,7},{4,0},{5,1},{6,2},{7,3},{8,12},{9,13},{10,... | collective-permute-start | bytes 393224 | tf_op jit(solution)/shard_map/ppermute | solution.py:390
  7.6 8.3 %collective-permute-start.3 = (f32[2,16,8,128]{3,2,1,0:T(8,128)S(1)}, f32[2,16,8,128]{3,2,1,0:T(8,128)S(1)}, u32[]{:S(2)}, u32[]{:S(2)}) collective-permute-start(f32[2,16,8,128]{3,2,1,0:T(8,128)S(1)} %get-tuple-element.55), channel_id=1, source_target_pairs={{0,7},{1,6},{2,5},{3,4},{4,3},{5,2},{6,1},{7,0},{8,15},{9,14},{10,... | collective-permute-start | bytes 393224 | tf_op jit(solution)/shard_map/ppermute | solution.py:390
  9.1 8.5 %collective-permute-start.4 = (f32[2,16,8,128]{3,2,1,0:T(8,128)S(1)}, f32[2,16,8,128]{3,2,1,0:T(8,128)S(1)}, u32[]{:S(2)}, u32[]{:S(2)}) collective-permute-start(f32[2,16,8,128]{3,2,1,0:T(8,128)S(1)} %get-tuple-element.56), channel_id=1, source_target_pairs={{0,5},{1,4},{2,7},{3,6},{4,1},{5,0},{6,3},{7,2},{8,13},{9,12},{10,... | collective-permute-start | bytes 393224 | tf_op jit(solution)/shard_map/ppermute | solution.py:390
  10.7 7.0 %collective-permute-start.5 = (f32[2,16,8,128]{3,2,1,0:T(8,128)S(1)}, f32[2,16,8,128]{3,2,1,0:T(8,128)S(1)}, u32[]{:S(2)}, u32[]{:S(2)}) collective-permute-start(f32[2,16,8,128]{3,2,1,0:T(8,128)S(1)} %get-tuple-element.57), channel_id=1, source_target_pairs={{0,3},{1,2},{2,1},{3,0},{4,7},{5,6},{6,5},{7,4},{8,11},{9,10},{10,... | collective-permute-start | bytes 393224 | tf_op jit(solution)/shard_map/ppermute | solution.py:390
  13.4 4.3 %collective-permute-start.6 = (f32[2,16,8,128]{3,2,1,0:T(8,128)S(1)}, f32[2,16,8,128]{3,2,1,0:T(8,128)S(1)}, u32[]{:S(2)}, u32[]{:S(2)}) collective-permute-start(f32[2,16,8,128]{3,2,1,0:T(8,128)S(1)} %get-tuple-element.58), channel_id=1, source_target_pairs={{0,1},{1,0},{2,3},{3,2},{4,5},{5,4},{6,7},{7,6},{8,9},{9,8},{10,11... | collective-permute-start | bytes 393224 | tf_op jit(solution)/shard_map/ppermute | solution.py:390
  18.4 5.6 %collective-permute-start.9 = (f32[2,16,128]{2,1,0:T(8,128)S(1)}, f32[2,16,128]{2,1,0:T(8,128)S(1)}, u32[]{:S(2)}, u32[]{:S(2)}) collective-permute-start(f32[2,16,128]{2,1,0:T(8,128)S(1)} %get-tuple-element.64.rest_0_), channel_id=1, source_target_pairs={{0,24},{8,16},{16,8},{24,0},{1,25},{9,17},{17,9},{25,1},{2,26},{10... | collective-permute-start | bytes 49160 | tf_op jit(solution)/shard_map/ppermute | solution.py:390
  22.1 4.6 %collective-permute-start.8 = (f32[2,16,128]{2,1,0:T(8,128)S(1)}, f32[2,16,128]{2,1,0:T(8,128)S(1)}, u32[]{:S(2)}, u32[]{:S(2)}) collective-permute-start(f32[2,16,128]{2,1,0:T(8,128)S(1)} %get-tuple-element.64.rest_0_), channel_id=1, source_target_pairs={{0,16},{8,24},{16,0},{24,8},{1,17},{9,25},{17,1},{25,9},{2,18},{10... | collective-permute-start | bytes 49160 | tf_op jit(solution)/shard_map/ppermute | solution.py:390
  22.1 4.6 %collective-permute-start.7 = (f32[2,16,128]{2,1,0:T(8,128)S(1)}, f32[2,16,128]{2,1,0:T(8,128)S(1)}, u32[]{:S(2)}, u32[]{:S(2)}) collective-permute-start(f32[2,16,128]{2,1,0:T(8,128)S(1)} %get-tuple-element.64.rest_0_), channel_id=1, source_target_pairs={{0,8},{8,0},{16,24},{24,16},{1,9},{9,1},{17,25},{25,17},{2,10},{10... | collective-permute-start | bytes 49160 | tf_op jit(solution)/shard_map/ppermute | solution.py:390
  26.7 12.8 %copy-start = (bf16[256,256]{1,0:T(8,128)(2,1)S(1)}, bf16[256,256]{1,0:T(8,128)(2,1)}, u32[]{:S(2)}) copy-start(bf16[256,256]{1,0:T(8,128)(2,1)} %constant.25.clone.refs_3_) | copy-start | bytes 393220
  26.7 12.8 %copy-start.1 = (bf16[256,256]{1,0:T(8,128)(2,1)S(1)}, bf16[256,256]{1,0:T(8,128)(2,1)}, u32[]{:S(2)}) copy-start(bf16[256,256]{1,0:T(8,128)(2,1)} %constant.24.clone.refs_2_) | copy-start | bytes 393220
  26.8 12.8 %copy-start.2 = (bf16[256,256]{1,0:T(8,128)(2,1)S(1)}, bf16[256,256]{1,0:T(8,128)(2,1)}, u32[]{:S(2)}) copy-start(bf16[256,256]{1,0:T(8,128)(2,1)} %constant.23.clone.refs_1_) | copy-start | bytes 393220
  26.8 12.8 %copy-start.3 = (bf16[256,256]{1,0:T(8,128)(2,1)S(1)}, bf16[256,256]{1,0:T(8,128)(2,1)}, u32[]{:S(2)}) copy-start(bf16[256,256]{1,0:T(8,128)(2,1)} %constant.22.clone.refs_0_) | copy-start | bytes 393220
  27.6 6.9 %collective-permute-start.10 = (f32[2,16,8,128]{3,2,1,0:T(8,128)S(1)}, f32[2,16,8,128]{3,2,1,0:T(8,128)S(1)}, u32[]{:S(2)}, u32[]{:S(2)}) collective-permute-start(f32[2,16,8,128]{3,2,1,0:T(8,128)S(1)} %get-tuple-element.66), channel_id=1, source_target_pairs={{0,6},{1,7},{2,4},{3,5},{4,2},{5,3},{6,0},{7,1},{8,14},{9,15},{10,... | collective-permute-start | bytes 393224 | tf_op jit(solution)/shard_map/ppermute | solution.py:390
  30.4 5.7 %collective-permute-start.11 = (f32[2,16,8,128]{3,2,1,0:T(8,128)S(1)}, f32[2,16,8,128]{3,2,1,0:T(8,128)S(1)}, u32[]{:S(2)}, u32[]{:S(2)}) collective-permute-start(f32[2,16,8,128]{3,2,1,0:T(8,128)S(1)} %get-tuple-element.67), channel_id=1, source_target_pairs={{0,2},{1,3},{2,0},{3,1},{4,6},{5,7},{6,4},{7,5},{8,10},{9,11},{10,... | collective-permute-start | bytes 393224 | tf_op jit(solution)/shard_map/ppermute | solution.py:390
  30.9 8.7 %collective-permute-start.12 = (f32[2,16,8,128]{3,2,1,0:T(8,128)S(1)}, f32[2,16,8,128]{3,2,1,0:T(8,128)S(1)}, u32[]{:S(2)}, u32[]{:S(2)}) collective-permute-start(f32[2,16,8,128]{3,2,1,0:T(8,128)S(1)} %get-tuple-element.68), channel_id=1, source_target_pairs={{0,4},{1,5},{2,6},{3,7},{4,0},{5,1},{6,2},{7,3},{8,12},{9,13},{10,... | collective-permute-start | bytes 393224 | tf_op jit(solution)/shard_map/ppermute | solution.py:390
  31.1 9.1 %collective-permute-start.13 = (f32[2,16,8,128]{3,2,1,0:T(8,128)S(1)}, f32[2,16,8,128]{3,2,1,0:T(8,128)S(1)}, u32[]{:S(2)}, u32[]{:S(2)}) collective-permute-start(f32[2,16,8,128]{3,2,1,0:T(8,128)S(1)} %get-tuple-element.69), channel_id=1, source_target_pairs={{0,7},{1,6},{2,5},{3,4},{4,3},{5,2},{6,1},{7,0},{8,15},{9,14},{10,... | collective-permute-start | bytes 393224 | tf_op jit(solution)/shard_map/ppermute | solution.py:390
  31.3 9.2 %collective-permute-start.14 = (f32[2,16,8,128]{3,2,1,0:T(8,128)S(1)}, f32[2,16,8,128]{3,2,1,0:T(8,128)S(1)}, u32[]{:S(2)}, u32[]{:S(2)}) collective-permute-start(f32[2,16,8,128]{3,2,1,0:T(8,128)S(1)} %get-tuple-element.70), channel_id=1, source_target_pairs={{0,5},{1,4},{2,7},{3,6},{4,1},{5,0},{6,3},{7,2},{8,13},{9,12},{10,... | collective-permute-start | bytes 393224 | tf_op jit(solution)/shard_map/ppermute | solution.py:390
  34.4 6.6 %collective-permute-start.15 = (f32[2,16,8,128]{3,2,1,0:T(8,128)S(1)}, f32[2,16,8,128]{3,2,1,0:T(8,128)S(1)}, u32[]{:S(2)}, u32[]{:S(2)}) collective-permute-start(f32[2,16,8,128]{3,2,1,0:T(8,128)S(1)} %get-tuple-element.71), channel_id=1, source_target_pairs={{0,3},{1,2},{2,1},{3,0},{4,7},{5,6},{6,5},{7,4},{8,11},{9,10},{10,... | collective-permute-start | bytes 393224 | tf_op jit(solution)/shard_map/ppermute | solution.py:390
  36.1 4.9 %collective-permute-start.16 = (f32[2,16,8,128]{3,2,1,0:T(8,128)S(1)}, f32[2,16,8,128]{3,2,1,0:T(8,128)S(1)}, u32[]{:S(2)}, u32[]{:S(2)}) collective-permute-start(f32[2,16,8,128]{3,2,1,0:T(8,128)S(1)} %get-tuple-element.72), channel_id=1, source_target_pairs={{0,1},{1,0},{2,3},{3,2},{4,5},{5,4},{6,7},{7,6},{8,9},{9,8},{10,11... | collective-permute-start | bytes 393224 | tf_op jit(solution)/shard_map/ppermute | solution.py:390
